TPU v7x, 128 devices: a whole 4x4x4 slice. The times are simulated.
128 devices in a mesh: occ: 8 (over x, core), vir: 16 (over y, z).
Axes of the slice: x: 4, y: 4, z: 4, core: 2. Of those that a mesh axis runs over, the one named last changes fastest.
Arguments:
- amplitudes: bfloat16 [8, 2, 4096, 4096], P('occ', None, None, 'vir'), may hold values from -6 to 6
- coulomb: bfloat16 [8, 2, 4096, 4096], P('occ', None, None, 'vir'), may hold values from -6 to 6
- ladder_tiles: bfloat16 [256, 128, 128], P('vir'), may hold values from -0.1875 to 0.1875
- cycle_tiles: bfloat16 [256, 128, 128], P('vir'), may hold values from -0.25 to 0.25
- ladder_screen: int32 [32, 8], replicated, may hold values from 0 to 31, as said below
- tile_slot: int32 [256], replicated, may hold values from 0 to 255, each once
- cycle_screen: int32 [64, 4], replicated, may hold values from 0 to 63, as said below
- cycle_rows: int32 [32, 48], replicated, may hold values from 0 to 63, as said below
- cycle_count: int32 [32], replicated, may hold values from 1 to 48, 1024 in all
- slab_occ: int32 [8], replicated, may hold values from 0 to 399
- window_occ: int32 [2], replicated, may hold values from 0 to 399
- occ_energy: float32 [400], replicated, may hold values from -3 to -0.5
- vir_energy: float32 [4096], replicated, may hold values from 0.4 to 4
Outputs:
- updated: bfloat16 [8, 2, 4096, 4096], P('occ', None, None, 'vir')
Inputs may be any that keep to these rules, and one draw needn't show every extreme that they name: `ladder_screen`: each row names 8 different tiles. `cycle_screen`: each row names 4 different row tiles. `cycle_rows`: each row names 48 different block columns; the first cycle_count of them are used. `cycle_count`: the counts sum to exactly 1024, and the largest is exactly 48.
All inputs are finite; a program needn't handle non-finite values.
Results may differ from a plain program's by a relative error of at most 0.003.
Values may be sent and summed in bfloat16 or wider, within the bound.
No kernel may reach another device: no remote copies, remote signals or barrier semaphores. Data moves between devices by JAX's collectives and lax.ppermute only.
A program may use at most 192 MiB of HBM per device.

v0:
```python
import math

import jax
import jax.numpy as jnp
from jax import lax
from jax.sharding import PartitionSpec as P


def body(
    amplitudes,
    coulomb,
    ladder_tiles,
    cycle_tiles,
    ladder_screen,
    tile_slot,
    cycle_screen,
    cycle_rows,
    cycle_count,
    slab_occ,
    window_occ,
    occ_energy,
    vir_energy,
):
    occ_count = lax.axis_size("occ")
    vir_count = lax.axis_size("vir")
    dev_count = occ_count * vir_count
    slab_rows, window, width_all, block_cols = amplitudes.shape
    tile_side = ladder_tiles.shape[1]
    tile_count = width_all // tile_side
    ladder_keep = ladder_screen.shape[1]
    cycle_keep = cycle_screen.shape[1]
    column_tiles = cycle_screen.shape[0]
    rows_here = width_all // dev_count
    slab_all = slab_rows * occ_count
    all_ladder, all_cycle = (
        lax.all_gather(ladder_tiles, "vir", axis=0, tiled=True),
        lax.all_gather(cycle_tiles, "vir", axis=0, tiled=True),
    )
    front, inner = (1, rows_here)
    split = amplitudes.reshape(slab_rows, window, front, occ_count, vir_count, inner, block_cols)
    flat = split.reshape(1, slab_rows, window, front, dev_count, inner, block_cols)
    moved = lax.all_to_all(flat, ("occ", "vir"), split_axis=4, concat_axis=0, tiled=True)
    moved = moved.reshape(occ_count, vir_count, slab_rows, window, front, inner, block_cols)
    moved = moved.transpose(0, 2, 3, 4, 5, 1, 6)
    cycle_amp = moved.reshape(slab_all, window, front * inner, width_all)
    extent = slab_rows * window * block_cols
    arranged = amplitudes.transpose(2, 0, 1, 3).reshape(tile_count, tile_side, extent)
    slots = tile_slot.reshape(tile_count, ladder_keep)
    group = math.gcd(tile_count, 8)

    def ladder_block(start):
        screen_part = lax.dynamic_slice_in_dim(ladder_screen, start, group, 0)
        slot_part = lax.dynamic_slice_in_dim(slots, start, group, 0)
        picked_rows = arranged[screen_part]
        weights = all_ladder[slot_part]
        return jnp.einsum(
            "akrc,akce->are", weights, picked_rows, preferred_element_type=jnp.float32
        )

    starts = jnp.arange(0, tile_count, group, dtype=jnp.int32)
    total = lax.map(ladder_block, starts)
    ladder = total.reshape(width_all, slab_rows, window, block_cols).transpose(1, 2, 0, 3)
    source = cycle_amp.reshape(slab_all, window, front, inner, tile_count, tile_side)
    source = source.transpose(1, 4, 2, 0, 3, 5).reshape(
        window * tile_count, front, slab_all * inner, tile_side
    )
    cycle_sel = all_cycle.reshape(column_tiles, cycle_keep, tile_side, tile_side)
    device = lax.axis_index("occ") * vir_count + lax.axis_index("vir")
    my_tile = device * rows_here // tile_side
    columns = lax.dynamic_index_in_dim(cycle_rows, my_tile, 0, keepdims=False)
    used = lax.dynamic_index_in_dim(cycle_count, my_tile, 0, keepdims=False)
    valid = jnp.arange(columns.shape[0], dtype=jnp.int32) < used
    picked = source[cycle_screen[columns], 0]
    part = jnp.einsum(
        "emrc,emcb->erb", picked, cycle_sel[columns], preferred_element_type=jnp.float32
    )
    part = jnp.where(valid[:, None, None], part, 0.0)
    placed = (
        jnp.zeros((column_tiles, slab_all * inner, tile_side), jnp.float32).at[columns].add(part)
    )
    cycle_cols = placed.reshape(column_tiles, front, slab_all * inner, tile_side)
    cycle_cols = cycle_cols.astype(jnp.bfloat16).reshape(
        window, tile_count, front, slab_all, inner, tile_side
    )
    cycle_view = cycle_cols.transpose(3, 0, 2, 4, 1, 5).reshape(
        slab_all, window, front * inner, width_all
    )
    shaped = cycle_view.reshape(occ_count, slab_rows, window, front, inner, vir_count, block_cols)
    shaped = shaped.transpose(0, 5, 1, 2, 3, 4, 6).reshape(
        dev_count, slab_rows, window, front, 1, inner, block_cols
    )
    back = lax.all_to_all(shaped, ("occ", "vir"), split_axis=0, concat_axis=4, tiled=True)
    cycle = back.reshape(slab_rows, window, width_all, block_cols)
    occ_total = occ_energy.shape[0]
    orbital_ids = jnp.arange(occ_total, dtype=jnp.int32)
    my_slab = lax.dynamic_slice_in_dim(slab_occ, lax.axis_index("occ") * slab_rows, slab_rows)
    energy_i = jnp.sum(
        jnp.where(my_slab[:, None] == orbital_ids[None, :], occ_energy[None, :], 0.0), axis=1
    )
    energy_j = jnp.sum(
        jnp.where(window_occ[:, None] == orbital_ids[None, :], occ_energy[None, :], 0.0), axis=1
    )
    energy_b = lax.dynamic_slice_in_dim(vir_energy, lax.axis_index("vir") * block_cols, block_cols)
    denominator = (
        vir_energy[None, None, :, None]
        + energy_b[None, None, None, :]
        - energy_i[:, None, None, None]
        - energy_j[None, :, None, None]
    )
    value = coulomb.astype(jnp.float32) + ladder + cycle.astype(jnp.float32)
    return (value / denominator).astype(jnp.bfloat16)


def solution(mesh):
    return jax.shard_map(
        body,
        mesh=mesh,
        in_specs=(
            P("occ", None, None, "vir"),
            P("occ", None, None, "vir"),
            P("vir", None, None),
            P("vir", None, None),
            P(),
            P(),
            P(),
            P(),
            P(),
            P(),
            P(),
            P(),
            P(),
        ),
        out_specs=P("occ", None, None, "vir"),
        check_vma=False,
    )
```

profile of v0, /device:TPU:1, one launch (start us, length us, event | category | flops | bytes accessed | tf_op | source)
XLA Modules:
  0.0 347.0 jit_solution(11415876466510590525)
XLA Ops:
  12.9 11.9 %all-to-all-start = ((bf16[1,1,2,1,128,32,256]{6,5,2,3,1,0,4:T(8,128)(2,1)}), bf16[1,1,2,1,128,32,256]{6,5,2,3,1,0,4:T(8,128)(2,1)}, u32[]{:S(2)}, u32[]{:S(2)}) async-start(bf16[1,1,2,1,128,32,256]{6,5,2,3,1,0,4:T(8,128)(2,1)} %copy.67), calls=%async_computation | async-start | bytes 8388608 | tf_op jit(solution)/shard_map/all_to_all | solution.py:42
  27.1 10.1 %copy.64 = bf16[4096,1,2,256]{3,2,0,1:T(2,128)(2,1)} copy(bf16[4096,1,2,256]{3,0,2,1:T(8,128)(2,1)} %bitcast.88) | data formatting | bytes 8388608 | tf_op jit(solution)/shard_map/transpose | solution.py:47
  37.1 7.6 %reshape.148 = bf16[32,128,512]{2,1,0:T(8,128)(2,1)} reshape(bf16[4096,1,2,256]{3,2,0,1:T(2,128)(2,1)} %copy.64) | data formatting | bytes 8388608 | tf_op jit(solution)/shard_map/reshape | solution.py:47
  44.8 6.5 %copy.63 = bf16[1,2,4096,256]{2,3,1,0:T(8,128)(2,1)} copy(bf16[1,2,4096,256]{3,2,1,0:T(8,128)(2,1)} %param.16) | data formatting | bytes 8388608 | tf_op args[1]
  57.3 24.8 %all-to-all-done = bf16[1,1,2,1,128,32,256]{6,5,2,3,1,0,4:T(8,128)(2,1)} async-done(((bf16[1,1,2,1,128,32,256]{6,5,2,3,1,0,4:T(8,128)(2,1)}), bf16[1,1,2,1,128,32,256]{6,5,2,3,1,0,4:T(8,128)(2,1)}, u32[]{:S(2)}, u32[]{:S(2)}) %all-to-all-start) | async-done | bytes 4194336 | tf_op jit(solution)/shard_map/all_to_all | solution.py:42
  82.1 7.1 %copy.68 = bf16[8,1,2,1,32,16,256]{6,5,4,2,0,3,1:T(8,128)(2,1)} copy(bf16[8,1,2,1,32,16,256]{6,4,2,5,0,3,1:T(8,128)(2,1)} %bitcast.15) | data formatting | bytes 8388608 | tf_op jit(solution)/shard_map/transpose | solution.py:44
  89.2 7.2 %reshape_reshape.10 = bf16[8,2,1,32,32,128]{5,4,3,1,0,2:T(8,128)(2,1)} reshape(bf16[8,1,2,1,32,16,256]{6,5,4,2,0,3,1:T(8,128)(2,1)} %copy.68) | data formatting | bytes 8388608 | tf_op jit(solution)/shard_map/reshape;reshape | solution.py:63
  102.3 10.7 %gather_fusion.3 = bf16[192,256,128]{2,1,0:T(8,128)(2,1)} fusion(bf16[64,1,256,128]{3,2,0,1:T(8,128)(2,1)} %bitcast.84, s32[192]{0:T(256)S(1)} %reshape.181), kind=kCustom, calls=%fused_computation.3 | custom fusion | bytes 25167360 | tf_op jit(solution)/shard_map/gather | solution.py:73
  112.9 13.7 %all-gather.5.cloned.1.call-done = bf16[256,128,128]{2,1,0:T(8,128)(2,1)} async-done(((bf16[16,128,128]{2,1,0:T(8,128)(2,1)}), bf16[256,128,128]{2,1,0:T(8,128)(2,1)}) %all-gather.5.cloned.1.call-update) | async-done | bytes 8388624 | tf_op jit(solution)/shard_map/all_gather | solution.py:37
  126.6 8.3 %gather_fusion.4 = bf16[48,4,128,128]{3,2,1,0:T(8,128)(2,1)} fusion(bf16[64,4,128,128]{3,2,1,0:T(8,128)(2,1)} %bitcast.93, s32[1024]{0:T(1024)S(1)} %pad_clamp_fusion.2), kind=kCustom, calls=%fused_computation.4 | custom fusion | bytes 12583104 | tf_op jit(solution)/shard_map/gather | solution.py:75
  134.9 13.0 %bitcast_select_fusion = f32[48,256,128]{2,1,0:T(8,128)} fusion(pred[48]{0:T(512)(128)(4,1)S(1)} %iota_compare_fusion.1, bf16[48,4,256,128]{3,2,1,0:T(8,128)(2,1)} %bitcast.92, bf16[48,4,128,128]{3,2,1,0:T(8,128)(2,1)} %gather_fusion.4), kind=kOutput, calls=%fused_computation.16 | convolution fusion | flops 1612185600 | bytes 25165872 | tf_op jit(solution)/shard_map/emrc,emcb->erb/dot_general | solution.py:74
  152.2 15.3 %scatter_fusion = f32[64,256,128]{2,1,0:T(8,128)} fusion(f32[64,256,128]{2,1,0:T(8,128)} %broadcast_in_dim.61, s32[48]{0:T(128)S(1)} %fusion.6, f32[48,256,128]{2,1,0:T(8,128)} %bitcast_select_fusion), kind=kCustom, calls=%fused_computation.5 | custom fusion | flops 1572864 | bytes 18874560 | tf_op jit(solution)/shard_map/scatter-add | solution.py:79
  176.4 7.2 %reshape_reshape.11 = bf16[8,1,2,1,32,16,256]{6,5,4,2,0,3,1:T(8,128)(2,1)} reshape(bf16[8,2,1,32,32,128]{5,4,3,1,0,2:T(8,128)(2,1)} %copy.71) | data formatting | bytes 8388608 | tf_op jit(solution)/shard_map/reshape;reshape | solution.py:88
  189.5 8.6 %all-to-all-start.1 = ((bf16[128,1,2,1,1,32,256]{6,5,2,4,3,1,0:T(8,128)(2,1)}), bf16[128,1,2,1,1,32,256]{6,5,2,4,3,1,0:T(8,128)(2,1)}, u32[]{:S(2)}, u32[]{:S(2)}) async-start(bf16[128,1,2,1,1,32,256]{6,5,2,4,3,1,0:T(8,128)(2,1)} %bitcast.89), calls=%async_computation.1 | async-start | bytes 8388608 | tf_op jit(solution)/shard_map/all_to_all | solution.py:92
  199.3 83.7 %while.10 = (s32[]{:T(128)}, f32[4,8,128,512]{3,2,1,0:T(8,128)}, s32[4]{0:T(128)S(1)}, s32[32,8]{1,0:T(8,128)S(1)}, bf16[256,128,128]{2,1,0:T(8,128)(2,1)}, /*in...) while((s32[]{:T(128)}, f32[4,8,128,512]{3,2,1,0:T(8,128)}, ...), condition=%wide.region_1.2_spmd, body=%wide.region_0.1_spmd.sunk | while | flops 1073744256 | bytes 33566888 | solution.py:61
  206.5 7.7 %gather_fusion.1 = bf16[64,128,512]{2,1,0:T(8,128)(2,1)} fusion(bf16[32,128,512]{2,1,0:T(8,128)(2,1)} %get-tuple-element.168, s32[1024]{0:T(1024)S(1)} %pad_clamp_fusion.6), kind=kCustom, calls=%fused_computation.1.clone.1 | custom fusion | bytes 16777472 | tf_op jit(solution)/shard_map/while/body/eval_jaxpr/gather | solution.py:54
  227.4 7.7 %gather_fusion.1 = bf16[64,128,512]{2,1,0:T(8,128)(2,1)} fusion(bf16[32,128,512]{2,1,0:T(8,128)(2,1)} %get-tuple-element.168, s32[1024]{0:T(1024)S(1)} %pad_clamp_fusion.6), kind=kCustom, calls=%fused_computation.1.clone.1 | custom fusion | bytes 16777472 | tf_op jit(solution)/shard_map/while/body/eval_jaxpr/gather | solution.py:54
  248.4 7.7 %gather_fusion.1 = bf16[64,128,512]{2,1,0:T(8,128)(2,1)} fusion(bf16[32,128,512]{2,1,0:T(8,128)(2,1)} %get-tuple-element.168, s32[1024]{0:T(1024)S(1)} %pad_clamp_fusion.6), kind=kCustom, calls=%fused_computation.1.clone.1 | custom fusion | bytes 16777472 | tf_op jit(solution)/shard_map/while/body/eval_jaxpr/gather | solution.py:54
  269.3 7.7 %gather_fusion.1 = bf16[64,128,512]{2,1,0:T(8,128)(2,1)} fusion(bf16[32,128,512]{2,1,0:T(8,128)(2,1)} %get-tuple-element.168, s32[1024]{0:T(1024)S(1)} %pad_clamp_fusion.6), kind=kCustom, calls=%fused_computation.1.clone.1 | custom fusion | bytes 16777472 | tf_op jit(solution)/shard_map/while/body/eval_jaxpr/gather | solution.py:54
  283.0 10.5 %reshape.209 = f32[4096,1,2,256]{3,2,0,1:T(2,128)} reshape(f32[4,8,128,512]{3,2,1,0:T(8,128)} %get-tuple-element.42) | data formatting | bytes 16777216 | tf_op jit(solution)/shard_map/reshape | solution.py:62
  293.5 13.1 %copy.79 = f32[4096,1,2,256]{0,3,2,1:T(8,128)} copy(f32[4096,1,2,256]{3,2,0,1:T(2,128)} %reshape.209) | data formatting | bytes 16777216 | tf_op jit(solution)/shard_map/reshape | solution.py:62
  306.7 6.5 %bitcast_convert_fusion = f32[128,1,1,2,1,1,32,256]{7,6,0,3,5,4,2,1:T(8,128)} fusion(bf16[128,1,2,1,1,32,256]{6,5,2,4,3,1,0:T(8,128)(2,1)} %all-to-all-done.1), kind=kLoop, calls=%fused_computation.17 | loop fusion | flops 2097152 | bytes 12582912 | tf_op jit(solution)/shard_map/convert_element_type | solution.py:110
  313.2 9.0 %copy.75 = f32[1,2,4096,256]{2,3,1,0:T(8,128)} copy(f32[1,2,4096,256]{3,2,1,0:T(8,128)} %bitcast.85) | data formatting | bytes 16777216 | tf_op jit(solution)/shard_map/convert_element_type | solution.py:110
  322.1 11.7 %fusion.2 = bf16[1,2,4096,256]{2,3,1,0:T(8,128)(2,1)} fusion(f32[1,2,4096,256]{2,3,1,0:T(8,128)} %copy.75, f32[4096,1,2,256]{0,3,2,1:T(8,128)} %copy.79, bf16[1,2,4096,256]{2,3,1,0:T(8,128)(2,1)} %copy.63, f32[2]{0:T(128)S(1)} %fusion.5, f32[4096,256]{0,1:T(8,128)} %add_subtract_fusion), kind=kLoop, calls=%fused_computation.15 | loop fusion | flops 12582912 | bytes 29360136 | tf_op jit(solution)/shard_map/convert_element_type | solution.py:111
  (89 shorter events, 92.2 us)
Async XLA Ops:
  6.5 120.1 %all-gather.5.cloned.1.call-start = ((), (), s32[]{:S(2)}) async-start(), calls=%async_computation.3 | async-start | bytes 8912896 | tf_op jit(solution)/shard_map/all_gather | solution.py:37
  7.3 192.0 %all-gather.3.cloned.1.call-start = ((), (), s32[]{:S(2)}) async-start(), calls=%async_computation.2 | async-start | bytes 8912896 | tf_op jit(solution)/shard_map/all_gather | solution.py:36
  12.9 12.0 %copy-start.3 = (s32[64,4]{0,1:T(4,128)S(1)}, s32[64,4]{0,1:T(4,128)}, u32[]{:S(2)}) copy-start(s32[64,4]{0,1:T(4,128)} %param.21) | copy-start | bytes 3076
  12.9 12.1 %copy-start.6 = (s32[32]{0:T(128)S(1)}, s32[32]{0:T(128)}, u32[]{:S(2)}) copy-start(s32[32]{0:T(128)} %param.23) | copy-start | bytes 388
  12.9 14.1 %copy-start.4 = (s32[256]{0:T(256)S(1)}, s32[256]{0:T(256)}, u32[]{:S(2)}) copy-start(s32[256]{0:T(256)} %param.20) | copy-start | bytes 3076
  12.9 69.2 %all-to-all-start = ((bf16[1,1,2,1,128,32,256]{6,5,2,3,1,0,4:T(8,128)(2,1)}), bf16[1,1,2,1,128,32,256]{6,5,2,3,1,0,4:T(8,128)(2,1)}, u32[]{:S(2)}, u32[]{:S(2)}) async-start(bf16[1,1,2,1,128,32,256]{6,5,2,3,1,0,4:T(8,128)(2,1)} %copy.67), calls=%async_computation | async-start | bytes 8388608 | tf_op jit(solution)/shard_map/all_to_all | solution.py:42
  44.7 6.5 %copy-start.7 = (s32[8]{0:T(128)S(1)}, s32[8]{0:T(128)}, u32[]{:S(2)}) copy-start(s32[8]{0:T(128)} %param.24) | copy-start | bytes 100
  44.7 7.2 %copy-start.1 = (f32[4096]{0:T(1024)S(1)}, f32[4096]{0:T(1024)}, u32[]{:S(2)}) copy-start(f32[4096]{0:T(1024)} %param.27) | copy-start | bytes 49156
  44.7 7.9 %copy-start.2 = (f32[400]{0:T(512)S(1)}, f32[400]{0:T(512)}, u32[]{:S(2)}) copy-start(f32[400]{0:T(512)} %param.26) | copy-start | bytes 4804
  44.7 9.2 %copy-start.5 = (s32[2]{0:T(128)S(1)}, s32[2]{0:T(128)}, u32[]{:S(2)}) copy-start(s32[2]{0:T(128)} %param.25) | copy-start | bytes 28
  189.5 9.8 %copy-start = (s32[32,8]{0,1:T(8,128)S(1)}, s32[32,8]{0,1:T(8,128)}, u32[]{:S(2)}) copy-start(s32[32,8]{0,1:T(8,128)} %param.19) | copy-start | bytes 3076
  189.5 117.2 %all-to-all-start.1 = ((bf16[128,1,2,1,1,32,256]{6,5,2,4,3,1,0:T(8,128)(2,1)}), bf16[128,1,2,1,1,32,256]{6,5,2,4,3,1,0:T(8,128)(2,1)}, u32[]{:S(2)}, u32[]{:S(2)}) async-start(bf16[128,1,2,1,1,32,256]{6,5,2,4,3,1,0:T(8,128)(2,1)} %bitcast.89), calls=%async_computation.1 | async-start | bytes 8388608 | tf_op jit(solution)/shard_map/all_to_all | solution.py:92
Sparse Core Ops, SparseCore 0:
  9.5 117.1 all-gather.4
  128.8 70.4 all-gather.2
where the time goes:
time: 350 us; the launch traced here: 347 us
  local copies, waits for them, and re-layouts  183 us (52%)
  other arithmetic  43.8 us (13%)
  waiting for transfers between devices  41.2 us (12%)
  matrix products  37 us (11%)
  starting transfers between devices  20.6 us (6%)
  between operations  13.5 us (4%)
  loops' own time  7.72 us (2%)
    gather x4, local copies, waits for them, and re-layouts, ladder_block(): picked_rows = arranged[screen_part]  30.8 us
    all_to_all x1, waiting for transfers between devices, body(): lax.all_to_all(flat, ('occ', 'vir'), split_axis=4, concat_axis=0, tiled=T...  24.8 us
    dot_general x4, matrix products, ladder_block(): jnp.einsum('akrc,akce->are', weights, picked_rows, preferred_element_type...  24 us
    reshape x2, local copies, waits for them, and re-layouts, body(): total.reshape(width_all, slab_rows, window, block_cols)  23.7 us
    gather x4, local copies, waits for them, and re-layouts, ladder_block(): weights = all_ladder[slot_part]  17.3 us
    scatter-add x1, other arithmetic, body(): jnp.zeros((column_tiles, slab_all * inner, tile_side), jnp.float32)  15.3 us
    all_gather x1, waiting for transfers between devices, body(): lax.all_gather(cycle_tiles, 'vir', axis=0, tiled=True)  13.7 us
    dot_general x1, matrix products, body(): jnp.einsum('emrc,emcb->erb', picked, cycle_sel[columns], preferred_elemen...  13 us
  transfers between devices with their start and end apart: 4, of which 3 were waited for; matrix products, arithmetic and copies ran while one was open for 66% of the time, Pallas kernels for 0%

commit v1 on v0

v1 whole, which is shorter than its diff:
```python
import jax
import jax.numpy as jnp
from jax import lax
from jax.experimental import pallas as pl
from jax.experimental.pallas import tpu as pltpu
from jax.sharding import PartitionSpec as P

F32 = jnp.float32
BF16 = jnp.bfloat16


def tile_of(ref, slot):
    per_dev = ref.shape[0] * ref.shape[2]
    return ref[(slot % per_dev) // ref.shape[2], slot // per_dev, slot % ref.shape[2]]


def cycle_kernel(screen, rows, count, place, t_ref, z_ref, out_ref, mask):
    step = pl.program_id(0)
    tile = z_ref.shape[-1]
    height, width = t_ref.shape[2:]
    tiles_here, tiles_wide = height // tile, width // tile
    window, keep = t_ref.shape[1], screen.shape[1]
    tile_count = screen.shape[0] // window
    first = place[1] * tiles_here

    @pl.when(step == 0)
    def _():
        for a in range(tiles_here):

            @pl.loop(0, mask.shape[1])
            def _(q):
                mask[a, q] = 0

            @pl.loop(0, count[first + a])
            def _(e):
                mask[a, rows[first + a, e]] = 1

    for j in range(window):
        for b in range(tiles_wide):
            q = j * tile_count + step * tiles_wide + b
            left, right = [], []
            for m in range(keep):
                u = screen[q, m]
                c = u % tile_count
                lane = pl.multiple_of((c % tiles_wide) * tile, tile)
                left.append(t_ref[c // tiles_wide, u // tile_count, :, pl.ds(lane, tile)])
                right.append(tile_of(z_ref, q * keep + m))
            part = jnp.dot(
                jnp.concatenate(left, axis=1),
                jnp.concatenate(right, axis=0),
                preferred_element_type=F32,
            )
            for a in range(tiles_here):
                rows_a = part[a * tile : (a + 1) * tile]
                used = jnp.full(rows_a.shape, mask[a, q], jnp.int32) > 0
                out_ref[0, j, a * tile : (a + 1) * tile, b * tile : (b + 1) * tile] = jnp.where(
                    used, rows_a, 0.0
                ).astype(BF16)


def ladder_kernel(screen, slots, t_ref, w_ref, near_ref, out_ref):
    step = pl.program_id(0)
    tile = w_ref.shape[-1]
    keep = screen.shape[1]
    group = out_ref.shape[1] // tile
    for a in range(group):
        block = step * group + a
        left = jnp.concatenate([tile_of(w_ref, slots[block * keep + k]) for k in range(keep)], axis=1)
        for j in range(out_ref.shape[0]):
            right = jnp.concatenate([t_ref[j, screen[block, k]] for k in range(keep)], axis=0)
            here = slice(a * tile, (a + 1) * tile)
            out_ref[j, here, :] = near_ref[j, here, :].astype(F32) + jnp.dot(
                left, right, preferred_element_type=F32
            )


def final_kernel(slab, pair, place, occ_ref, base_ref, cycle_ref, va_ref, vb_ref, out_ref):
    rows = base_ref.shape[1]
    energy_a = jnp.broadcast_to(va_ref[...], (128, rows)).T[:, :1]
    pairs = energy_a + vb_ref[...]
    for j in range(base_ref.shape[0]):
        below = (pairs - occ_ref[slab[place[0]]]) - occ_ref[pair[j]]
        value = base_ref[j] + cycle_ref[0, j].astype(F32)
        out_ref[j] = (value / below).astype(BF16)


def body(
    amplitudes,
    coulomb,
    ladder_tiles,
    cycle_tiles,
    ladder_screen,
    tile_slot,
    cycle_screen,
    cycle_rows,
    cycle_count,
    slab_occ,
    window_occ,
    occ_energy,
    vir_energy,
):
    occ_count, vir_count = lax.axis_size("occ"), lax.axis_size("vir")
    _, window, width_all, block_cols = amplitudes.shape
    stored, tile, _ = ladder_tiles.shape
    tile_count = width_all // tile
    rows_here = width_all // vir_count
    share = stored // occ_count
    occ_at, vir_at = lax.axis_index("occ"), lax.axis_index("vir")
    place = jnp.stack([occ_at, vir_at]).astype(jnp.int32)
    t = amplitudes[0]
    near = coulomb[0]

    def gather(tiles):
        mine = lax.dynamic_slice_in_dim(tiles, occ_at * share, share, 0)
        full = lax.all_gather(mine, ("occ", "vir"), axis=0, tiled=True)
        return full.reshape(occ_count, vir_count, share, tile, tile)

    all_cycle = gather(cycle_tiles)
    all_ladder = gather(ladder_tiles)
    flat = t.reshape(window, vir_count, rows_here, block_cols).transpose(1, 0, 2, 3)
    moved = lax.all_to_all(flat, "vir", 0, 0, tiled=True)

    resident = lambda *shape: pl.BlockSpec(shape, lambda *_: (0,) * len(shape))
    step_block = pl.BlockSpec((window, rows_here, block_cols), lambda g, *_: (0, g, 0))
    swap_block = pl.BlockSpec((1, window, rows_here, block_cols), lambda g, *_: (g, 0, 0, 0))
    limit = pltpu.CompilerParams(vmem_limit_bytes=48 << 20)
    part = pl.pallas_call(
        cycle_kernel,
        out_shape=jax.ShapeDtypeStruct(moved.shape, BF16),
        grid_spec=pltpu.PrefetchScalarGridSpec(
            num_scalar_prefetch=4,
            grid=(vir_count,),
            in_specs=[resident(*moved.shape), resident(*all_cycle.shape)],
            out_specs=swap_block,
            scratch_shapes=[pltpu.SMEM((rows_here // tile, window * tile_count), jnp.int32)],
        ),
        compiler_params=limit,
    )(cycle_screen, cycle_rows, cycle_count, place, moved, all_cycle)
    cycle = lax.all_to_all(part, "vir", 0, 0, tiled=True)

    base = pl.pallas_call(
        ladder_kernel,
        out_shape=jax.ShapeDtypeStruct(t.shape, F32),
        grid_spec=pltpu.PrefetchScalarGridSpec(
            num_scalar_prefetch=2,
            grid=(vir_count,),
            in_specs=[
                resident(window, tile_count, tile, block_cols),
                resident(*all_ladder.shape),
                step_block,
            ],
            out_specs=step_block,
        ),
        compiler_params=limit,
    )(ladder_screen, tile_slot, t.reshape(window, tile_count, tile, block_cols), all_ladder, near)

    energies = vir_energy.reshape(1, width_all)
    out = pl.pallas_call(
        final_kernel,
        out_shape=jax.ShapeDtypeStruct(t.shape, BF16),
        grid_spec=pltpu.PrefetchScalarGridSpec(
            num_scalar_prefetch=3,
            grid=(vir_count,),
            in_specs=[
                pl.BlockSpec(memory_space=pltpu.SMEM),
                step_block,
                swap_block,
                pl.BlockSpec((1, rows_here), lambda g, *_: (0, g)),
                pl.BlockSpec((1, block_cols), lambda g, slab, pair, place: (0, place[1])),
            ],
            out_specs=step_block,
        ),
        compiler_params=limit,
    )(slab_occ, window_occ, place, occ_energy, base, cycle, energies, energies)
    return out[None]


def solution(mesh):
    wide = P("occ", None, None, "vir")
    tiles = P("vir", None, None)
    return jax.shard_map(
        body,
        mesh=mesh,
        in_specs=(wide, wide, tiles, tiles) + (P(),) * 9,
        out_specs=wide,
        check_vma=False,
    )
```

time: 350 us -> 277 us (0.79)
  local copies, waits for them, and re-layouts: 183 us -> 12.2 us
  waiting for transfers between devices: 41.2 us -> 188 us
  Pallas kernels: 0 us -> 48.5 us
  other arithmetic: 43.8 us -> 0.07 us
  matrix products: 37 us -> 0 us
  loops' own time: 7.72 us -> 0 us
  starting transfers between devices: 20.6 us -> 13.5 us
    all_gather x2, waiting for transfers between devices: 14.9 us -> 130 us  [gather(): full = lax.all_gather(mine, ('occ', 'vir'), axis=0, tiled=True)]
    gather x11 -> x0, local copies, waits for them, and re-layouts: 67.7 us -> none  [the longest x4 30.8 us: ladder_block(): picked_rows = arranged[screen_part]]
    pallas_call x0 -> x3, Pallas kernels: none -> 48.5 us  [the longest x1 17.7 us: body(): pl.pallas_call(ladder_kernel, out_shape=jax.ShapeDtypeStruct(t.shape, F32...]
    dot_general x5 -> x0, matrix products: 37 us -> none  [the longest x4 24 us: ladder_block(): jnp.einsum('akrc,akce->are', weights, picked_rows, preferred_element_type...]
    transpose x5 -> x0, local copies, waits for them, and re-layouts: 33.6 us -> none  [the longest x1 10.1 us: body(): amplitudes.transpose(2, 0, 1, 3).reshape(tile_count, tile_side, extent)]
    all_to_all x2, waiting for transfers between devices: 24.9 us -> 58.1 us  [the longest x1 58 us: body(): moved = lax.all_to_all(flat, 'vir', 0, 0, tiled=True)]
    reshape x4 -> x0, local copies, waits for them, and re-layouts: 31.3 us -> none  [the longest x2 23.7 us: body(): total.reshape(width_all, slab_rows, window, block_cols)]
    convert_element_type x3 -> x0, other arithmetic: 22.5 us -> none  [the longest x1 11.7 us: body(): return (value / denominator).astype(jnp.bfloat16)]
  transfers between devices with their start and end apart: 4 -> 4, of which waited for: 3 -> 3; matrix products, arithmetic and copies ran while one was open for 66% -> 2% of each run, Pallas kernels for 0% -> 13%
where the time goes in v1:
time: 277 us; the launch traced here: 275 us
  waiting for transfers between devices  188 us (68%)
  Pallas kernels  48.5 us (18%)
  starting transfers between devices  13.5 us (5%)
  between operations  13.5 us (5%)
  local copies, waits for them, and re-layouts  12.2 us (4%)
    all_gather x2, waiting for transfers between devices, gather(): full = lax.all_gather(mine, ('occ', 'vir'), axis=0, tiled=True)  130 us
    all_to_all x1, waiting for transfers between devices, body(): moved = lax.all_to_all(flat, 'vir', 0, 0, tiled=True)  58 us
    pallas_call x1, Pallas kernels, body(): pl.pallas_call(ladder_kernel, out_shape=jax.ShapeDtypeStruct(t.shape, F32...  17.7 us
    pallas_call x1, Pallas kernels, body(): pl.pallas_call(cycle_kernel, out_shape=jax.ShapeDtypeStruct(moved.shape,...  16.9 us
    pallas_call x1, Pallas kernels, body(): pl.pallas_call(final_kernel, out_shape=jax.ShapeDtypeStruct(t.shape, BF16...  13.9 us
    all_to_all x1, starting transfers between devices, body(): moved = lax.all_to_all(flat, 'vir', 0, 0, tiled=True)  8.77 us
  transfers between devices with their start and end apart: 4, of which 3 were waited for; matrix products, arithmetic and copies ran while one was open for 2% of the time, Pallas kernels for 13%

profile of v1, /device:TPU:1, one launch (start us, length us, event | category | flops | bytes accessed | tf_op | source)
XLA Modules:
  0.0 275.5 jit_solution(12690804074327827181)
XLA Ops:
  6.5 0.0 copy-start
  6.5 1.0 copy-done
  7.6 0.6 constant_dynamic-slice_fusion
  8.2 0.0 all-gather.5.cloned.1.call-update
  8.2 0.0 all-gather.3.cloned.1.call-start
  8.3 1.5 constant_dynamic-slice_fusion.1
  9.7 0.0 all-gather.3.cloned.1.call-update
  9.8 4.6 %copy.23 = bf16[2,16,256,256]{3,2,0,1:T(8,128)(2,1)} copy(bf16[2,16,256,256]{3,2,1,0:T(8,128)(2,1)} %bitcast.12) | data formatting | bytes 8388608 | tf_op jit(solution)/shard_map/reshape;squeeze | solution.py:120
  14.4 8.8 %all-to-all-start = ((bf16[16,2,256,256]{3,2,1,0:T(8,128)(2,1)}), bf16[16,2,256,256]{3,2,1,0:T(8,128)(2,1)}, u32[]{:S(2)}, u32[]{:S(2)}) async-start(bf16[16,2,256,256]{3,2,1,0:T(8,128)(2,1)} %bitcast.16), calls=%async_computation | async-start | bytes 8388608 | tf_op jit(solution)/shard_map/all_to_all | solution.py:121
  23.2 0.0 copy-done.11
  23.2 0.1 copy.21.screen
  23.3 0.1 pad_add_fusion.place
  23.4 58.0 %all-to-all-done.t_ref = bf16[16,2,256,256]{3,2,1,0:T(8,128)(2,1)} async-done(((bf16[16,2,256,256]{3,2,1,0:T(8,128)(2,1)}), bf16[16,2,256,256]{3,2,1,0:T(8,128)(2,1)}, u32[]{:S(2)}, u32[]{:S(2)}) %all-to-all-start) | async-done | bytes 4194336 | tf_op jit(solution)/shard_map/all_to_all | solution.py:121
  81.4 44.8 %all-gather.5.cloned.1.call-done = bf16[256,128,128]{2,1,0:T(8,128)(2,1)} async-done(((bf16[2,128,128]{2,1,0:T(8,128)(2,1)}), bf16[256,128,128]{2,1,0:T(8,128)(2,1)}) %all-gather.5.cloned.1.call-update) | async-done | bytes 8388624 | tf_op jit(solution)/shard_map/all_gather | solution.py:115
  126.2 16.9 %shard_map.128 = bf16[16,2,256,256]{3,2,1,0:T(8,128)(2,1)S(1)} custom-call(s32[64,4]{1,0:T(8,128)S(1)} %copy.21.screen, s32[32,48]{1,0:T(8,128)S(1)} %copy-done.4, s32[32]{0:T(128)S(1)} %copy-done.7, s32[2]{0:T(128)S(1)} %pad_add_fusion.place, bf16[16,2,256,256]{3,2,1,0:T(8,128)(2,1)} %all-to-all-done.t_ref, bf16[8,16,2,128,128]{4,3,2,1,0:T(8,128)(2,1)} %bitcast.17), custom_call_target="tpu_custom_call" | custom-call | tf_op jit(solution)/shard_map/pallas_call | solution.py:127
  143.1 0.0 copy-start.1
  143.1 2.0 copy-done.1
  145.1 4.7 %all-to-all-start.1 = ((bf16[16,2,256,256]{3,2,1,0:T(8,128)(2,1)}), bf16[16,2,256,256]{3,2,1,0:T(8,128)(2,1)}, u32[]{:S(2)}, u32[]{:S(2)}) async-start(bf16[16,2,256,256]{3,2,1,0:T(8,128)(2,1)} %copy-done.1), calls=%async_computation.1 | async-start | bytes 8388608 | tf_op jit(solution)/shard_map/all_to_all | solution.py:139
  149.8 0.1 copy.19.screen
  149.9 84.9 %all-gather.3.cloned.1.call-done = bf16[256,128,128]{2,1,0:T(8,128)(2,1)} async-done(((bf16[2,128,128]{2,1,0:T(8,128)(2,1)}), bf16[256,128,128]{2,1,0:T(8,128)(2,1)}) %all-gather.3.cloned.1.call-update) | async-done | bytes 8388624 | tf_op jit(solution)/shard_map/all_gather | solution.py:115
  234.8 2.2 copy-done.2
  237.0 17.7 %shard_map.127.base_ref = f32[2,4096,256]{2,1,0:T(8,128)} custom-call(s32[32,8]{1,0:T(8,128)S(1)} %copy.19.screen, s32[256]{0:T(256)S(1)} %copy-done.6, bf16[2,32,128,256]{3,2,1,0:T(8,128)(2,1)S(1)} %bitcast.13, bf16[8,16,2,128,128]{4,3,2,1,0:T(8,128)(2,1)} %bitcast.18, bf16[2,4096,256]{2,1,0:T(8,128)(2,1)} %bitcast.19), custom_call_target="tpu_custom_call" | custom-call | tf_op jit(solution)/shard_map/pallas_call | solution.py:141
  254.7 0.0 all-to-all-done.1.cycle_ref
  254.7 13.9 %shard_map.129 = bf16[2,4096,256]{2,1,0:T(8,128)(2,1)} custom-call(s32[8]{0:T(128)S(1)} %copy-done.8, s32[2]{0:T(128)S(1)} %copy-done.9, s32[2]{0:T(128)S(1)} %pad_add_fusion.place, f32[400]{0:T(512)S(1)} %copy-done.5, f32[2,4096,256]{2,1,0:T(8,128)} %shard_map.127.base_ref, bf16[16,2,256,256]{3,2,1,0:T(8,128)(2,1)} %all-to-all-done.1.cycle_ref, ...), custom_call_target="tpu_custom_call" | custom-call | tf_op jit(solution)/shard_map/pallas_call | solution.py:158
  (19 shorter events, 0.0 us)
Async XLA Ops:
  6.5 1.0 copy-start
  6.5 119.7 %all-gather.5.cloned.1.call-start = ((), (), s32[]{:S(2)}) async-start(), calls=%async_computation.3 | async-start | bytes 8454144 | tf_op jit(solution)/shard_map/all_gather | solution.py:115
  8.2 226.6 %all-gather.3.cloned.1.call-start = ((), (), s32[]{:S(2)}) async-start(), calls=%async_computation.2 | async-start | bytes 8454144 | tf_op jit(solution)/shard_map/all_gather | solution.py:115
  14.4 8.8 %copy-start.11 = (s32[64,4]{0,1:T(4,128)S(1)}, s32[64,4]{0,1:T(4,128)}, u32[]{:S(2)}) copy-start(s32[64,4]{0,1:T(4,128)} %param.19) | copy-start | bytes 3076
  14.4 111.8 %copy-start.4 = (s32[32,48]{1,0:T(8,128)S(1)}, s32[32,48]{1,0:T(8,128)}, u32[]{:S(2)}) copy-start(s32[32,48]{1,0:T(8,128)} %rows.1) | copy-start | bytes 18436
  14.4 111.8 %copy-start.7 = (s32[32]{0:T(128)S(1)}, s32[32]{0:T(128)}, u32[]{:S(2)}) copy-start(s32[32]{0:T(128)} %count.1) | copy-start | bytes 388
  14.4 67.0 %all-to-all-start = ((bf16[16,2,256,256]{3,2,1,0:T(8,128)(2,1)}), bf16[16,2,256,256]{3,2,1,0:T(8,128)(2,1)}, u32[]{:S(2)}, u32[]{:S(2)}) async-start(bf16[16,2,256,256]{3,2,1,0:T(8,128)(2,1)} %bitcast.16), calls=%async_computation | async-start | bytes 8388608 | tf_op jit(solution)/shard_map/all_to_all | solution.py:121
  143.1 2.0 copy-start.1
  145.1 4.7 %copy-start.10 = (s32[32,8]{0,1:T(8,128)S(1)}, s32[32,8]{0,1:T(8,128)}, u32[]{:S(2)}) copy-start(s32[32,8]{0,1:T(8,128)} %param.17) | copy-start | bytes 3076
  145.1 89.6 %copy-start.6 = (s32[256]{0:T(256)S(1)}, s32[256]{0:T(256)}, u32[]{:S(2)}) copy-start(s32[256]{0:T(256)} %slots.1) | copy-start | bytes 3076
  145.1 109.5 %all-to-all-start.1 = ((bf16[16,2,256,256]{3,2,1,0:T(8,128)(2,1)}), bf16[16,2,256,256]{3,2,1,0:T(8,128)(2,1)}, u32[]{:S(2)}, u32[]{:S(2)}) async-start(bf16[16,2,256,256]{3,2,1,0:T(8,128)(2,1)} %copy-done.1), calls=%async_computation.1 | async-start | bytes 8388608 | tf_op jit(solution)/shard_map/all_to_all | solution.py:139
  234.8 2.2 copy-start.2
  237.0 17.7 %copy-start.3 = (f32[4096]{0:T(1024)S(1)}, f32[4096]{0:T(1024)}, u32[]{:S(2)}) copy-start(f32[4096]{0:T(1024)} %param.25) | copy-start | bytes 49156
  237.0 17.7 %copy-start.5 = (f32[400]{0:T(512)S(1)}, f32[400]{0:T(512)}, u32[]{:S(2)}) copy-start(f32[400]{0:T(512)} %occ_ref.1) | copy-start | bytes 4804
  237.0 17.7 %copy-start.8 = (s32[8]{0:T(128)S(1)}, s32[8]{0:T(128)}, u32[]{:S(2)}) copy-start(s32[8]{0:T(128)} %slab.1) | copy-start | bytes 100
  237.0 17.7 %copy-start.9 = (s32[2]{0:T(128)S(1)}, s32[2]{0:T(128)}, u32[]{:S(2)}) copy-start(s32[2]{0:T(128)} %pair.1) | copy-start | bytes 28
Sparse Core Ops, SparseCore 0:
  10.5 115.6 all-gather.4
  129.3 105.3 all-gather.2

commit v2 on v1

--- a/solution.py
+++ b/solution.py
@@ -7,14 +7,37 @@
 
 F32 = jnp.float32
 BF16 = jnp.bfloat16
-
-
-def tile_of(ref, slot):
-    per_dev = ref.shape[0] * ref.shape[2]
-    return ref[(slot % per_dev) // ref.shape[2], slot // per_dev, slot % ref.shape[2]]
-
-
-def cycle_kernel(screen, rows, count, place, t_ref, z_ref, out_ref, mask):
+ANY = pl.BlockSpec(memory_space=pl.ANY)
+
+
+def tile_of(ref, slot, x):
+    xs, cores, _, share = ref.shape[:4]
+    within = slot % (xs * cores * share)
+    ahead = (within // (cores * share) - x) & (xs - 1)
+    return ref[ahead, (within // share) % cores, slot // (xs * cores * share), within % share]
+
+
+def load_tiles(place, mine, swapped, buf, sem):
+    copies = []
+    core = place[0] & 1
+    for pieces, at in ((mine, core), (swapped, 1 - core)):
+        near, behind, ahead, far_low, far_high = pieces
+        half = far_low.shape[0]
+        for src, dst in (
+            (near, buf.at[0, at]),
+            (ahead, buf.at[1, at]),
+            (behind, buf.at[3, at]),
+            (far_low, buf.at[2, at, pl.ds(0, half)]),
+            (far_high, buf.at[2, at, pl.ds(half, half)]),
+        ):
+            copies.append(pltpu.make_async_copy(src, dst, sem.at[len(copies)]))
+    for copy in copies:
+        copy.start()
+    return copies
+
+
+def cycle_kernel(screen, rows, count, place, t_hbm, *refs):
+    mine, swapped, (out_ref, mask, t_ref, z_ref, sem, t_sem) = refs[:5], refs[5:10], refs[10:]
     step = pl.program_id(0)
     tile = z_ref.shape[-1]
     height, width = t_ref.shape[2:]
@@ -22,9 +45,13 @@
     window, keep = t_ref.shape[1], screen.shape[1]
     tile_count = screen.shape[0] // window
     first = place[1] * tiles_here
+    x = place[0] // 2
 
     @pl.when(step == 0)
     def _():
+        copies = load_tiles(place, mine, swapped, z_ref, sem)
+        copies.append(pltpu.make_async_copy(t_hbm, t_ref, t_sem))
+        copies[-1].start()
         for a in range(tiles_here):
 
             @pl.loop(0, mask.shape[1])
@@ -34,6 +61,9 @@
             @pl.loop(0, count[first + a])
             def _(e):
                 mask[a, rows[first + a, e]] = 1
+
+        for copy in copies:
+            copy.wait()
 
     for j in range(window):
         for b in range(tiles_wide):
@@ -44,7 +74,7 @@
                 c = u % tile_count
                 lane = pl.multiple_of((c % tiles_wide) * tile, tile)
                 left.append(t_ref[c // tiles_wide, u // tile_count, :, pl.ds(lane, tile)])
-                right.append(tile_of(z_ref, q * keep + m))
+                right.append(tile_of(z_ref, q * keep + m, x))
             part = jnp.dot(
                 jnp.concatenate(left, axis=1),
                 jnp.concatenate(right, axis=0),
@@ -58,14 +88,24 @@
                 ).astype(BF16)
 
 
-def ladder_kernel(screen, slots, t_ref, w_ref, near_ref, out_ref):
+def ladder_kernel(screen, slots, place, t_ref, near_ref, *refs):
+    mine, swapped, (out_ref, w_ref, sem) = refs[:5], refs[5:10], refs[10:]
     step = pl.program_id(0)
     tile = w_ref.shape[-1]
     keep = screen.shape[1]
     group = out_ref.shape[1] // tile
+    x = place[0] // 2
+
+    @pl.when(step == 0)
+    def _():
+        for copy in load_tiles(place, mine, swapped, w_ref, sem):
+            copy.wait()
+
     for a in range(group):
         block = step * group + a
-        left = jnp.concatenate([tile_of(w_ref, slots[block * keep + k]) for k in range(keep)], axis=1)
+        left = jnp.concatenate(
+            [tile_of(w_ref, slots[block * keep + k], x) for k in range(keep)], axis=1
+        )
         for j in range(out_ref.shape[0]):
             right = jnp.concatenate([t_ref[j, screen[block, k]] for k in range(keep)], axis=0)
             here = slice(a * tile, (a + 1) * tile)
@@ -105,24 +145,58 @@
     tile_count = width_all // tile
     rows_here = width_all // vir_count
     share = stored // occ_count
+    xs, zs = occ_count // 2, 4
     occ_at, vir_at = lax.axis_index("occ"), lax.axis_index("vir")
     place = jnp.stack([occ_at, vir_at]).astype(jnp.int32)
     t = amplitudes[0]
     near = coulomb[0]
 
-    def gather(tiles):
-        mine = lax.dynamic_slice_in_dim(tiles, occ_at * share, share, 0)
-        full = lax.all_gather(mine, ("occ", "vir"), axis=0, tiled=True)
-        return full.reshape(occ_count, vir_count, share, tile, tile)
-
-    all_cycle = gather(cycle_tiles)
-    all_ladder = gather(ladder_tiles)
+    def occ_shift(value, by):
+        return lax.ppermute(value, "occ", [(i, (i + 2 * by) % occ_count) for i in range(occ_count)])
+
+    def core_swap(value):
+        return lax.ppermute(value, "occ", [(i, i ^ 1) for i in range(occ_count)])
+
+    def vir_shift(value, dy, dz):
+        ys = vir_count // zs
+        return lax.ppermute(
+            value,
+            "vir",
+            [(y * zs + z, (y + dy) % ys * zs + (z + dz) % zs) for y in range(ys) for z in range(zs)],
+        )
+
+    def spread(piece):
+        half = vir_count // 2
+        behind, ahead = occ_shift(piece, 1), occ_shift(piece, -1)
+        far_low, far_high = occ_shift(behind[:half], 1), occ_shift(ahead[half:], -1)
+        mine = (piece, behind, ahead, far_low, far_high)
+        return mine + tuple(core_swap(p) for p in mine)
+
+    def my_share(tiles):
+        return lax.dynamic_slice_in_dim(tiles, occ_at * share, share, 0)
+
+    sent = jnp.broadcast_to(my_share(cycle_tiles)[None], (vir_count, share, tile, tile))
+    cycle_piece = lax.all_to_all(sent, "vir", 0, 0, tiled=True)
     flat = t.reshape(window, vir_count, rows_here, block_cols).transpose(1, 0, 2, 3)
+    flat, cycle_piece, ladder_share = lax.optimization_barrier(
+        (flat, cycle_piece, my_share(ladder_tiles))
+    )
     moved = lax.all_to_all(flat, "vir", 0, 0, tiled=True)
+    cycle_parts = spread(cycle_piece)
+
+    line = jnp.stack([ladder_share] + [vir_shift(ladder_share, 0, d) for d in range(1, zs)])
+    plane = jnp.stack([line] + [vir_shift(line, d, 0) for d in range(1, vir_count // zs)])
+    y, z = vir_at // zs, vir_at % zs
+    plane = jnp.roll(jnp.flip(plane, (0, 1)), (y + 1, z + 1), (0, 1))
+    ladder_piece = plane.reshape(vir_count, share, tile, tile)
+    ladder_piece, *cycle_parts = lax.optimization_barrier((ladder_piece, *cycle_parts))
+    ladder_parts = spread(ladder_piece)
 
     resident = lambda *shape: pl.BlockSpec(shape, lambda *_: (0,) * len(shape))
     step_block = pl.BlockSpec((window, rows_here, block_cols), lambda g, *_: (0, g, 0))
     swap_block = pl.BlockSpec((1, window, rows_here, block_cols), lambda g, *_: (g, 0, 0, 0))
+    tile_buf = pltpu.VMEM((xs, 2, vir_count, share, tile, tile), BF16)
+    tile_sem = pltpu.SemaphoreType.DMA((10,))
     limit = pltpu.CompilerParams(vmem_limit_bytes=48 << 20)
     part = pl.pallas_call(
         cycle_kernel,
@@ -130,29 +204,39 @@
         grid_spec=pltpu.PrefetchScalarGridSpec(
             num_scalar_prefetch=4,
             grid=(vir_count,),
-            in_specs=[resident(*moved.shape), resident(*all_cycle.shape)],
+            in_specs=[ANY] * 11,
             out_specs=swap_block,
-            scratch_shapes=[pltpu.SMEM((rows_here // tile, window * tile_count), jnp.int32)],
+            scratch_shapes=[
+                pltpu.SMEM((rows_here // tile, window * tile_count), jnp.int32),
+                pltpu.VMEM(moved.shape, BF16),
+                tile_buf,
+                tile_sem,
+                pltpu.SemaphoreType.DMA(()),
+            ],
         ),
         compiler_params=limit,
-    )(cycle_screen, cycle_rows, cycle_count, place, moved, all_cycle)
+    )(cycle_screen, cycle_rows, cycle_count, place, moved, *cycle_parts)
     cycle = lax.all_to_all(part, "vir", 0, 0, tiled=True)
 
     base = pl.pallas_call(
         ladder_kernel,
         out_shape=jax.ShapeDtypeStruct(t.shape, F32),
         grid_spec=pltpu.PrefetchScalarGridSpec(
-            num_scalar_prefetch=2,
+            num_scalar_prefetch=3,
             grid=(vir_count,),
-            in_specs=[
-                resident(window, tile_count, tile, block_cols),
-                resident(*all_ladder.shape),
-                step_block,
-            ],
+            in_specs=[resident(window, tile_count, tile, block_cols), step_block] + [ANY] * 10,
             out_specs=step_block,
+            scratch_shapes=[tile_buf, tile_sem],
         ),
         compiler_params=limit,
-    )(ladder_screen, tile_slot, t.reshape(window, tile_count, tile, block_cols), all_ladder, near)
+    )(
+        ladder_screen,
+        tile_slot,
+        place,
+        t.reshape(window, tile_count, tile, block_cols),
+        near,
+        *ladder_parts,
+    )
 
     energies = vir_energy.reshape(1, width_all)
     out = pl.pallas_call(

time: 277 us -> 216 us (0.78)
  waiting for transfers between devices: 188 us -> 86.8 us
  starting transfers between devices: 13.5 us -> 57.8 us
  between operations: 13.5 us -> 0.28 us
  Pallas kernels: 48.5 us -> 52.2 us
  other arithmetic: 0.07 us -> 3.07 us
    all_gather x2 -> x0, waiting for transfers between devices: 130 us -> none  [gather(): full = lax.all_gather(mine, ('occ', 'vir'), axis=0, tiled=True)]
    ppermute x0 -> x24, waiting for transfers between devices: none -> 76.6 us  [the longest x6 42.1 us: vir_shift(): lax.ppermute(value, 'vir', [(y * zs + z, (y + dy) % ys * zs + (z + dz) %...]
    all_to_all x1, waiting for transfers between devices: 58 us -> 0.01 us  [body(): moved = lax.all_to_all(flat, 'vir', 0, 0, tiled=True)]
    ppermute x0 -> x24, starting transfers between devices: none -> 39.5 us  [the longest x10 21.5 us: core_swap(): return lax.ppermute(value, 'occ', [(i, i ^ 1) for i in range(occ_count)])]
    all_to_all x0 -> x1, waiting for transfers between devices: none -> 10.2 us  [body(): cycle_piece = lax.all_to_all(sent, 'vir', 0, 0, tiled=True)]
    all_to_all x0 -> x1, starting transfers between devices: none -> 8.59 us  [body(): cycle_piece = lax.all_to_all(sent, 'vir', 0, 0, tiled=True)]
    all_to_all x1, starting transfers between devices: 8.77 us -> 4.67 us  [body(): moved = lax.all_to_all(flat, 'vir', 0, 0, tiled=True)]
    slice x0 -> x4, local copies, waits for them, and re-layouts: none -> 4.08 us  [the longest x2 2.97 us: spread(): behind[:half]]
  transfers between devices with their start and end apart: 4 -> 27, of which waited for: 3 -> 8; matrix products, arithmetic and copies ran while one was open for 2% -> 7% of each run, Pallas kernels for 13% -> 9%
where the time goes in v2:
time: 216 us; the launch traced here: 215 us
  waiting for transfers between devices  86.8 us (40%)
  starting transfers between devices  57.8 us (27%)
  Pallas kernels  52.2 us (24%)
  local copies, waits for them, and re-layouts  14.7 us (7%)
  other arithmetic  3.07 us (1%)
    ppermute x6, waiting for transfers between devices, vir_shift(): lax.ppermute(value, 'vir', [(y * zs + z, (y + dy) % ys * zs + (z + dz) %...  42.1 us
    ppermute x8, waiting for transfers between devices, occ_shift(): lax.ppermute(value, 'occ', [(i, (i + 2 * by) % occ_count) for i in range(...  32.8 us
    ppermute x10, starting transfers between devices, core_swap(): return lax.ppermute(value, 'occ', [(i, i ^ 1) for i in range(occ_count)])  21.5 us
    pallas_call x1, Pallas kernels, body(): pl.pallas_call(ladder_kernel, out_shape=jax.ShapeDtypeStruct(t.shape, F32...  19.7 us
    pallas_call x1, Pallas kernels, body(): pl.pallas_call(cycle_kernel, out_shape=jax.ShapeDtypeStruct(moved.shape,...  18.5 us
    pallas_call x1, Pallas kernels, body(): pl.pallas_call(final_kernel, out_shape=jax.ShapeDtypeStruct(t.shape, BF16...  13.9 us
    all_to_all x1, waiting for transfers between devices, body(): cycle_piece = lax.all_to_all(sent, 'vir', 0, 0, tiled=True)  10.2 us
    ppermute x6, starting transfers between devices, vir_shift(): lax.ppermute(value, 'vir', [(y * zs + z, (y + dy) % ys * zs + (z + dz) %...  9.71 us
  transfers between devices with their start and end apart: 27, of which 8 were waited for; matrix products, arithmetic and copies ran while one was open for 7% of the time, Pallas kernels for 9%

profile of v2, /device:TPU:1, one launch (start us, length us, event | category | flops | bytes accessed | tf_op | source)
XLA Modules:
  0.0 214.8 jit_solution(2077170418189673985)
XLA Ops:
  2.3 8.6 %all-to-all-start = ((bf16[16,2,128,128]{3,2,1,0:T(8,128)(2,1)}), bf16[16,2,128,128]{3,2,1,0:T(8,128)(2,1)S(1)}, u32[]{:S(2)}, u32[]{:S(2)}) async-start(bf16[16,2,128,128]{3,2,1,0:T(8,128)(2,1)} %broadcast_in_dim.4), calls=%async_computation | async-start | bytes 2097152 | tf_op jit(solution)/shard_map/all_to_all | solution.py:179
  10.9 4.6 %copy.20 = bf16[2,16,256,256]{3,2,0,1:T(8,128)(2,1)} copy(bf16[2,16,256,256]{3,2,1,0:T(8,128)(2,1)} %bitcast.26) | data formatting | bytes 8388608 | tf_op jit(solution)/shard_map/reshape;squeeze | solution.py:180
  16.4 10.2 %all-to-all-done.refs_0_ = bf16[16,2,128,128]{3,2,1,0:T(8,128)(2,1)S(1)} async-done(((bf16[16,2,128,128]{3,2,1,0:T(8,128)(2,1)}), bf16[16,2,128,128]{3,2,1,0:T(8,128)(2,1)S(1)}, u32[]{:S(2)}, u32[]{:S(2)}) %all-to-all-start) | async-done | bytes 1048608 | tf_op jit(solution)/shard_map/all_to_all | solution.py:179
  26.5 4.7 %all-to-all-start.1 = ((bf16[16,2,256,256]{3,2,1,0:T(8,128)(2,1)}), bf16[16,2,256,256]{3,2,1,0:T(8,128)(2,1)}, u32[]{:S(2)}, u32[]{:S(2)}) async-start(bf16[16,2,256,256]{3,2,1,0:T(8,128)(2,1)} %bitcast.28), calls=%async_computation.1 | async-start | bytes 8388608 | tf_op jit(solution)/shard_map/all_to_all | solution.py:184
  31.2 2.5 %collective-permute-start.7 = (bf16[16,2,128,128]{3,2,1,0:T(8,128)(2,1)S(1)}, bf16[16,2,128,128]{3,2,1,0:T(8,128)(2,1)}, u32[]{:S(2)}, u32[]{:S(2)}) collective-permute-start(bf16[16,2,128,128]{3,2,1,0:T(8,128)(2,1)S(1)} %all-to-all-done.refs_0_), channel_id=1, source_target_pairs={{0,96},{16,112},{32,0},{48,16},{64,32},{80,48},{96,64},{112,80},{1... | collective-permute-start | bytes 3145736 | tf_op jit(solution)/shard_map/ppermute | solution.py:155
  33.8 2.3 %collective-permute-start.2 = (bf16[2,128,128]{2,1,0:T(8,128)(2,1)S(1)}, bf16[2,128,128]{2,1,0:T(8,128)(2,1)S(1)}, u32[]{:S(2)}, u32[]{:S(2)}) collective-permute-start(bf16[2,128,128]{2,1,0:T(8,128)(2,1)S(1)} %constant_dynamic-slice_fusion), channel_id=1, source_target_pairs={{0,3},{1,0},{2,1},{3,2},{4,7},{5,4},{6,5},{7,6},{8,11},{9,8},{10,9... | collective-permute-start | bytes 196616 | tf_op jit(solution)/shard_map/ppermute | solution.py:162
  37.3 9.6 %collective-permute-done.2 = bf16[2,128,128]{2,1,0:T(8,128)(2,1)S(1)} collective-permute-done((bf16[2,128,128]{2,1,0:T(8,128)(2,1)S(1)}, bf16[2,128,128]{2,1,0:T(8,128)(2,1)S(1)}, u32[]{:S(2)}, u32[]{:S(2)}) %collective-permute-start.2) | collective-permute-done | bytes 65568 | tf_op jit(solution)/shard_map/ppermute | solution.py:162
  46.8 10.6 %collective-permute-done.1 = bf16[2,128,128]{2,1,0:T(8,128)(2,1)S(1)} collective-permute-done((bf16[2,128,128]{2,1,0:T(8,128)(2,1)S(1)}, bf16[2,128,128]{2,1,0:T(8,128)(2,1)S(1)}, u32[]{:S(2)}, u32[]{:S(2)}) %collective-permute-start.1) | collective-permute-done | bytes 65568 | tf_op jit(solution)/shard_map/ppermute | solution.py:162
  57.4 21.9 %collective-permute-done = bf16[2,128,128]{2,1,0:T(8,128)(2,1)S(1)} collective-permute-done((bf16[2,128,128]{2,1,0:T(8,128)(2,1)S(1)}, bf16[2,128,128]{2,1,0:T(8,128)(2,1)S(1)}, u32[]{:S(2)}, u32[]{:S(2)}) %collective-permute-start) | collective-permute-done | bytes 65568 | tf_op jit(solution)/shard_map/ppermute | solution.py:162
  79.4 3.6 %collective-permute-start.4 = (bf16[4,2,128,128]{3,2,1,0:T(8,128)(2,1)S(1)}, bf16[4,2,128,128]{3,2,1,0:T(8,128)(2,1)S(1)}, u32[]{:S(2)}, u32[]{:S(2)}) collective-permute-start(bf16[4,2,128,128]{3,2,1,0:T(8,128)(2,1)S(1)} %get-tuple-element.34), channel_id=1, source_target_pairs={{0,8},{1,9},{2,10},{3,11},{4,12},{5,13},{6,14},{7,15},{8,0},{9,1},... | collective-permute-start | bytes 786440 | tf_op jit(solution)/shard_map/ppermute | solution.py:162
  86.7 2.5 %collective-permute-start.9 = (bf16[8,2,128,128]{3,2,1,0:T(8,128)(2,1)S(1)}, bf16[8,2,128,128]{3,2,1,0:T(8,128)(2,1)S(1)}, u32[]{:S(2)}, u32[]{:S(2)}) collective-permute-start(bf16[8,2,128,128]{3,2,1,0:T(8,128)(2,1)S(1)} %slice.17), channel_id=1, source_target_pairs={{0,96},{16,112},{32,0},{48,16},{64,32},{80,48},{96,64},{112,80},{1... | collective-permute-start | bytes 1572872 | tf_op jit(solution)/shard_map/ppermute | solution.py:155
  89.2 1.9 slice.16
  91.1 6.2 %collective-permute-start.10 = (bf16[16,2,128,128]{3,2,1,0:T(8,128)(2,1)S(1)}, bf16[16,2,128,128]{3,2,1,0:T(8,128)(2,1)}, u32[]{:S(2)}, u32[]{:S(2)}) collective-permute-start(bf16[16,2,128,128]{3,2,1,0:T(8,128)(2,1)S(1)} %all-to-all-done.refs_0_), channel_id=1, source_target_pairs={{0,16},{16,0},{32,48},{48,32},{64,80},{80,64},{96,112},{112,96},{1... | collective-permute-start | bytes 3145736 | tf_op jit(solution)/shard_map/ppermute | solution.py:158
  98.9 3.3 %collective-permute-start.14 = (bf16[8,2,128,128]{3,2,1,0:T(8,128)(2,1)S(1)}, bf16[8,2,128,128]{3,2,1,0:T(8,128)(2,1)}, u32[]{:S(2)}, u32[]{:S(2)}) collective-permute-start(bf16[8,2,128,128]{3,2,1,0:T(8,128)(2,1)S(1)} %collective-permute-done.9.refs_4_), channel_id=1, source_target_pairs={{0,16},{16,0},{32,48},{48,32},{64,80},{80,64},{96,112},{112,96},{1... | collective-permute-start | bytes 1572872 | tf_op jit(solution)/shard_map/ppermute | solution.py:158
  102.1 5.9 %collective-permute-start.13 = (bf16[8,2,128,128]{3,2,1,0:T(8,128)(2,1)}, bf16[8,2,128,128]{3,2,1,0:T(8,128)(2,1)}, u32[]{:S(2)}, u32[]{:S(2)}) collective-permute-start(bf16[8,2,128,128]{3,2,1,0:T(8,128)(2,1)} %collective-permute-done.8.refs_3_), channel_id=1, source_target_pairs={{0,16},{16,0},{32,48},{48,32},{64,80},{80,64},{96,112},{112,96},{1... | collective-permute-start | bytes 1572872 | tf_op jit(solution)/shard_map/ppermute | solution.py:158
  108.1 2.2 %pad_maximum_fusion = bf16[4,4,2,128,128]{4,3,2,1,0:T(8,128)(2,1)} fusion(bf16[1,4,2,128,128]{4,3,2,1,0:T(8,128)(2,1)} %bitcast.33, bf16[1,4,2,128,128]{4,3,2,1,0:T(8,128)(2,1)S(1)} %bitcast.31, bf16[1,4,2,128,128]{4,3,2,1,0:T(8,128)(2,1)} %bitcast.32, bf16[1,4,2,128,128]{4,3,2,1,0:T(8,128)(2,1)S(1)} %get-tuple-element.33), kind=kLoop, calls=%fused_computation.7 | loop fusion | flops 1572864 | bytes 2097152 | tf_op jit(solution)/shard_map/stack | solution.py:188
  112.5 18.5 %shard_map.128 = bf16[16,2,256,256]{3,2,1,0:T(8,128)(2,1)} custom-call(s32[64,4]{1,0:T(8,128)S(1)} %copy.18.screen, s32[32,48]{1,0:T(8,128)S(1)} %copy-done.2, s32[32]{0:T(128)S(1)} %copy-done.5, s32[2]{0:T(128)S(1)} %pad_add_fusion.place, bf16[16,2,256,256]{3,2,1,0:T(8,128)(2,1)} %all-to-all-done.1.t_hbm, ...), custom_call_target="tpu_custom_call" | custom-call | tf_op jit(solution)/shard_map/pallas_call | solution.py:201
  131.0 5.1 %all-to-all-start.2 = ((bf16[16,2,256,256]{3,2,1,0:T(8,128)(2,1)}), bf16[16,2,256,256]{3,2,1,0:T(8,128)(2,1)}, u32[]{:S(2)}, u32[]{:S(2)}) async-start(bf16[16,2,256,256]{3,2,1,0:T(8,128)(2,1)} %shard_map.128), calls=%async_computation.2 | async-start | bytes 8388608 | tf_op jit(solution)/shard_map/all_to_all | solution.py:219
  138.5 22.3 %collective-permute-done.16.refs_2_ = bf16[16,2,128,128]{3,2,1,0:T(8,128)(2,1)S(1)} collective-permute-done((bf16[16,2,128,128]{3,2,1,0:T(8,128)(2,1)S(1)}, bf16[16,2,128,128]{3,2,1,0:T(8,128)(2,1)S(1)}, u32[]{:S(2)}, u32[]{:S(2)}) %collective-permute-start.16) | collective-permute-done | bytes 1048608 | tf_op jit(solution)/shard_map/ppermute | solution.py:155
  165.1 8.4 %collective-permute-done.18.refs_4_ = bf16[8,2,128,128]{3,2,1,0:T(8,128)(2,1)S(1)} collective-permute-done((bf16[8,2,128,128]{3,2,1,0:T(8,128)(2,1)S(1)}, bf16[8,2,128,128]{3,2,1,0:T(8,128)(2,1)S(1)}, u32[]{:S(2)}, u32[]{:S(2)}) %collective-permute-start.18) | collective-permute-done | bytes 524320 | tf_op jit(solution)/shard_map/ppermute | solution.py:155
  175.2 2.1 collective-permute-done.17.refs_3_
  177.3 1.9 collective-permute-start.22
  181.1 19.7 %shard_map.127.base_ref = f32[2,4096,256]{2,1,0:T(8,128)} custom-call(s32[32,8]{1,0:T(8,128)S(1)} %copy.17.screen, s32[256]{0:T(256)S(1)} %copy-done.4, s32[2]{0:T(128)S(1)} %pad_add_fusion.place, bf16[2,32,128,256]{3,2,1,0:T(8,128)(2,1)} %bitcast.27, bf16[2,4096,256]{2,1,0:T(8,128)(2,1)} %bitcast.29, bf16[16,2,128,128]{3,2,1,0:T(8,128)(2,1)S(1)} %bitcast.23, ...), custom_call_target="tpu_custom_call" | custom-call | tf_op jit(solution)/shard_map/pallas_call | solution.py:221
  200.9 13.9 %shard_map.129 = bf16[2,4096,256]{2,1,0:T(8,128)(2,1)} custom-call(s32[8]{0:T(128)S(1)} %copy-done.6, s32[2]{0:T(128)S(1)} %copy-done.7, s32[2]{0:T(128)S(1)} %pad_add_fusion.place, f32[400]{0:T(512)S(1)} %copy-done.3, f32[2,4096,256]{2,1,0:T(8,128)} %shard_map.127.base_ref, bf16[16,2,256,256]{3,2,1,0:T(8,128)(2,1)} %all-to-all-done.2.cycle_ref, ...), custom_call_target="tpu_custom_call" | custom-call | tf_op jit(solution)/shard_map/pallas_call | solution.py:242
  (73 shorter events, 22.1 us)
Async XLA Ops:
  2.3 24.3 %all-to-all-start = ((bf16[16,2,128,128]{3,2,1,0:T(8,128)(2,1)}), bf16[16,2,128,128]{3,2,1,0:T(8,128)(2,1)S(1)}, u32[]{:S(2)}, u32[]{:S(2)}) async-start(bf16[16,2,128,128]{3,2,1,0:T(8,128)(2,1)} %broadcast_in_dim.4), calls=%async_computation | async-start | bytes 2097152 | tf_op jit(solution)/shard_map/all_to_all | solution.py:179
  26.5 85.9 %all-to-all-start.1 = ((bf16[16,2,256,256]{3,2,1,0:T(8,128)(2,1)}), bf16[16,2,256,256]{3,2,1,0:T(8,128)(2,1)}, u32[]{:S(2)}, u32[]{:S(2)}) async-start(bf16[16,2,256,256]{3,2,1,0:T(8,128)(2,1)} %bitcast.28), calls=%async_computation.1 | async-start | bytes 8388608 | tf_op jit(solution)/shard_map/all_to_all | solution.py:184
  31.2 54.4 %collective-permute-start.7 = (bf16[16,2,128,128]{3,2,1,0:T(8,128)(2,1)S(1)}, bf16[16,2,128,128]{3,2,1,0:T(8,128)(2,1)}, u32[]{:S(2)}, u32[]{:S(2)}) collective-permute-start(bf16[16,2,128,128]{3,2,1,0:T(8,128)(2,1)S(1)} %all-to-all-done.refs_0_), channel_id=1, source_target_pairs={{0,96},{16,112},{32,0},{48,16},{64,32},{80,48},{96,64},{112,80},{1... | collective-permute-start | bytes 3145736 | tf_op jit(solution)/shard_map/ppermute | solution.py:155
  33.8 55.5 %collective-permute-start.6 = (bf16[16,2,128,128]{3,2,1,0:T(8,128)(2,1)S(1)}, bf16[16,2,128,128]{3,2,1,0:T(8,128)(2,1)}, u32[]{:S(2)}, u32[]{:S(2)}) collective-permute-start(bf16[16,2,128,128]{3,2,1,0:T(8,128)(2,1)S(1)} %all-to-all-done.refs_0_), channel_id=1, source_target_pairs={{0,32},{16,48},{32,64},{48,80},{64,96},{80,112},{96,0},{112,16},{1... | collective-permute-start | bytes 3145736 | tf_op jit(solution)/shard_map/ppermute | solution.py:155
  33.8 13.1 %collective-permute-start.2 = (bf16[2,128,128]{2,1,0:T(8,128)(2,1)S(1)}, bf16[2,128,128]{2,1,0:T(8,128)(2,1)S(1)}, u32[]{:S(2)}, u32[]{:S(2)}) collective-permute-start(bf16[2,128,128]{2,1,0:T(8,128)(2,1)S(1)} %constant_dynamic-slice_fusion), channel_id=1, source_target_pairs={{0,3},{1,0},{2,1},{3,2},{4,7},{5,4},{6,5},{7,6},{8,11},{9,8},{10,9... | collective-permute-start | bytes 196616 | tf_op jit(solution)/shard_map/ppermute | solution.py:162
  36.1 21.3 %collective-permute-start.1 = (bf16[2,128,128]{2,1,0:T(8,128)(2,1)S(1)}, bf16[2,128,128]{2,1,0:T(8,128)(2,1)S(1)}, u32[]{:S(2)}, u32[]{:S(2)}) collective-permute-start(bf16[2,128,128]{2,1,0:T(8,128)(2,1)S(1)} %constant_dynamic-slice_fusion), channel_id=1, source_target_pairs={{0,2},{1,3},{2,0},{3,1},{4,6},{5,7},{6,4},{7,5},{8,10},{9,11},{10,... | collective-permute-start | bytes 196616 | tf_op jit(solution)/shard_map/ppermute | solution.py:162
  36.7 42.6 %collective-permute-start = (bf16[2,128,128]{2,1,0:T(8,128)(2,1)S(1)}, bf16[2,128,128]{2,1,0:T(8,128)(2,1)S(1)}, u32[]{:S(2)}, u32[]{:S(2)}) collective-permute-start(bf16[2,128,128]{2,1,0:T(8,128)(2,1)S(1)} %constant_dynamic-slice_fusion), channel_id=1, source_target_pairs={{0,1},{1,2},{2,3},{3,0},{4,5},{5,6},{6,7},{7,4},{8,9},{9,10},{10,1... | collective-permute-start | bytes 196616 | tf_op jit(solution)/shard_map/ppermute | solution.py:162
  79.4 11.8 %collective-permute-start.4 = (bf16[4,2,128,128]{3,2,1,0:T(8,128)(2,1)S(1)}, bf16[4,2,128,128]{3,2,1,0:T(8,128)(2,1)S(1)}, u32[]{:S(2)}, u32[]{:S(2)}) collective-permute-start(bf16[4,2,128,128]{3,2,1,0:T(8,128)(2,1)S(1)} %get-tuple-element.34), channel_id=1, source_target_pairs={{0,8},{1,9},{2,10},{3,11},{4,12},{5,13},{6,14},{7,15},{8,0},{9,1},... | collective-permute-start | bytes 786440 | tf_op jit(solution)/shard_map/ppermute | solution.py:162
  82.9 14.4 %collective-permute-start.3 = (bf16[4,2,128,128]{3,2,1,0:T(8,128)(2,1)S(1)}, bf16[4,2,128,128]{3,2,1,0:T(8,128)(2,1)S(1)}, u32[]{:S(2)}, u32[]{:S(2)}) collective-permute-start(bf16[4,2,128,128]{3,2,1,0:T(8,128)(2,1)S(1)} %get-tuple-element.34), channel_id=1, source_target_pairs={{0,4},{1,5},{2,6},{3,7},{4,8},{5,9},{6,10},{7,11},{8,12},{9,13},{1... | collective-permute-start | bytes 786440 | tf_op jit(solution)/shard_map/ppermute | solution.py:162
  84.0 13.4 %collective-permute-start.5 = (bf16[4,2,128,128]{3,2,1,0:T(8,128)(2,1)S(1)}, bf16[4,2,128,128]{3,2,1,0:T(8,128)(2,1)S(1)}, u32[]{:S(2)}, u32[]{:S(2)}) collective-permute-start(bf16[4,2,128,128]{3,2,1,0:T(8,128)(2,1)S(1)} %get-tuple-element.34), channel_id=1, source_target_pairs={{0,12},{1,13},{2,14},{3,15},{4,0},{5,1},{6,2},{7,3},{8,4},{9,5},{1... | collective-permute-start | bytes 786440 | tf_op jit(solution)/shard_map/ppermute | solution.py:162
  86.7 12.2 %collective-permute-start.9 = (bf16[8,2,128,128]{3,2,1,0:T(8,128)(2,1)S(1)}, bf16[8,2,128,128]{3,2,1,0:T(8,128)(2,1)S(1)}, u32[]{:S(2)}, u32[]{:S(2)}) collective-permute-start(bf16[8,2,128,128]{3,2,1,0:T(8,128)(2,1)S(1)} %slice.17), channel_id=1, source_target_pairs={{0,96},{16,112},{32,0},{48,16},{64,32},{80,48},{96,64},{112,80},{1... | collective-permute-start | bytes 1572872 | tf_op jit(solution)/shard_map/ppermute | solution.py:155
  91.1 11.0 %collective-permute-start.8 = (bf16[8,2,128,128]{3,2,1,0:T(8,128)(2,1)}, bf16[8,2,128,128]{3,2,1,0:T(8,128)(2,1)}, u32[]{:S(2)}, u32[]{:S(2)}) collective-permute-start(bf16[8,2,128,128]{3,2,1,0:T(8,128)(2,1)} %slice.16), channel_id=1, source_target_pairs={{0,32},{16,48},{32,64},{48,80},{64,96},{80,112},{96,0},{112,16},{1... | collective-permute-start | bytes 1572872 | tf_op jit(solution)/shard_map/ppermute | solution.py:155
  91.1 21.3 %collective-permute-start.10 = (bf16[16,2,128,128]{3,2,1,0:T(8,128)(2,1)S(1)}, bf16[16,2,128,128]{3,2,1,0:T(8,128)(2,1)}, u32[]{:S(2)}, u32[]{:S(2)}) collective-permute-start(bf16[16,2,128,128]{3,2,1,0:T(8,128)(2,1)S(1)} %all-to-all-done.refs_0_), channel_id=1, source_target_pairs={{0,16},{16,0},{32,48},{48,32},{64,80},{80,64},{96,112},{112,96},{1... | collective-permute-start | bytes 3145736 | tf_op jit(solution)/shard_map/ppermute | solution.py:158
  97.3 15.1 %collective-permute-start.12 = (bf16[16,2,128,128]{3,2,1,0:T(8,128)(2,1)}, bf16[16,2,128,128]{3,2,1,0:T(8,128)(2,1)}, u32[]{:S(2)}, u32[]{:S(2)}) collective-permute-start(bf16[16,2,128,128]{3,2,1,0:T(8,128)(2,1)} %collective-permute-done.7.refs_2_), channel_id=1, source_target_pairs={{0,16},{16,0},{32,48},{48,32},{64,80},{80,64},{96,112},{112,96},{1... | collective-permute-start | bytes 3145736 | tf_op jit(solution)/shard_map/ppermute | solution.py:158
  98.7 13.7 %collective-permute-start.11 = (bf16[16,2,128,128]{3,2,1,0:T(8,128)(2,1)}, bf16[16,2,128,128]{3,2,1,0:T(8,128)(2,1)}, u32[]{:S(2)}, u32[]{:S(2)}) collective-permute-start(bf16[16,2,128,128]{3,2,1,0:T(8,128)(2,1)} %collective-permute-done.6.refs_1_), channel_id=1, source_target_pairs={{0,16},{16,0},{32,48},{48,32},{64,80},{80,64},{96,112},{112,96},{1... | collective-permute-start | bytes 3145736 | tf_op jit(solution)/shard_map/ppermute | solution.py:158
  98.9 13.5 %collective-permute-start.14 = (bf16[8,2,128,128]{3,2,1,0:T(8,128)(2,1)S(1)}, bf16[8,2,128,128]{3,2,1,0:T(8,128)(2,1)}, u32[]{:S(2)}, u32[]{:S(2)}) collective-permute-start(bf16[8,2,128,128]{3,2,1,0:T(8,128)(2,1)S(1)} %collective-permute-done.9.refs_4_), channel_id=1, source_target_pairs={{0,16},{16,0},{32,48},{48,32},{64,80},{80,64},{96,112},{112,96},{1... | collective-permute-start | bytes 1572872 | tf_op jit(solution)/shard_map/ppermute | solution.py:158
  131.0 69.9 %all-to-all-start.2 = ((bf16[16,2,256,256]{3,2,1,0:T(8,128)(2,1)}), bf16[16,2,256,256]{3,2,1,0:T(8,128)(2,1)}, u32[]{:S(2)}, u32[]{:S(2)}) async-start(bf16[16,2,256,256]{3,2,1,0:T(8,128)(2,1)} %shard_map.128), calls=%async_computation.2 | async-start | bytes 8388608 | tf_op jit(solution)/shard_map/all_to_all | solution.py:219
  136.1 24.6 %collective-permute-start.16 = (bf16[16,2,128,128]{3,2,1,0:T(8,128)(2,1)S(1)}, bf16[16,2,128,128]{3,2,1,0:T(8,128)(2,1)S(1)}, u32[]{:S(2)}, u32[]{:S(2)}) collective-permute-start(bf16[16,2,128,128]{3,2,1,0:T(8,128)(2,1)S(1)} %bitcast.20), channel_id=1, source_target_pairs={{0,96},{16,112},{32,0},{48,16},{64,32},{80,48},{96,64},{112,80},{1... | collective-permute-start | bytes 3145736 | tf_op jit(solution)/shard_map/ppermute | solution.py:155
  136.2 26.2 %collective-permute-start.15 = (bf16[16,2,128,128]{3,2,1,0:T(8,128)(2,1)S(1)}, bf16[16,2,128,128]{3,2,1,0:T(8,128)(2,1)}, u32[]{:S(2)}, u32[]{:S(2)}) collective-permute-start(bf16[16,2,128,128]{3,2,1,0:T(8,128)(2,1)S(1)} %bitcast.21), channel_id=1, source_target_pairs={{0,32},{16,48},{32,64},{48,80},{64,96},{80,112},{96,0},{112,16},{1... | collective-permute-start | bytes 3145736 | tf_op jit(solution)/shard_map/ppermute | solution.py:155
  137.7 41.6 %collective-permute-start.19 = (bf16[16,2,128,128]{3,2,1,0:T(8,128)(2,1)S(1)}, bf16[16,2,128,128]{3,2,1,0:T(8,128)(2,1)}, u32[]{:S(2)}, u32[]{:S(2)}) collective-permute-start(bf16[16,2,128,128]{3,2,1,0:T(8,128)(2,1)S(1)} %bitcast.22), channel_id=1, source_target_pairs={{0,16},{16,0},{32,48},{48,32},{64,80},{80,64},{96,112},{112,96},{1... | collective-permute-start | bytes 3145736 | tf_op jit(solution)/shard_map/ppermute | solution.py:158
  160.8 12.6 %collective-permute-start.18 = (bf16[8,2,128,128]{3,2,1,0:T(8,128)(2,1)S(1)}, bf16[8,2,128,128]{3,2,1,0:T(8,128)(2,1)S(1)}, u32[]{:S(2)}, u32[]{:S(2)}) collective-permute-start(bf16[8,2,128,128]{3,2,1,0:T(8,128)(2,1)S(1)} %slice.19), channel_id=1, source_target_pairs={{0,96},{16,112},{32,0},{48,16},{64,32},{80,48},{96,64},{112,80},{1... | collective-permute-start | bytes 1572872 | tf_op jit(solution)/shard_map/ppermute | solution.py:155
  163.5 13.9 %collective-permute-start.17 = (bf16[8,2,128,128]{3,2,1,0:T(8,128)(2,1)S(1)}, bf16[8,2,128,128]{3,2,1,0:T(8,128)(2,1)}, u32[]{:S(2)}, u32[]{:S(2)}) collective-permute-start(bf16[8,2,128,128]{3,2,1,0:T(8,128)(2,1)S(1)} %slice.18), channel_id=1, source_target_pairs={{0,32},{16,48},{32,64},{48,80},{64,96},{80,112},{96,0},{112,16},{1... | collective-permute-start | bytes 1572872 | tf_op jit(solution)/shard_map/ppermute | solution.py:155
  163.6 17.5 %collective-permute-start.21 = (bf16[16,2,128,128]{3,2,1,0:T(8,128)(2,1)S(1)}, bf16[16,2,128,128]{3,2,1,0:T(8,128)(2,1)}, u32[]{:S(2)}, u32[]{:S(2)}) collective-permute-start(bf16[16,2,128,128]{3,2,1,0:T(8,128)(2,1)S(1)} %collective-permute-done.16.refs_2_), channel_id=1, source_target_pairs={{0,16},{16,0},{32,48},{48,32},{64,80},{80,64},{96,112},{112,96},{1... | collective-permute-start | bytes 3145736 | tf_op jit(solution)/shard_map/ppermute | solution.py:158
  165.1 16.0 %collective-permute-start.20 = (bf16[16,2,128,128]{3,2,1,0:T(8,128)(2,1)}, bf16[16,2,128,128]{3,2,1,0:T(8,128)(2,1)}, u32[]{:S(2)}, u32[]{:S(2)}) collective-permute-start(bf16[16,2,128,128]{3,2,1,0:T(8,128)(2,1)} %collective-permute-done.15.refs_1_), channel_id=1, source_target_pairs={{0,16},{16,0},{32,48},{48,32},{64,80},{80,64},{96,112},{112,96},{1... | collective-permute-start | bytes 3145736 | tf_op jit(solution)/shard_map/ppermute | solution.py:158
  (15 other events, 280.6 us)

commit v3 on v2

v3 whole, which is shorter than its diff:
```python
import jax
import jax.numpy as jnp
from jax import lax
from jax.experimental import pallas as pl
from jax.experimental.pallas import tpu as pltpu
from jax.sharding import PartitionSpec as P

F32 = jnp.float32
BF16 = jnp.bfloat16
ANY = pl.BlockSpec(memory_space=pl.ANY)


SCALARS = pl.BlockSpec(memory_space=pltpu.SMEM)
FULL_VMEM = pltpu.CompilerParams(vmem_limit_bytes=60 << 20)


def tile_copies(place, pieces, buf, sem):
    xs = buf.shape[1]
    core, x = place[0] & 1, place[0] // 2
    groups = [[], [], [], []]
    for side, at in ((pieces[:5], core), (pieces[5:], 1 - core)):
        near, behind, ahead, far_low, far_high = side
        half = far_low.shape[0]
        whole = slice(None)
        for src, group, shift, where in (
            (near, 0, 0, whole),
            (behind, 1, xs - 1, whole),
            (ahead, 2, 1, whole),
            (far_low, 3, 2, pl.ds(0, half)),
            (far_high, 3, 2, pl.ds(half, half)),
        ):
            dst = buf.at[where, (x + shift) & (xs - 1), at]
            count = sum(map(len, groups))
            groups[group].append(pltpu.make_async_copy(src, dst, sem.at[count]))
    return groups


def chunk_copies(src, dst, sem):
    chunk = dst.shape[0] // sem.shape[0]
    return [
        pltpu.make_async_copy(src.at[pl.ds(i * chunk, chunk)], dst.at[pl.ds(i * chunk, chunk)], sem.at[i])
        for i in range(sem.shape[0])
    ]


def cycle_kernel(screen, rows, count, place, t_hbm, *refs):
    pieces, (out_hbm, mask, t_ref, z_ref, o_ref, t_sem, z_sem, o_sem) = refs[:10], refs[10:]
    keep, tile = screen.shape[1], z_ref.shape[-1]
    parts, window, height, width = t_ref.shape
    tiles_here, tiles_wide = height // tile, width // tile
    tile_count = screen.shape[0] // window
    vir, xs = z_ref.shape[:2]
    first = place[1] * tiles_here
    moves = chunk_copies(t_hbm, t_ref, t_sem)
    groups = tile_copies(place, pieces, z_ref, z_sem)
    for copy in moves + sum(groups, []):
        copy.start()
    for a in range(tiles_here):

        @pl.loop(0, mask.shape[1])
        def _(q):
            mask[a, q] = 0

        @pl.loop(0, count[first + a])
        def _(e):
            mask[a, rows[first + a, e]] = 1

    for copy in moves:
        copy.wait()

    def one(v, x):
        q = v * xs + x
        j, c_out = q // tile_count, q % tile_count
        step, lane_out = c_out // tiles_wide, c_out % tiles_wide
        left = []
        for m in range(keep):
            u = screen[q, m]
            c = u % tile_count
            lane = pl.multiple_of((c % tiles_wide) * tile, tile)
            left.append(t_ref[c // tiles_wide, u // tile_count, :, pl.ds(lane, tile)])
        right = z_ref[v, x].reshape(keep * tile, tile)
        part = jnp.dot(jnp.concatenate(left, axis=1), right, preferred_element_type=F32)
        for a in range(tiles_here):
            here = slice(a * tile, (a + 1) * tile)
            used = jnp.full((tile, tile), mask[a, q], jnp.int32) > 0
            lanes = pl.ds(pl.multiple_of(lane_out * tile, tile), tile)
            o_ref[step, j, here, lanes] = jnp.where(used, part[here], 0.0).astype(BF16)

    unroll = 4
    for group, shift in zip(groups, (0, xs - 1, 1, 2), strict=True):
        for copy in group:
            copy.wait()
        x = (place[0] // 2 + shift) & (xs - 1)

        @pl.loop(0, vir // unroll)
        def _(outer):
            for inner in range(unroll):
                one(outer * unroll + inner, x)

    out = pltpu.make_async_copy(o_ref, out_hbm, o_sem)
    out.start()
    out.wait()


def ladder_kernel(screen, slots, place, t_hbm, near_hbm, *refs):
    pieces, (out_hbm, t_ref, near_ref, w_ref, out_ref, t_sem, near_sem, w_sem, o_sem) = (
        refs[:10],
        refs[10:],
    )
    keep = screen.shape[1]
    window, blocks, tile, _ = t_ref.shape
    per_dev = w_ref.shape[1] * w_ref.shape[2] * w_ref.shape[3]
    share = w_ref.shape[3]
    copies = sum(tile_copies(place, pieces, w_ref, w_sem), []) + chunk_copies(t_hbm, t_ref, t_sem)
    copies += chunk_copies(near_hbm, near_ref, near_sem)
    for copy in copies:
        copy.start()
    for copy in copies:
        copy.wait()

    def one(block):
        tiles = []
        for k in range(keep):
            slot = slots[block * keep + k]
            within = slot % per_dev
            tiles.append(
                w_ref[slot // per_dev, within // (2 * share), (within // share) % 2, within % share]
            )
        left = jnp.concatenate(tiles, axis=1)
        for j in range(window):
            right = jnp.concatenate([t_ref[j, screen[block, k]] for k in range(keep)], axis=0)
            out_ref[j, block] = near_ref[j, block].astype(F32) + jnp.dot(
                left, right, preferred_element_type=F32
            )

    unroll = 2
    quarter = blocks // 4
    for part in range(4):

        @pl.loop(0, quarter // unroll)
        def _(outer):
            for inner in range(unroll):
                one(part * quarter + outer * unroll + inner)

        where = pl.ds(part * quarter, quarter)
        pltpu.make_async_copy(out_ref.at[:, where], out_hbm.at[:, where], o_sem.at[part]).start()
    for part in range(4):
        where = pl.ds(part * quarter, quarter)
        pltpu.make_async_copy(out_ref.at[:, where], out_hbm.at[:, where], o_sem.at[part]).wait()


def final_kernel(slab, pair, place, occ_ref, base_ref, cycle_ref, va_ref, vb_ref, out_ref):
    group, window, rows, cols = cycle_ref.shape
    for g in range(group):
        here = slice(g * rows, (g + 1) * rows)
        energy_a = jnp.broadcast_to(va_ref[:, here], (128, rows)).T
        pairs = jnp.concatenate([energy_a] * (cols // 128), axis=1) + vb_ref[...]
        for j in range(window):
            below = (pairs - occ_ref[slab[place[0]]]) - occ_ref[pair[j]]
            value = base_ref[j, here] + cycle_ref[g, j].astype(F32)
            out_ref[j, here] = (value / below).astype(BF16)


def body(
    amplitudes,
    coulomb,
    ladder_tiles,
    cycle_tiles,
    ladder_screen,
    tile_slot,
    cycle_screen,
    cycle_rows,
    cycle_count,
    slab_occ,
    window_occ,
    occ_energy,
    vir_energy,
):
    occ_count, vir_count = lax.axis_size("occ"), lax.axis_size("vir")
    _, window, width_all, block_cols = amplitudes.shape
    stored, tile, _ = ladder_tiles.shape
    tile_count = width_all // tile
    rows_here = width_all // vir_count
    share = stored // occ_count
    xs, zs = occ_count // 2, 4
    occ_at, vir_at = lax.axis_index("occ"), lax.axis_index("vir")
    place = jnp.stack([occ_at, vir_at]).astype(jnp.int32)
    t = amplitudes[0]
    near = coulomb[0]

    def occ_shift(value, by):
        return lax.ppermute(value, "occ", [(i, (i + 2 * by) % occ_count) for i in range(occ_count)])

    def core_swap(value):
        return lax.ppermute(value, "occ", [(i, i ^ 1) for i in range(occ_count)])

    def vir_shift(value, dy, dz):
        ys = vir_count // zs
        return lax.ppermute(
            value,
            "vir",
            [(y * zs + z, (y + dy) % ys * zs + (z + dz) % zs) for y in range(ys) for z in range(zs)],
        )

    def ring(value, shift):
        half = value.shape[0] // 2
        behind, ahead = shift(value, 1), shift(value, -1)
        far = jnp.concatenate([shift(behind[:half], 1), shift(ahead[half:], -1)])
        return jnp.stack([value, behind, far, ahead])

    def spread(piece):
        half = vir_count // 2
        behind, ahead = occ_shift(piece, 1), occ_shift(piece, -1)
        far_low, far_high = occ_shift(behind[:half], 1), occ_shift(ahead[half:], -1)
        mine = (piece, behind, ahead, far_low, far_high)
        return mine + tuple(core_swap(p) for p in mine)

    def my_share(tiles):
        return lax.dynamic_slice_in_dim(tiles, occ_at * share, share, 0)

    sent = jnp.broadcast_to(my_share(cycle_tiles)[None], (vir_count, share, tile, tile))
    cycle_piece = lax.all_to_all(sent, "vir", 0, 0, tiled=True)
    line = ring(my_share(ladder_tiles), lambda value, by: vir_shift(value, 0, by))
    plane = ring(line, lambda value, by: vir_shift(value, by, 0))
    flat = t.reshape(window, vir_count, rows_here, block_cols).transpose(1, 0, 2, 3)
    flat, cycle_piece, plane = lax.optimization_barrier((flat, cycle_piece, plane))
    moved = lax.all_to_all(flat, "vir", 0, 0, tiled=True)
    cycle_parts = spread(cycle_piece)

    y, z = vir_at // zs, vir_at % zs
    plane = jnp.roll(jnp.flip(plane, (0, 1)), (y + 1, z + 1), (0, 1))
    ladder_piece = plane.reshape(vir_count, share, tile, tile)
    ladder_piece, *_ = lax.optimization_barrier((ladder_piece, *cycle_parts[3:5]))
    ladder_parts = spread(ladder_piece)

    tile_buf = pltpu.VMEM((vir_count, xs, 2, share, tile, tile), BF16)
    dma = pltpu.SemaphoreType.DMA
    part = pl.pallas_call(
        cycle_kernel,
        out_shape=jax.ShapeDtypeStruct(moved.shape, BF16),
        grid_spec=pltpu.PrefetchScalarGridSpec(
            num_scalar_prefetch=4,
            grid=(1,),
            in_specs=[ANY] * 11,
            out_specs=ANY,
            scratch_shapes=[
                pltpu.SMEM((rows_here // tile, window * tile_count), jnp.int32),
                pltpu.VMEM(moved.shape, BF16),
                tile_buf,
                pltpu.VMEM(moved.shape, BF16),
                dma((2,)),
                dma((10,)),
                dma(()),
            ],
        ),
        compiler_params=FULL_VMEM,
    )(cycle_screen, cycle_rows, cycle_count, place, moved, *cycle_parts)
    cycle = lax.all_to_all(part, "vir", 0, 0, tiled=True)

    blocked = (window, tile_count, tile, block_cols)
    base = pl.pallas_call(
        ladder_kernel,
        out_shape=jax.ShapeDtypeStruct(blocked, F32),
        grid_spec=pltpu.PrefetchScalarGridSpec(
            num_scalar_prefetch=3,
            grid=(1,),
            in_specs=[ANY] * 12,
            out_specs=ANY,
            scratch_shapes=[
                pltpu.VMEM(blocked, BF16),
                pltpu.VMEM(blocked, BF16),
                tile_buf,
                pltpu.VMEM(blocked, F32),
                dma((2,)),
                dma((2,)),
                dma((10,)),
                dma((4,)),
            ],
        ),
        compiler_params=FULL_VMEM,
    )(ladder_screen, tile_slot, place, t.reshape(blocked), near.reshape(blocked), *ladder_parts)

    energies = vir_energy.reshape(1, width_all)
    group = 4
    out = pl.pallas_call(
        final_kernel,
        out_shape=jax.ShapeDtypeStruct(t.shape, BF16),
        grid_spec=pltpu.PrefetchScalarGridSpec(
            num_scalar_prefetch=3,
            grid=(vir_count // group,),
            in_specs=[
                SCALARS,
                pl.BlockSpec((window, group * rows_here, block_cols), lambda g, *_: (0, g, 0)),
                pl.BlockSpec((group, window, rows_here, block_cols), lambda g, *_: (g, 0, 0, 0)),
                pl.BlockSpec((1, group * rows_here), lambda g, *_: (0, g)),
                pl.BlockSpec((1, block_cols), lambda g, slab, pair, place: (0, place[1])),
            ],
            out_specs=pl.BlockSpec((window, group * rows_here, block_cols), lambda g, *_: (0, g, 0)),
        ),
        compiler_params=FULL_VMEM,
    )(
        slab_occ,
        window_occ,
        place,
        occ_energy,
        base.reshape(t.shape),
        cycle,
        energies,
        energies,
    )
    return out[None]


def solution(mesh):
    wide = P("occ", None, None, "vir")
    tiles = P("vir", None, None)
    return jax.shard_map(
        body,
        mesh=mesh,
        in_specs=(wide, wide, tiles, tiles) + (P(),) * 9,
        out_specs=wide,
        check_vma=False,
    )
```

time: 216 us -> 191 us (0.88)
  waiting for transfers between devices: 86.8 us -> 58.1 us
  starting transfers between devices: 57.8 us -> 77.5 us
  Pallas kernels: 52.2 us -> 40.2 us
    ppermute x6 -> x8, waiting for transfers between devices: 42.1 us -> 8.52 us  [vir_shift(): lax.ppermute(value, 'vir', [(y * zs + z, (y + dy) % ys * zs + (z + dz) %...]
    ppermute x6 -> x8, starting transfers between devices: 9.71 us -> 22.2 us  [vir_shift(): lax.ppermute(value, 'vir', [(y * zs + z, (y + dy) % ys * zs + (z + dz) %...]
    all_to_all x1, waiting for transfers between devices: 10.2 us -> 0.01 us  [body(): cycle_piece = lax.all_to_all(sent, 'vir', 0, 0, tiled=True)]
    all_to_all x1, waiting for transfers between devices: 0.01 us -> 8.48 us  [body(): moved = lax.all_to_all(flat, 'vir', 0, 0, tiled=True)]
    ppermute x8, waiting for transfers between devices: 32.8 us -> 39.3 us  [occ_shift(): lax.ppermute(value, 'occ', [(i, (i + 2 * by) % occ_count) for i in range(...]
    ppermute x10, starting transfers between devices: 21.5 us -> 26.7 us  [core_swap(): return lax.ppermute(value, 'occ', [(i, i ^ 1) for i in range(occ_count)])]
    pallas_call x1, Pallas kernels: 13.9 us -> 8.76 us  [body(): pl.pallas_call(final_kernel, out_shape=jax.ShapeDtypeStruct(t.shape, BF16...]
    pallas_call x1, Pallas kernels: 18.5 us -> 14.2 us  [body(): pl.pallas_call(cycle_kernel, out_shape=jax.ShapeDtypeStruct(moved.shape,...]
  transfers between devices with their start and end apart: 27 -> 29, of which waited for: 8 -> 9; matrix products, arithmetic and copies ran while one was open for 7% -> 7% of each run, Pallas kernels for 9% -> 9%
where the time goes in v3:
time: 191 us; the launch traced here: 190 us
  starting transfers between devices  77.5 us (41%)
  waiting for transfers between devices  58.1 us (30%)
  Pallas kernels  40.2 us (21%)
  local copies, waits for them, and re-layouts  12.6 us (7%)
    ppermute x8, waiting for transfers between devices, occ_shift(): lax.ppermute(value, 'occ', [(i, (i + 2 * by) % occ_count) for i in range(...  39.3 us
    ppermute x10, starting transfers between devices, core_swap(): return lax.ppermute(value, 'occ', [(i, i ^ 1) for i in range(occ_count)])  26.7 us
    ppermute x8, starting transfers between devices, vir_shift(): lax.ppermute(value, 'vir', [(y * zs + z, (y + dy) % ys * zs + (z + dz) %...  22.2 us
    pallas_call x1, Pallas kernels, body(): pl.pallas_call(ladder_kernel, out_shape=jax.ShapeDtypeStruct(blocked, F32...  17.3 us
    pallas_call x1, Pallas kernels, body(): pl.pallas_call(cycle_kernel, out_shape=jax.ShapeDtypeStruct(moved.shape,...  14.2 us
    ppermute x8, starting transfers between devices, occ_shift(): lax.ppermute(value, 'occ', [(i, (i + 2 * by) % occ_count) for i in range(...  11.2 us
    pallas_call x1, Pallas kernels, body(): pl.pallas_call(final_kernel, out_shape=jax.ShapeDtypeStruct(t.shape, BF16...  8.76 us
    ppermute x8, waiting for transfers between devices, vir_shift(): lax.ppermute(value, 'vir', [(y * zs + z, (y + dy) % ys * zs + (z + dz) %...  8.52 us
  transfers between devices with their start and end apart: 29, of which 9 were waited for; matrix products, arithmetic and copies ran while one was open for 7% of the time, Pallas kernels for 9%

profile of v3, /device:TPU:1, one launch (start us, length us, event | category | flops | bytes accessed | tf_op | source)
XLA Modules:
  0.0 190.4 jit_solution(16520525314593090402)
XLA Ops:
  1.0 2.5 %collective-permute-start = (bf16[2,128,128]{2,1,0:T(8,128)(2,1)S(1)}, bf16[2,128,128]{2,1,0:T(8,128)(2,1)S(1)}, u32[]{:S(2)}, u32[]{:S(2)}) collective-permute-start(bf16[2,128,128]{2,1,0:T(8,128)(2,1)S(1)} %constant_dynamic-slice_fusion), channel_id=1, source_target_pairs={{0,1},{1,2},{2,3},{3,0},{4,5},{5,6},{6,7},{7,4},{8,9},{9,10},{10,1... | collective-permute-start | bytes 196616 | tf_op jit(solution)/shard_map/ppermute | solution.py:199
  7.8 5.4 %all-to-all-start = ((bf16[16,2,128,128]{3,2,1,0:T(8,128)(2,1)}), bf16[16,2,128,128]{3,2,1,0:T(8,128)(2,1)S(1)}, u32[]{:S(2)}, u32[]{:S(2)}) async-start(bf16[16,2,128,128]{3,2,1,0:T(8,128)(2,1)} %broadcast_in_dim.4), calls=%async_computation | async-start | bytes 2097152 | tf_op jit(solution)/shard_map/all_to_all | solution.py:222
  16.0 2.7 %collective-permute-done.1 = bf16[1,128,128]{2,1,0:T(8,128)(2,1)S(1)} collective-permute-done((bf16[1,128,128]{2,1,0:T(8,128)(2,1)S(1)}, bf16[1,128,128]{2,1,0:T(8,128)(2,1)S(1)}, u32[]{:S(2)}, u32[]{:S(2)}) %collective-permute-start.1) | collective-permute-done | bytes 32800 | tf_op jit(solution)/shard_map/ppermute | solution.py:199
  18.7 10.3 %collective-permute-start.4 = (bf16[4,2,128,128]{3,2,1,0:T(8,128)(2,1)S(1)}, bf16[4,2,128,128]{3,2,1,0:T(8,128)(2,1)S(1)}, u32[]{:S(2)}, u32[]{:S(2)}) collective-permute-start(bf16[4,2,128,128]{3,2,1,0:T(8,128)(2,1)S(1)} %get-tuple-element.14), channel_id=1, source_target_pairs={{0,4},{1,5},{2,6},{3,7},{4,8},{5,9},{6,10},{7,11},{8,12},{9,13},{1... | collective-permute-start | bytes 786440 | tf_op jit(solution)/shard_map/ppermute | solution.py:199
  30.7 5.8 %collective-permute-done.4 = bf16[4,2,128,128]{3,2,1,0:T(8,128)(2,1)S(1)} collective-permute-done((bf16[4,2,128,128]{3,2,1,0:T(8,128)(2,1)S(1)}, bf16[4,2,128,128]{3,2,1,0:T(8,128)(2,1)S(1)}, u32[]{:S(2)}, u32[]{:S(2)}) %collective-permute-start.4) | collective-permute-done | bytes 262176 | tf_op jit(solution)/shard_map/ppermute | solution.py:199
  36.6 2.7 %collective-permute-start.7 = (bf16[2,2,128,128]{3,2,1,0:T(8,128)(2,1)S(1)}, bf16[2,2,128,128]{3,2,1,0:T(8,128)(2,1)S(1)}, u32[]{:S(2)}, u32[]{:S(2)}) collective-permute-start(bf16[2,2,128,128]{3,2,1,0:T(8,128)(2,1)S(1)} %slice.35), channel_id=1, source_target_pairs={{0,12},{1,13},{2,14},{3,15},{4,0},{5,1},{6,2},{7,3},{8,4},{9,5},{1... | collective-permute-start | bytes 393224 | tf_op jit(solution)/shard_map/ppermute | solution.py:199
  39.3 4.6 %copy.20 = bf16[2,16,256,256]{3,2,0,1:T(8,128)(2,1)} copy(bf16[2,16,256,256]{3,2,1,0:T(8,128)(2,1)} %bitcast.25) | data formatting | bytes 8388608 | tf_op jit(solution)/shard_map/reshape;squeeze | solution.py:225
  44.2 4.7 %all-to-all-start.1 = ((bf16[16,2,256,256]{3,2,1,0:T(8,128)(2,1)}), bf16[16,2,256,256]{3,2,1,0:T(8,128)(2,1)}, u32[]{:S(2)}, u32[]{:S(2)}) async-start(bf16[16,2,256,256]{3,2,1,0:T(8,128)(2,1)} %bitcast.27), calls=%async_computation.1 | async-start | bytes 8388608 | tf_op jit(solution)/shard_map/all_to_all | solution.py:227
  51.6 2.5 %collective-permute-start.21 = (bf16[16,2,128,128]{3,2,1,0:T(8,128)(2,1)S(1)}, bf16[16,2,128,128]{3,2,1,0:T(8,128)(2,1)}, u32[]{:S(2)}, u32[]{:S(2)}) collective-permute-start(bf16[16,2,128,128]{3,2,1,0:T(8,128)(2,1)S(1)} %all-to-all-done.refs_0_), channel_id=1, source_target_pairs={{0,16},{16,0},{32,48},{48,32},{64,80},{80,64},{96,112},{112,96},{1... | collective-permute-start | bytes 3145736 | tf_op jit(solution)/shard_map/ppermute | solution.py:195
  54.1 19.0 %collective-permute-done.8.refs_1_ = bf16[16,2,128,128]{3,2,1,0:T(8,128)(2,1)} collective-permute-done((bf16[16,2,128,128]{3,2,1,0:T(8,128)(2,1)S(1)}, bf16[16,2,128,128]{3,2,1,0:T(8,128)(2,1)}, u32[]{:S(2)}, u32[]{:S(2)}) %collective-permute-start.8) | collective-permute-done | bytes 1048608 | tf_op jit(solution)/shard_map/ppermute | solution.py:192
  75.3 2.7 %collective-permute-start.11 = (bf16[8,2,128,128]{3,2,1,0:T(8,128)(2,1)S(1)}, bf16[8,2,128,128]{3,2,1,0:T(8,128)(2,1)}, u32[]{:S(2)}, u32[]{:S(2)}) collective-permute-start(bf16[8,2,128,128]{3,2,1,0:T(8,128)(2,1)S(1)} %slice.37), channel_id=1, source_target_pairs={{0,96},{16,112},{32,0},{48,16},{64,32},{80,48},{96,64},{112,80},{1... | collective-permute-start | bytes 1572872 | tf_op jit(solution)/shard_map/ppermute | solution.py:192
  78.1 3.3 %collective-permute-start.22 = (bf16[16,2,128,128]{3,2,1,0:T(8,128)(2,1)}, bf16[16,2,128,128]{3,2,1,0:T(8,128)(2,1)}, u32[]{:S(2)}, u32[]{:S(2)}) collective-permute-start(bf16[16,2,128,128]{3,2,1,0:T(8,128)(2,1)} %collective-permute-done.8.refs_1_), channel_id=1, source_target_pairs={{0,16},{16,0},{32,48},{48,32},{64,80},{80,64},{96,112},{112,96},{1... | collective-permute-start | bytes 3145736 | tf_op jit(solution)/shard_map/ppermute | solution.py:195
  81.4 4.9 %collective-permute-done.9.refs_3_ = bf16[8,2,128,128]{3,2,1,0:T(8,128)(2,1)S(1)} collective-permute-done((bf16[8,2,128,128]{3,2,1,0:T(8,128)(2,1)S(1)}, bf16[8,2,128,128]{3,2,1,0:T(8,128)(2,1)S(1)}, u32[]{:S(2)}, u32[]{:S(2)}) %collective-permute-start.9) | collective-permute-done | bytes 524320 | tf_op jit(solution)/shard_map/ppermute | solution.py:192
  86.3 3.5 %collective-permute-start.24 = (bf16[8,2,128,128]{3,2,1,0:T(8,128)(2,1)S(1)}, bf16[8,2,128,128]{3,2,1,0:T(8,128)(2,1)}, u32[]{:S(2)}, u32[]{:S(2)}) collective-permute-start(bf16[8,2,128,128]{3,2,1,0:T(8,128)(2,1)S(1)} %collective-permute-done.9.refs_3_), channel_id=1, source_target_pairs={{0,16},{16,0},{32,48},{48,32},{64,80},{80,64},{96,112},{112,96},{1... | collective-permute-start | bytes 1572872 | tf_op jit(solution)/shard_map/ppermute | solution.py:195
  92.2 8.5 %all-to-all-done.1.t_hbm = bf16[16,2,256,256]{3,2,1,0:T(8,128)(2,1)} async-done(((bf16[16,2,256,256]{3,2,1,0:T(8,128)(2,1)}), bf16[16,2,256,256]{3,2,1,0:T(8,128)(2,1)}, u32[]{:S(2)}, u32[]{:S(2)}) %all-to-all-start.1) | async-done | bytes 4194336 | tf_op jit(solution)/shard_map/all_to_all | solution.py:227
  100.7 14.2 %shard_map.128 = bf16[16,2,256,256]{3,2,1,0:T(8,128)(2,1)} custom-call(s32[64,4]{1,0:T(8,128)} %copy.18.screen, s32[32,48]{1,0:T(8,128)} %rows.1, s32[32]{0:T(128)} %count.1, s32[2]{0:T(128)} %pad_add_fusion.place, bf16[16,2,256,256]{3,2,1,0:T(8,128)(2,1)} %all-to-all-done.1.t_hbm, bf16[16,2,128,128]{3,2,1,0:T(8,128)(2,1)} %copy-done.2, ...), custom_call_target="tpu_custom_call" | custom-call | tf_op jit(solution)/shard_map/pallas_call | solution.py:238
  114.9 7.3 %all-to-all-start.2 = ((bf16[16,2,256,256]{3,2,1,0:T(8,128)(2,1)}), bf16[16,2,256,256]{3,2,1,0:T(8,128)(2,1)}, u32[]{:S(2)}, u32[]{:S(2)}) async-start(bf16[16,2,256,256]{3,2,1,0:T(8,128)(2,1)} %shard_map.128), calls=%async_computation.2 | async-start | bytes 8388608 | tf_op jit(solution)/shard_map/all_to_all | solution.py:258
  125.9 4.6 %collective-permute-start.16 = (bf16[16,2,128,128]{3,2,1,0:T(8,128)(2,1)S(1)}, bf16[16,2,128,128]{3,2,1,0:T(8,128)(2,1)}, u32[]{:S(2)}, u32[]{:S(2)}) collective-permute-start(bf16[16,2,128,128]{3,2,1,0:T(8,128)(2,1)S(1)} %bitcast.31), channel_id=1, source_target_pairs={{0,16},{16,0},{32,48},{48,32},{64,80},{80,64},{96,112},{112,96},{1... | collective-permute-start | bytes 3145736 | tf_op jit(solution)/shard_map/ppermute | solution.py:195
  130.5 14.7 %collective-permute-done.12.refs_1_ = bf16[16,2,128,128]{3,2,1,0:T(8,128)(2,1)S(1)} collective-permute-done((bf16[16,2,128,128]{3,2,1,0:T(8,128)(2,1)S(1)}, bf16[16,2,128,128]{3,2,1,0:T(8,128)(2,1)S(1)}, u32[]{:S(2)}, u32[]{:S(2)}) %collective-permute-start.12) | collective-permute-done | bytes 1048608 | tf_op jit(solution)/shard_map/ppermute | solution.py:192
  146.6 2.7 %collective-permute-start.15 = (bf16[8,2,128,128]{3,2,1,0:T(8,128)(2,1)S(1)}, bf16[8,2,128,128]{3,2,1,0:T(8,128)(2,1)}, u32[]{:S(2)}, u32[]{:S(2)}) collective-permute-start(bf16[8,2,128,128]{3,2,1,0:T(8,128)(2,1)S(1)} %slice.39), channel_id=1, source_target_pairs={{0,96},{16,112},{32,0},{48,16},{64,32},{80,48},{96,64},{112,80},{1... | collective-permute-start | bytes 1572872 | tf_op jit(solution)/shard_map/ppermute | solution.py:192
  149.3 5.6 %collective-permute-start.17 = (bf16[16,2,128,128]{3,2,1,0:T(8,128)(2,1)S(1)}, bf16[16,2,128,128]{3,2,1,0:T(8,128)(2,1)}, u32[]{:S(2)}, u32[]{:S(2)}) collective-permute-start(bf16[16,2,128,128]{3,2,1,0:T(8,128)(2,1)S(1)} %collective-permute-done.12.refs_1_), channel_id=1, source_target_pairs={{0,16},{16,0},{32,48},{48,32},{64,80},{80,64},{96,112},{112,96},{1... | collective-permute-start | bytes 3145736 | tf_op jit(solution)/shard_map/ppermute | solution.py:195
  155.7 5.6 %collective-permute-start.19 = (bf16[8,2,128,128]{3,2,1,0:T(8,128)(2,1)S(1)}, bf16[8,2,128,128]{3,2,1,0:T(8,128)(2,1)}, u32[]{:S(2)}, u32[]{:S(2)}) collective-permute-start(bf16[8,2,128,128]{3,2,1,0:T(8,128)(2,1)S(1)} %collective-permute-done.14.refs_3_), channel_id=1, source_target_pairs={{0,16},{16,0},{32,48},{48,32},{64,80},{80,64},{96,112},{112,96},{1... | collective-permute-start | bytes 1572872 | tf_op jit(solution)/shard_map/ppermute | solution.py:195
  164.3 17.3 %shard_map.127 = f32[2,32,128,256]{3,2,1,0:T(8,128)} custom-call(s32[32,8]{1,0:T(8,128)} %copy.17.screen, s32[256]{0:T(256)} %slots.1, s32[2]{0:T(128)} %pad_add_fusion.place, bf16[2,32,128,256]{3,2,1,0:T(8,128)(2,1)} %bitcast.26, bf16[2,32,128,256]{3,2,1,0:T(8,128)(2,1)} %bitcast.28, bf16[16,2,128,128]{3,2,1,0:T(8,128)(2,1)} %bitcast.32, ...), custom_call_target="tpu_custom_call" | custom-call | tf_op jit(solution)/shard_map/pallas_call | solution.py:261
  181.6 8.8 %shard_map.129 = bf16[2,4096,256]{2,1,0:T(8,128)(2,1)} custom-call(s32[8]{0:T(128)} %slab.1, s32[2]{0:T(128)} %pair.1, s32[2]{0:T(128)} %pad_add_fusion.place, f32[400]{0:T(512)} %occ_ref.1, f32[2,4096,256]{2,1,0:T(8,128)} %bitcast.24, bf16[16,2,256,256]{3,2,1,0:T(8,128)(2,1)} %all-to-all-done.2.cycle_ref, f32[1,4096]{1,0:T(1,128)} %bitcast.37, ...), custom_call_target="tpu_custom_call" | custom-call | tf_op jit(solution)/shard_map/pallas_call | solution.py:285
  (76 shorter events, 26.3 us)
Async XLA Ops:
  1.0 12.1 %collective-permute-start = (bf16[2,128,128]{2,1,0:T(8,128)(2,1)S(1)}, bf16[2,128,128]{2,1,0:T(8,128)(2,1)S(1)}, u32[]{:S(2)}, u32[]{:S(2)}) collective-permute-start(bf16[2,128,128]{2,1,0:T(8,128)(2,1)S(1)} %constant_dynamic-slice_fusion), channel_id=1, source_target_pairs={{0,1},{1,2},{2,3},{3,0},{4,5},{5,6},{6,7},{7,4},{8,9},{9,10},{10,1... | collective-permute-start | bytes 196616 | tf_op jit(solution)/shard_map/ppermute | solution.py:199
  3.5 11.1 %collective-permute-start.2 = (bf16[2,128,128]{2,1,0:T(8,128)(2,1)S(1)}, bf16[2,128,128]{2,1,0:T(8,128)(2,1)S(1)}, u32[]{:S(2)}, u32[]{:S(2)}) collective-permute-start(bf16[2,128,128]{2,1,0:T(8,128)(2,1)S(1)} %constant_dynamic-slice_fusion), channel_id=1, source_target_pairs={{0,3},{1,0},{2,1},{3,2},{4,7},{5,4},{6,5},{7,6},{8,11},{9,8},{10,9... | collective-permute-start | bytes 196616 | tf_op jit(solution)/shard_map/ppermute | solution.py:199
  7.8 36.4 %all-to-all-start = ((bf16[16,2,128,128]{3,2,1,0:T(8,128)(2,1)}), bf16[16,2,128,128]{3,2,1,0:T(8,128)(2,1)S(1)}, u32[]{:S(2)}, u32[]{:S(2)}) async-start(bf16[16,2,128,128]{3,2,1,0:T(8,128)(2,1)} %broadcast_in_dim.4), calls=%async_computation | async-start | bytes 2097152 | tf_op jit(solution)/shard_map/all_to_all | solution.py:222
  18.7 17.8 %collective-permute-start.4 = (bf16[4,2,128,128]{3,2,1,0:T(8,128)(2,1)S(1)}, bf16[4,2,128,128]{3,2,1,0:T(8,128)(2,1)S(1)}, u32[]{:S(2)}, u32[]{:S(2)}) collective-permute-start(bf16[4,2,128,128]{3,2,1,0:T(8,128)(2,1)S(1)} %get-tuple-element.14), channel_id=1, source_target_pairs={{0,4},{1,5},{2,6},{3,7},{4,8},{5,9},{6,10},{7,11},{8,12},{9,13},{1... | collective-permute-start | bytes 786440 | tf_op jit(solution)/shard_map/ppermute | solution.py:199
  29.1 7.5 %collective-permute-start.6 = (bf16[4,2,128,128]{3,2,1,0:T(8,128)(2,1)S(1)}, bf16[4,2,128,128]{3,2,1,0:T(8,128)(2,1)S(1)}, u32[]{:S(2)}, u32[]{:S(2)}) collective-permute-start(bf16[4,2,128,128]{3,2,1,0:T(8,128)(2,1)S(1)} %get-tuple-element.14), channel_id=1, source_target_pairs={{0,12},{1,13},{2,14},{3,15},{4,0},{5,1},{6,2},{7,3},{8,4},{9,5},{1... | collective-permute-start | bytes 786440 | tf_op jit(solution)/shard_map/ppermute | solution.py:199
  36.5 7.5 %collective-permute-start.5 = (bf16[2,2,128,128]{3,2,1,0:T(8,128)(2,1)S(1)}, bf16[2,2,128,128]{3,2,1,0:T(8,128)(2,1)S(1)}, u32[]{:S(2)}, u32[]{:S(2)}) collective-permute-start(bf16[2,2,128,128]{3,2,1,0:T(8,128)(2,1)S(1)} %slice.34), channel_id=1, source_target_pairs={{0,4},{1,5},{2,6},{3,7},{4,8},{5,9},{6,10},{7,11},{8,12},{9,13},{1... | collective-permute-start | bytes 393224 | tf_op jit(solution)/shard_map/ppermute | solution.py:199
  36.6 7.4 %collective-permute-start.7 = (bf16[2,2,128,128]{3,2,1,0:T(8,128)(2,1)S(1)}, bf16[2,2,128,128]{3,2,1,0:T(8,128)(2,1)S(1)}, u32[]{:S(2)}, u32[]{:S(2)}) collective-permute-start(bf16[2,2,128,128]{3,2,1,0:T(8,128)(2,1)S(1)} %slice.35), channel_id=1, source_target_pairs={{0,12},{1,13},{2,14},{3,15},{4,0},{5,1},{6,2},{7,3},{8,4},{9,5},{1... | collective-permute-start | bytes 393224 | tf_op jit(solution)/shard_map/ppermute | solution.py:199
  44.2 56.5 %all-to-all-start.1 = ((bf16[16,2,256,256]{3,2,1,0:T(8,128)(2,1)}), bf16[16,2,256,256]{3,2,1,0:T(8,128)(2,1)}, u32[]{:S(2)}, u32[]{:S(2)}) async-start(bf16[16,2,256,256]{3,2,1,0:T(8,128)(2,1)} %bitcast.27), calls=%async_computation.1 | async-start | bytes 8388608 | tf_op jit(solution)/shard_map/all_to_all | solution.py:227
  48.9 24.2 %collective-permute-start.8 = (bf16[16,2,128,128]{3,2,1,0:T(8,128)(2,1)S(1)}, bf16[16,2,128,128]{3,2,1,0:T(8,128)(2,1)}, u32[]{:S(2)}, u32[]{:S(2)}) collective-permute-start(bf16[16,2,128,128]{3,2,1,0:T(8,128)(2,1)S(1)} %all-to-all-done.refs_0_), channel_id=1, source_target_pairs={{0,32},{16,48},{32,64},{48,80},{64,96},{80,112},{96,0},{112,16},{1... | collective-permute-start | bytes 3145736 | tf_op jit(solution)/shard_map/ppermute | solution.py:192
  50.2 24.1 %collective-permute-start.10 = (bf16[16,2,128,128]{3,2,1,0:T(8,128)(2,1)S(1)}, bf16[16,2,128,128]{3,2,1,0:T(8,128)(2,1)}, u32[]{:S(2)}, u32[]{:S(2)}) collective-permute-start(bf16[16,2,128,128]{3,2,1,0:T(8,128)(2,1)S(1)} %all-to-all-done.refs_0_), channel_id=1, source_target_pairs={{0,96},{16,112},{32,0},{48,16},{64,32},{80,48},{96,64},{112,80},{1... | collective-permute-start | bytes 3145736 | tf_op jit(solution)/shard_map/ppermute | solution.py:192
  51.6 39.9 %collective-permute-start.21 = (bf16[16,2,128,128]{3,2,1,0:T(8,128)(2,1)S(1)}, bf16[16,2,128,128]{3,2,1,0:T(8,128)(2,1)}, u32[]{:S(2)}, u32[]{:S(2)}) collective-permute-start(bf16[16,2,128,128]{3,2,1,0:T(8,128)(2,1)S(1)} %all-to-all-done.refs_0_), channel_id=1, source_target_pairs={{0,16},{16,0},{32,48},{48,32},{64,80},{80,64},{96,112},{112,96},{1... | collective-permute-start | bytes 3145736 | tf_op jit(solution)/shard_map/ppermute | solution.py:195
  74.2 12.1 %collective-permute-start.9 = (bf16[8,2,128,128]{3,2,1,0:T(8,128)(2,1)S(1)}, bf16[8,2,128,128]{3,2,1,0:T(8,128)(2,1)S(1)}, u32[]{:S(2)}, u32[]{:S(2)}) collective-permute-start(bf16[8,2,128,128]{3,2,1,0:T(8,128)(2,1)S(1)} %slice.36), channel_id=1, source_target_pairs={{0,32},{16,48},{32,64},{48,80},{64,96},{80,112},{96,0},{112,16},{1... | collective-permute-start | bytes 1572872 | tf_op jit(solution)/shard_map/ppermute | solution.py:192
  75.3 14.4 %collective-permute-start.11 = (bf16[8,2,128,128]{3,2,1,0:T(8,128)(2,1)S(1)}, bf16[8,2,128,128]{3,2,1,0:T(8,128)(2,1)}, u32[]{:S(2)}, u32[]{:S(2)}) collective-permute-start(bf16[8,2,128,128]{3,2,1,0:T(8,128)(2,1)S(1)} %slice.37), channel_id=1, source_target_pairs={{0,96},{16,112},{32,0},{48,16},{64,32},{80,48},{96,64},{112,80},{1... | collective-permute-start | bytes 1572872 | tf_op jit(solution)/shard_map/ppermute | solution.py:192
  78.1 14.1 %collective-permute-start.22 = (bf16[16,2,128,128]{3,2,1,0:T(8,128)(2,1)}, bf16[16,2,128,128]{3,2,1,0:T(8,128)(2,1)}, u32[]{:S(2)}, u32[]{:S(2)}) collective-permute-start(bf16[16,2,128,128]{3,2,1,0:T(8,128)(2,1)} %collective-permute-done.8.refs_1_), channel_id=1, source_target_pairs={{0,16},{16,0},{32,48},{48,32},{64,80},{80,64},{96,112},{112,96},{1... | collective-permute-start | bytes 3145736 | tf_op jit(solution)/shard_map/ppermute | solution.py:195
  81.4 10.8 %collective-permute-start.23 = (bf16[16,2,128,128]{3,2,1,0:T(8,128)(2,1)}, bf16[16,2,128,128]{3,2,1,0:T(8,128)(2,1)}, u32[]{:S(2)}, u32[]{:S(2)}) collective-permute-start(bf16[16,2,128,128]{3,2,1,0:T(8,128)(2,1)} %collective-permute-done.10.refs_2_), channel_id=1, source_target_pairs={{0,16},{16,0},{32,48},{48,32},{64,80},{80,64},{96,112},{112,96},{1... | collective-permute-start | bytes 3145736 | tf_op jit(solution)/shard_map/ppermute | solution.py:195
  114.9 66.8 %all-to-all-start.2 = ((bf16[16,2,256,256]{3,2,1,0:T(8,128)(2,1)}), bf16[16,2,256,256]{3,2,1,0:T(8,128)(2,1)}, u32[]{:S(2)}, u32[]{:S(2)}) async-start(bf16[16,2,256,256]{3,2,1,0:T(8,128)(2,1)} %shard_map.128), calls=%async_computation.2 | async-start | bytes 8388608 | tf_op jit(solution)/shard_map/all_to_all | solution.py:258
  123.1 22.0 %collective-permute-start.12 = (bf16[16,2,128,128]{3,2,1,0:T(8,128)(2,1)S(1)}, bf16[16,2,128,128]{3,2,1,0:T(8,128)(2,1)S(1)}, u32[]{:S(2)}, u32[]{:S(2)}) collective-permute-start(bf16[16,2,128,128]{3,2,1,0:T(8,128)(2,1)S(1)} %bitcast.29), channel_id=1, source_target_pairs={{0,32},{16,48},{32,64},{48,80},{64,96},{80,112},{96,0},{112,16},{1... | collective-permute-start | bytes 3145736 | tf_op jit(solution)/shard_map/ppermute | solution.py:192
  124.4 21.1 %collective-permute-start.13 = (bf16[16,2,128,128]{3,2,1,0:T(8,128)(2,1)S(1)}, bf16[16,2,128,128]{3,2,1,0:T(8,128)(2,1)}, u32[]{:S(2)}, u32[]{:S(2)}) collective-permute-start(bf16[16,2,128,128]{3,2,1,0:T(8,128)(2,1)S(1)} %bitcast.30), channel_id=1, source_target_pairs={{0,96},{16,112},{32,0},{48,16},{64,32},{80,48},{96,64},{112,80},{1... | collective-permute-start | bytes 3145736 | tf_op jit(solution)/shard_map/ppermute | solution.py:192
  125.9 37.2 %collective-permute-start.16 = (bf16[16,2,128,128]{3,2,1,0:T(8,128)(2,1)S(1)}, bf16[16,2,128,128]{3,2,1,0:T(8,128)(2,1)}, u32[]{:S(2)}, u32[]{:S(2)}) collective-permute-start(bf16[16,2,128,128]{3,2,1,0:T(8,128)(2,1)S(1)} %bitcast.31), channel_id=1, source_target_pairs={{0,16},{16,0},{32,48},{48,32},{64,80},{80,64},{96,112},{112,96},{1... | collective-permute-start | bytes 3145736 | tf_op jit(solution)/shard_map/ppermute | solution.py:195
  145.2 10.4 %collective-permute-start.14 = (bf16[8,2,128,128]{3,2,1,0:T(8,128)(2,1)S(1)}, bf16[8,2,128,128]{3,2,1,0:T(8,128)(2,1)S(1)}, u32[]{:S(2)}, u32[]{:S(2)}) collective-permute-start(bf16[8,2,128,128]{3,2,1,0:T(8,128)(2,1)S(1)} %slice.38), channel_id=1, source_target_pairs={{0,32},{16,48},{32,64},{48,80},{64,96},{80,112},{96,0},{112,16},{1... | collective-permute-start | bytes 1572872 | tf_op jit(solution)/shard_map/ppermute | solution.py:192
  146.6 14.6 %collective-permute-start.15 = (bf16[8,2,128,128]{3,2,1,0:T(8,128)(2,1)S(1)}, bf16[8,2,128,128]{3,2,1,0:T(8,128)(2,1)}, u32[]{:S(2)}, u32[]{:S(2)}) collective-permute-start(bf16[8,2,128,128]{3,2,1,0:T(8,128)(2,1)S(1)} %slice.39), channel_id=1, source_target_pairs={{0,96},{16,112},{32,0},{48,16},{64,32},{80,48},{96,64},{112,80},{1... | collective-permute-start | bytes 1572872 | tf_op jit(solution)/shard_map/ppermute | solution.py:192
  149.3 15.0 %collective-permute-start.17 = (bf16[16,2,128,128]{3,2,1,0:T(8,128)(2,1)S(1)}, bf16[16,2,128,128]{3,2,1,0:T(8,128)(2,1)}, u32[]{:S(2)}, u32[]{:S(2)}) collective-permute-start(bf16[16,2,128,128]{3,2,1,0:T(8,128)(2,1)S(1)} %collective-permute-done.12.refs_1_), channel_id=1, source_target_pairs={{0,16},{16,0},{32,48},{48,32},{64,80},{80,64},{96,112},{112,96},{1... | collective-permute-start | bytes 3145736 | tf_op jit(solution)/shard_map/ppermute | solution.py:195
  154.9 9.4 %collective-permute-start.18 = (bf16[16,2,128,128]{3,2,1,0:T(8,128)(2,1)}, bf16[16,2,128,128]{3,2,1,0:T(8,128)(2,1)}, u32[]{:S(2)}, u32[]{:S(2)}) collective-permute-start(bf16[16,2,128,128]{3,2,1,0:T(8,128)(2,1)} %collective-permute-done.13.refs_2_), channel_id=1, source_target_pairs={{0,16},{16,0},{32,48},{48,32},{64,80},{80,64},{96,112},{112,96},{1... | collective-permute-start | bytes 3145736 | tf_op jit(solution)/shard_map/ppermute | solution.py:195
  155.7 7.4 %collective-permute-start.19 = (bf16[8,2,128,128]{3,2,1,0:T(8,128)(2,1)S(1)}, bf16[8,2,128,128]{3,2,1,0:T(8,128)(2,1)}, u32[]{:S(2)}, u32[]{:S(2)}) collective-permute-start(bf16[8,2,128,128]{3,2,1,0:T(8,128)(2,1)S(1)} %collective-permute-done.14.refs_3_), channel_id=1, source_target_pairs={{0,16},{16,0},{32,48},{48,32},{64,80},{80,64},{96,112},{112,96},{1... | collective-permute-start | bytes 1572872 | tf_op jit(solution)/shard_map/ppermute | solution.py:195
  (13 other events, 198.5 us)

commit v4 on v3

v4 whole, which is shorter than its diff:
```python
import functools

import jax
import jax.numpy as jnp
from jax import lax
from jax.experimental import pallas as pl
from jax.experimental.pallas import tpu as pltpu
from jax.sharding import PartitionSpec as P


F32 = jnp.float32
BF16 = jnp.bfloat16
ANY = pl.BlockSpec(memory_space=pl.ANY)


SCALARS = pl.BlockSpec(memory_space=pltpu.SMEM)
FULL_VMEM = pltpu.CompilerParams(vmem_limit_bytes=60 << 20)


def tile_copies(place, pieces, buf, sem):
    xs = buf.shape[1]
    core, x = place[0] & 1, place[0] // 2
    groups = [[], [], [], []]
    for side, at in ((pieces[:5], core), (pieces[5:], 1 - core)):
        near, behind, ahead, far_low, far_high = side
        half = far_low.shape[0]
        whole = slice(None)
        for src, group, shift, where in (
            (near, 0, 0, whole),
            (behind, 1, xs - 1, whole),
            (ahead, 2, 1, whole),
            (far_low, 3, 2, pl.ds(0, half)),
            (far_high, 3, 2, pl.ds(half, half)),
        ):
            dst = buf.at[where, (x + shift) & (xs - 1), at]
            count = sum(map(len, groups))
            groups[group].append(pltpu.make_async_copy(src, dst, sem.at[count]))
    return groups


def chunk_copies(src, dst, sem):
    chunk = dst.shape[0] // sem.shape[0]
    return [
        pltpu.make_async_copy(src.at[pl.ds(i * chunk, chunk)], dst.at[pl.ds(i * chunk, chunk)], sem.at[i])
        for i in range(sem.shape[0])
    ]


def cost(flops, bytes_accessed):
    return pl.CostEstimate(flops=flops, bytes_accessed=bytes_accessed, transcendentals=0)


def cycle_kernel(screen, rows, count, place, t_hbm, *refs, side):
    pieces, (out_hbm, t_ref, z_ref, o_ref, t_sem, z_sem, o_sem) = refs[:10], refs[10:]
    keep, tile = screen.shape[1], z_ref.shape[-1]
    parts, window, _, width = t_ref.shape
    tiles_wide = width // tile
    tile_count = screen.shape[0] // window
    xs = z_ref.shape[1]
    block = place[1] * (rows.shape[0] // parts) + side
    copies = chunk_copies(t_hbm, t_ref, t_sem) + sum(tile_copies(place, pieces, z_ref, z_sem), [])
    for copy in copies:
        copy.start()
    for part in range(parts):
        o_ref[part] = jnp.zeros(o_ref.shape[1:], BF16)
    for copy in copies:
        copy.wait()

    def one(entry):
        q = rows[block, entry]
        j, c_out = q // tile_count, q % tile_count
        left = []
        for m in range(keep):
            u = screen[q, m]
            c = u % tile_count
            lane = pl.multiple_of((c % tiles_wide) * tile, tile)
            left.append(t_ref[c // tiles_wide, u // tile_count, :, pl.ds(lane, tile)])
        right = z_ref[q // xs, q % xs].reshape(keep * tile, tile)
        part = jnp.dot(jnp.concatenate(left, axis=1), right, preferred_element_type=F32)
        lanes = pl.ds(pl.multiple_of((c_out % tiles_wide) * tile, tile), tile)
        o_ref[c_out // tiles_wide, j, :, lanes] = part.astype(BF16)

    used = count[block]
    unroll = 4

    @pl.loop(0, (used + unroll - 1) // unroll)
    def _(outer):
        for inner in range(unroll):
            one(jnp.minimum(outer * unroll + inner, used - 1))

    out = pltpu.make_async_copy(o_ref, out_hbm, o_sem)
    out.start()
    out.wait()


def ladder_kernel(screen, slots, place, t_hbm, near_hbm, *refs, side):
    pieces, (out_hbm, t_ref, near_ref, w_ref, out_ref, t_sem, near_sem, w_sem, o_sem) = (
        refs[:10],
        refs[10:],
    )
    keep = screen.shape[1]
    window, parts, _, _ = out_ref.shape
    sides = t_ref.shape[1] // parts
    share = w_ref.shape[3]
    per_dev = w_ref.shape[1] * w_ref.shape[2] * share
    copies = sum(tile_copies(place, pieces, w_ref, w_sem), []) + chunk_copies(t_hbm, t_ref, t_sem)
    copies.append(pltpu.make_async_copy(near_hbm.at[:, :, side], near_ref, near_sem))
    for copy in copies:
        copy.start()
    for copy in copies:
        copy.wait()

    def one(part):
        block = part * sides + side
        tiles = []
        for k in range(keep):
            slot = slots[block * keep + k]
            within = slot % per_dev
            tiles.append(
                w_ref[slot // per_dev, within // (2 * share), (within // share) % 2, within % share]
            )
        left = jnp.concatenate(tiles, axis=1)
        for j in range(window):
            right = jnp.concatenate([t_ref[j, screen[block, k]] for k in range(keep)], axis=0)
            out_ref[j, part] = near_ref[j, part].astype(F32) + jnp.dot(
                left, right, preferred_element_type=F32
            )

    unroll = 2
    chunks = o_sem.shape[0]
    size = parts // chunks

    def leave(chunk):
        where = pl.ds(chunk * size, size)
        return pltpu.make_async_copy(out_ref.at[:, where], out_hbm.at[:, where], o_sem.at[chunk])

    for chunk in range(chunks):

        @pl.loop(0, size // unroll)
        def _(outer):
            for inner in range(unroll):
                one(chunk * size + outer * unroll + inner)

        leave(chunk).start()
    for chunk in range(chunks):
        leave(chunk).wait()


def final_kernel(slab, pair, place, occ_ref, base_ref, cycle_ref, va_ref, vb_ref, *refs, side):
    out_ref = refs[-1]
    group, window, rows, cols = cycle_ref.shape
    sides = va_ref.shape[1] // (group * rows)
    for g in range(group):
        start = (g * sides + side) * rows
        energy_a = jnp.broadcast_to(va_ref[:, start : start + rows], (rows, rows)).T
        pairs = jnp.concatenate([energy_a] * (cols // rows), axis=1) + vb_ref[...]
        for j in range(window):
            below = (pairs - occ_ref[slab[place[0]]]) - occ_ref[pair[j]]
            value = base_ref[j, g] + cycle_ref[g, j].astype(F32)
            out_ref[j, g, 0] = (value / below).astype(BF16)


def body(
    amplitudes,
    coulomb,
    ladder_tiles,
    cycle_tiles,
    ladder_screen,
    tile_slot,
    cycle_screen,
    cycle_rows,
    cycle_count,
    slab_occ,
    window_occ,
    occ_energy,
    vir_energy,
):
    occ_count, vir_count = lax.axis_size("occ"), lax.axis_size("vir")
    _, window, width_all, block_cols = amplitudes.shape
    stored, tile, _ = ladder_tiles.shape
    tile_count = width_all // tile
    rows_here = width_all // vir_count
    share = stored // occ_count
    xs, zs = occ_count // 2, 4
    occ_at, vir_at = lax.axis_index("occ"), lax.axis_index("vir")
    place = jnp.stack([occ_at, vir_at]).astype(jnp.int32)
    t = amplitudes[0]
    near = coulomb[0]

    def occ_shift(value, by):
        return lax.ppermute(value, "occ", [(i, (i + 2 * by) % occ_count) for i in range(occ_count)])

    def core_swap(value):
        return lax.ppermute(value, "occ", [(i, i ^ 1) for i in range(occ_count)])

    def vir_shift(value, dy, dz):
        ys = vir_count // zs
        return lax.ppermute(
            value,
            "vir",
            [(y * zs + z, (y + dy) % ys * zs + (z + dz) % zs) for y in range(ys) for z in range(zs)],
        )

    def ring(value, shift, size):
        return jnp.stack([value] + [shift(value, d) for d in range(1, size)])

    def spread(piece):
        half = vir_count // 2
        behind, ahead = occ_shift(piece, 1), occ_shift(piece, -1)
        far_low, far_high = occ_shift(behind[:half], 1), occ_shift(ahead[half:], -1)
        mine = (piece, behind, ahead, far_low, far_high)
        return mine + tuple(core_swap(p) for p in mine)

    def my_share(tiles):
        return lax.dynamic_slice_in_dim(tiles, occ_at * share, share, 0)

    sent = jnp.broadcast_to(my_share(cycle_tiles)[None], (vir_count, share, tile, tile))
    cycle_piece = lax.all_to_all(sent, "vir", 0, 0, tiled=True)
    sides = rows_here // tile
    split = t.reshape(window, vir_count, sides, tile, block_cols)
    flats = [split[:, :, side].transpose(1, 0, 2, 3) for side in range(sides)]
    flats[0], ladder_share = lax.optimization_barrier((flats[0], my_share(ladder_tiles)))
    line = ring(ladder_share, lambda value, by: vir_shift(value, 0, by), zs)
    flats[0], cycle_piece, line = lax.optimization_barrier((flats[0], cycle_piece, line))
    plane = ring(line, lambda value, by: vir_shift(value, by, 0), vir_count // zs)
    moved = []
    for flat in flats:
        if moved:
            flat, moved[-1] = lax.optimization_barrier((flat, moved[-1]))
        moved.append(lax.all_to_all(flat, "vir", 0, 0, tiled=True))
    cycle_parts = spread(cycle_piece)

    plane, *_ = lax.optimization_barrier((plane, *cycle_parts))
    y, z = vir_at // zs, vir_at % zs
    plane = jnp.roll(jnp.flip(plane, (0, 1)), (y + 1, z + 1), (0, 1))
    ladder_parts = spread(plane.reshape(vir_count, share, tile, tile))

    tile_buf = pltpu.VMEM((vir_count, xs, 2, share, tile, tile), BF16)
    dma = pltpu.SemaphoreType.DMA
    half = (vir_count, window, tile, block_cols)
    size = vir_count * window * tile * block_cols
    tile_bytes = 2 * stored * vir_count * tile * tile

    def cycle_half(side):
        return pl.pallas_call(
            functools.partial(cycle_kernel, side=side),
            out_shape=pltpu.HBM(half, BF16),
            grid_spec=pltpu.PrefetchScalarGridSpec(
                num_scalar_prefetch=4,
                grid=(1,),
                in_specs=[ANY] * 11,
                out_specs=ANY,
                scratch_shapes=[
                    pltpu.VMEM(half, BF16),
                    tile_buf,
                    pltpu.VMEM(half, BF16),
                    dma((2,)),
                    dma((10,)),
                    dma(()),
                ],
            ),
            compiler_params=pltpu.CompilerParams(vmem_limit_bytes=16 << 20),
            cost_estimate=cost(8 * size * tile, 4 * size + tile_bytes),
        )(cycle_screen, cycle_rows, cycle_count, place, moved[side], *cycle_parts)

    blocked = (window, tile_count, tile, block_cols)
    base_shape = (window, vir_count, tile, block_cols)

    def base_half(side):
        return pl.pallas_call(
            functools.partial(ladder_kernel, side=side),
            out_shape=jax.ShapeDtypeStruct(base_shape, F32),
            grid_spec=pltpu.PrefetchScalarGridSpec(
                num_scalar_prefetch=3,
                grid=(1,),
                in_specs=[ANY] * 12,
                out_specs=ANY,
                scratch_shapes=[
                    pltpu.VMEM(blocked, BF16),
                    pltpu.VMEM(base_shape, BF16),
                    tile_buf,
                    pltpu.VMEM(base_shape, F32),
                    dma((2,)),
                    dma(()),
                    dma((10,)),
                    dma((4,)),
                ],
            ),
            compiler_params=FULL_VMEM,
            cost_estimate=cost(16 * size * tile, 10 * size + tile_bytes),
        )(
            ladder_screen,
            tile_slot,
            place,
            t.reshape(blocked),
            near.reshape(window, vir_count, sides, tile, block_cols),
            *ladder_parts,
        )

    energies = vir_energy.reshape(1, width_all)
    group = 4

    def final_half(side, base, cycle, out):
        old = [] if out is None else [out]
        return pl.pallas_call(
            functools.partial(final_kernel, side=side),
            out_shape=jax.ShapeDtypeStruct(split.shape, BF16),
            grid_spec=pltpu.PrefetchScalarGridSpec(
                num_scalar_prefetch=3,
                grid=(vir_count // group,),
                in_specs=[
                    SCALARS,
                    pl.BlockSpec((window, group, tile, block_cols), lambda g, *_: (0, g, 0, 0)),
                    pl.BlockSpec((group, window, tile, block_cols), lambda g, *_: (g, 0, 0, 0)),
                    pl.BlockSpec((1, group * rows_here), lambda g, *_: (0, g)),
                    pl.BlockSpec((1, block_cols), lambda g, slab, pair, place: (0, place[1])),
                ]
                + [ANY] * len(old),
                out_specs=pl.BlockSpec(
                    (window, group, 1, tile, block_cols), lambda g, *_: (0, g, side, 0, 0)
                ),
            ),
            compiler_params=pltpu.CompilerParams(vmem_limit_bytes=61 << 20),
            cost_estimate=cost(8 * size, 8 * size),
            input_output_aliases={8: 0} if old else {},
        )(slab_occ, window_occ, place, occ_energy, base, cycle, energies, energies, *old)

    back, bases, out = [], [], None
    for side in range(sides):
        part = cycle_half(side)
        if not back:
            part, _ = lax.optimization_barrier((part, moved[-1]))
        back.append(lax.all_to_all(part, "vir", 0, 0, tiled=True))
    for side in range(sides):
        bases.append(base_half(side))
    for side in range(sides):
        out = final_half(side, bases[side], back[side], out)
    return out.reshape(amplitudes.shape)


def solution(mesh):
    wide = P("occ", None, None, "vir")
    tiles = P("vir", None, None)
    return jax.shard_map(
        body,
        mesh=mesh,
        in_specs=(wide, wide, tiles, tiles) + (P(),) * 9,
        out_specs=wide,
        check_vma=False,
    )
```

time: 191 us -> 242 us (1.27)
  waiting for transfers between devices: 58.1 us -> 92.9 us
  Pallas kernels: 40.2 us -> 51.4 us
  local copies, waits for them, and re-layouts: 12.6 us -> 23.6 us
  starting transfers between devices: 77.5 us -> 67.3 us
  other arithmetic: 1.64 us -> 5.37 us
    ppermute x8 -> x6, waiting for transfers between devices: 8.52 us -> 42.6 us  [vir_shift(): lax.ppermute(value, 'vir', [(y * zs + z, (y + dy) % ys * zs + (z + dz) %...]
    ppermute x8, waiting for transfers between devices: 39.3 us -> 23.9 us  [occ_shift(): lax.ppermute(value, 'occ', [(i, (i + 2 * by) % occ_count) for i in range(...]
    all_to_all x2 -> x4, waiting for transfers between devices: 8.48 us -> 23.5 us  [the longest x2 23.5 us: body(): moved.append(lax.all_to_all(flat, 'vir', 0, 0, tiled=True))]
    ppermute x8 -> x6, starting transfers between devices: 22.2 us -> 7.41 us  [vir_shift(): lax.ppermute(value, 'vir', [(y * zs + z, (y + dy) % ys * zs + (z + dz) %...]
    all_to_all x2 -> x4, starting transfers between devices: 12 us -> 26.5 us  [the longest x2 18.1 us: body(): back.append(lax.all_to_all(part, 'vir', 0, 0, tiled=True))]
    pallas_call x3 -> x6, Pallas kernels: 40.2 us -> 51.4 us  [the longest x2 23.5 us: base_half(): pl.pallas_call(functools.partial(ladder_kernel, side=side), out_shape=jax...]
    ppermute x10, starting transfers between devices: 26.7 us -> 16.5 us  [core_swap(): return lax.ppermute(value, 'occ', [(i, i ^ 1) for i in range(occ_count)])]
    unnamed x18 -> x26, local copies, waits for them, and re-layouts: 2.47 us -> 10.8 us
  transfers between devices with their start and end apart: 29 -> 29, of which waited for: 9 -> 14; matrix products, arithmetic and copies ran while one was open for 7% -> 9% of each run, Pallas kernels for 9% -> 19%
where the time goes in v4:
time: 242 us; the launch traced here: 241 us
  waiting for transfers between devices  92.9 us (38%)
  starting transfers between devices  67.3 us (28%)
  Pallas kernels  51.4 us (21%)
  local copies, waits for them, and re-layouts  23.6 us (10%)
  other arithmetic  5.37 us (2%)
    ppermute x6, waiting for transfers between devices, vir_shift(): lax.ppermute(value, 'vir', [(y * zs + z, (y + dy) % ys * zs + (z + dz) %...  42.6 us
    ppermute x8, waiting for transfers between devices, occ_shift(): lax.ppermute(value, 'occ', [(i, (i + 2 * by) % occ_count) for i in range(...  23.9 us
    all_to_all x2, waiting for transfers between devices, body(): moved.append(lax.all_to_all(flat, 'vir', 0, 0, tiled=True))  23.5 us
    pallas_call x2, Pallas kernels, base_half(): pl.pallas_call(functools.partial(ladder_kernel, side=side), out_shape=jax...  23.5 us
    all_to_all x2, starting transfers between devices, body(): back.append(lax.all_to_all(part, 'vir', 0, 0, tiled=True))  18.1 us
    ppermute x10, starting transfers between devices, core_swap(): return lax.ppermute(value, 'occ', [(i, i ^ 1) for i in range(occ_count)])  16.5 us
    pallas_call x2, Pallas kernels, cycle_half(): pl.pallas_call(functools.partial(cycle_kernel, side=side), out_shape=pltp...  15.7 us
    pallas_call x2, Pallas kernels, final_half(): pl.pallas_call(functools.partial(final_kernel, side=side), out_shape=jax....  12.2 us
  transfers between devices with their start and end apart: 29, of which 14 were waited for; matrix products, arithmetic and copies ran while one was open for 9% of the time, Pallas kernels for 19%

profile of v4, /device:TPU:1, one launch (start us, length us, event | category | flops | bytes accessed | tf_op | source)
XLA Modules:
  0.0 240.9 jit_solution(17043926502339121306)
XLA Ops:
  2.3 8.6 %all-to-all-start = ((bf16[16,2,128,128]{3,2,1,0:T(8,128)(2,1)}), bf16[16,2,128,128]{3,2,1,0:T(8,128)(2,1)S(1)}, u32[]{:S(2)}, u32[]{:S(2)}) async-start(bf16[16,2,128,128]{3,2,1,0:T(8,128)(2,1)} %broadcast_in_dim.2), calls=%async_computation | async-start | bytes 2097152 | tf_op jit(solution)/shard_map/all_to_all | solution.py:218
  10.9 4.1 %fusion.2 = (bf16[2,16,1,128,256]{4,3,2,1,0:T(8,128)(2,1)}, bf16[2,16,1,128,256]{4,3,2,1,0:T(8,128)(2,1)S(1)}) fusion(bf16[2,16,2,128,256]{4,3,2,1,0:T(8,128)(2,1)} %bitcast.26), kind=kLoop, calls=%fused_computation.13 | loop fusion | bytes 8388608 | tf_op jit(solution)/shard_map/slice | solution.py:221
  21.1 5.8 %collective-permute-done.2 = bf16[2,128,128]{2,1,0:T(8,128)(2,1)S(1)} collective-permute-done((bf16[2,128,128]{2,1,0:T(8,128)(2,1)S(1)}, bf16[2,128,128]{2,1,0:T(8,128)(2,1)S(1)}, u32[]{:S(2)}, u32[]{:S(2)}) %collective-permute-start.2) | collective-permute-done | bytes 65568 | tf_op jit(solution)/shard_map/ppermute | solution.py:198
  26.8 2.9 %collective-permute-done.1 = bf16[2,128,128]{2,1,0:T(8,128)(2,1)S(1)} collective-permute-done((bf16[2,128,128]{2,1,0:T(8,128)(2,1)S(1)}, bf16[2,128,128]{2,1,0:T(8,128)(2,1)S(1)}, u32[]{:S(2)}, u32[]{:S(2)}) %collective-permute-start.1) | collective-permute-done | bytes 65568 | tf_op jit(solution)/shard_map/ppermute | solution.py:198
  30.0 4.4 %all-to-all-start.1 = ((bf16[16,2,128,256]{3,2,1,0:T(8,128)(2,1)}), bf16[16,2,128,256]{3,2,1,0:T(8,128)(2,1)S(1)}, u32[]{:S(2)}, u32[]{:S(2)}) async-start(bf16[16,2,128,256]{3,2,1,0:T(8,128)(2,1)} %bitcast.32), calls=%async_computation.1 | async-start | bytes 4194304 | tf_op jit(solution)/shard_map/all_to_all | solution.py:230
  37.0 3.2 %copy.29 = bf16[2,16,1,128,256]{4,3,0,1,2:T(8,128)(2,1)} copy(bf16[2,16,1,128,256]{4,3,2,1,0:T(8,128)(2,1)} %get-tuple-element.23) | data formatting | bytes 4194304
  40.2 23.5 %all-to-all-done.1.t_hbm = bf16[16,2,128,256]{3,2,1,0:T(8,128)(2,1)S(1)} async-done(((bf16[16,2,128,256]{3,2,1,0:T(8,128)(2,1)}), bf16[16,2,128,256]{3,2,1,0:T(8,128)(2,1)S(1)}, u32[]{:S(2)}, u32[]{:S(2)}) %all-to-all-start.1) | async-done | bytes 2097184 | tf_op jit(solution)/shard_map/all_to_all | solution.py:230
  65.0 4.0 %all-to-all-start.2 = ((bf16[16,2,128,256]{3,2,1,0:T(8,128)(2,1)}), bf16[16,2,128,256]{3,2,1,0:T(8,128)(2,1)S(1)}, u32[]{:S(2)}, u32[]{:S(2)}) async-start(bf16[16,2,128,256]{3,2,1,0:T(8,128)(2,1)} %bitcast.31), calls=%async_computation.2 | async-start | bytes 4194304 | tf_op jit(solution)/shard_map/all_to_all | solution.py:230
  76.8 9.5 %collective-permute-done.9.refs_4_ = bf16[8,2,128,128]{3,2,1,0:T(8,128)(2,1)} collective-permute-done((bf16[8,2,128,128]{3,2,1,0:T(8,128)(2,1)S(1)}, bf16[8,2,128,128]{3,2,1,0:T(8,128)(2,1)}, u32[]{:S(2)}, u32[]{:S(2)}) %collective-permute-start.9) | collective-permute-done | bytes 524320 | tf_op jit(solution)/shard_map/ppermute | solution.py:191
  87.2 3.9 %collective-permute-done.8.refs_3_ = bf16[8,2,128,128]{3,2,1,0:T(8,128)(2,1)} collective-permute-done((bf16[8,2,128,128]{3,2,1,0:T(8,128)(2,1)S(1)}, bf16[8,2,128,128]{3,2,1,0:T(8,128)(2,1)}, u32[]{:S(2)}, u32[]{:S(2)}) %collective-permute-start.8) | collective-permute-done | bytes 524320 | tf_op jit(solution)/shard_map/ppermute | solution.py:191
  95.6 8.7 %shard_map.130 = bf16[16,2,128,256]{3,2,1,0:T(8,128)(2,1)} custom-call(s32[64,4]{1,0:T(8,128)S(1)} %copy.22.screen, s32[32,48]{1,0:T(8,128)S(1)} %copy-done.4, s32[32]{0:T(128)S(1)} %copy-done.6, s32[2]{0:T(128)S(1)} %pad_add_fusion.place, bf16[16,2,128,256]{3,2,1,0:T(8,128)(2,1)S(1)} %copy-done.3, bf16[16,2,128,128]{3,2,1,0:T(8,128)(2,1)S(1)} %all-to-all-done.refs_0_, ...), custom_call_target="tpu_custom_call" | custom-call | flops 1073741824 | bytes 12582912 | tf_op jit(solution)/shard_map/pallas_call | solution.py:245
  104.4 9.6 %all-to-all-start.4 = ((bf16[16,2,128,256]{3,2,1,0:T(8,128)(2,1)}), bf16[16,2,128,256]{3,2,1,0:T(8,128)(2,1)}, u32[]{:S(2)}, u32[]{:S(2)}) async-start(bf16[16,2,128,256]{3,2,1,0:T(8,128)(2,1)} %shard_map.130), calls=%async_computation.4 | async-start | bytes 4194304 | tf_op jit(solution)/shard_map/all_to_all | solution.py:333
  117.7 26.5 %collective-permute-done.5 = bf16[4,2,128,128]{3,2,1,0:T(8,128)(2,1)} collective-permute-done((bf16[4,2,128,128]{3,2,1,0:T(8,128)(2,1)S(1)}, bf16[4,2,128,128]{3,2,1,0:T(8,128)(2,1)}, u32[]{:S(2)}, u32[]{:S(2)}) %collective-permute-start.5) | collective-permute-done | bytes 262176 | tf_op jit(solution)/shard_map/ppermute | solution.py:198
  146.4 4.9 %collective-permute-done.3 = bf16[4,2,128,128]{3,2,1,0:T(8,128)(2,1)} collective-permute-done((bf16[4,2,128,128]{3,2,1,0:T(8,128)(2,1)S(1)}, bf16[4,2,128,128]{3,2,1,0:T(8,128)(2,1)}, u32[]{:S(2)}, u32[]{:S(2)}) %collective-permute-start.3) | collective-permute-done | bytes 262176 | tf_op jit(solution)/shard_map/ppermute | solution.py:198
  160.4 7.0 %shard_map.128 = bf16[16,2,128,256]{3,2,1,0:T(8,128)(2,1)} custom-call(s32[64,4]{1,0:T(8,128)S(1)} %copy.22.screen, s32[32,48]{1,0:T(8,128)S(1)} %copy-done.4, s32[32]{0:T(128)S(1)} %copy-done.6, s32[2]{0:T(128)S(1)} %pad_add_fusion.place, bf16[16,2,128,256]{3,2,1,0:T(8,128)(2,1)S(1)} %all-to-all-done.2.t_hbm, ...), custom_call_target="tpu_custom_call" | custom-call | flops 1073741824 | bytes 12582912 | tf_op jit(solution)/shard_map/pallas_call | solution.py:245
  167.4 8.5 %all-to-all-start.3 = ((bf16[16,2,128,256]{3,2,1,0:T(8,128)(2,1)}), bf16[16,2,128,256]{3,2,1,0:T(8,128)(2,1)S(1)}, u32[]{:S(2)}, u32[]{:S(2)}) async-start(bf16[16,2,128,256]{3,2,1,0:T(8,128)(2,1)} %shard_map.128), calls=%async_computation.3 | async-start | bytes 4194304 | tf_op jit(solution)/shard_map/all_to_all | solution.py:333
  178.3 4.1 %collective-permute-done.16.refs_2_ = bf16[16,2,128,128]{3,2,1,0:T(8,128)(2,1)} collective-permute-done((bf16[16,2,128,128]{3,2,1,0:T(8,128)(2,1)}, bf16[16,2,128,128]{3,2,1,0:T(8,128)(2,1)}, u32[]{:S(2)}, u32[]{:S(2)}) %collective-permute-start.16) | collective-permute-done | bytes 1048608 | tf_op jit(solution)/shard_map/ppermute | solution.py:191
  189.2 5.7 %collective-permute-done.18.refs_4_ = bf16[8,2,128,128]{3,2,1,0:T(8,128)(2,1)S(1)} collective-permute-done((bf16[8,2,128,128]{3,2,1,0:T(8,128)(2,1)S(1)}, bf16[8,2,128,128]{3,2,1,0:T(8,128)(2,1)S(1)}, u32[]{:S(2)}, u32[]{:S(2)}) %collective-permute-start.18) | collective-permute-done | bytes 524320 | tf_op jit(solution)/shard_map/ppermute | solution.py:191
  194.8 3.1 %collective-permute-start.23 = (bf16[8,2,128,128]{3,2,1,0:T(8,128)(2,1)S(1)}, bf16[8,2,128,128]{3,2,1,0:T(8,128)(2,1)}, u32[]{:S(2)}, u32[]{:S(2)}) collective-permute-start(bf16[8,2,128,128]{3,2,1,0:T(8,128)(2,1)S(1)} %collective-permute-done.18.refs_4_), channel_id=1, source_target_pairs={{0,16},{16,0},{32,48},{48,32},{64,80},{80,64},{96,112},{112,96},{1... | collective-permute-start | bytes 1572872 | tf_op jit(solution)/shard_map/ppermute | solution.py:194
  198.7 3.2 %collective-permute-start.22 = (bf16[8,2,128,128]{3,2,1,0:T(8,128)(2,1)}, bf16[8,2,128,128]{3,2,1,0:T(8,128)(2,1)}, u32[]{:S(2)}, u32[]{:S(2)}) collective-permute-start(bf16[8,2,128,128]{3,2,1,0:T(8,128)(2,1)} %collective-permute-done.17.refs_3_), channel_id=1, source_target_pairs={{0,16},{16,0},{32,48},{48,32},{64,80},{80,64},{96,112},{112,96},{1... | collective-permute-start | bytes 1572872 | tf_op jit(solution)/shard_map/ppermute | solution.py:194
  203.8 11.8 %shard_map.129.base_ref = f32[2,16,128,256]{3,2,1,0:T(8,128)} custom-call(s32[32,8]{1,0:T(8,128)} %copy.20.screen, s32[256]{0:T(256)} %slots.3, s32[2]{0:T(128)} %copy-done.5, bf16[2,32,128,256]{3,2,1,0:T(8,128)(2,1)} %bitcast.27, bf16[2,16,2,128,256]{4,3,2,1,0:T(8,128)(2,1)} %bitcast.29, bf16[16,2,128,128]{3,2,1,0:T(8,128)(2,1)} %bitcast.15.refs_0_, ...), custom_call_target="tpu_custom_call" | custom-call | flops 2147483648 | bytes 18874368 | tf_op jit(solution)/shard_map/pallas_call | solution.py:270
  215.6 11.7 %shard_map.127.base_ref = f32[2,16,128,256]{3,2,1,0:T(8,128)} custom-call(s32[32,8]{1,0:T(8,128)} %copy.20.screen, s32[256]{0:T(256)} %slots.3, s32[2]{0:T(128)} %copy-done.5, bf16[2,32,128,256]{3,2,1,0:T(8,128)(2,1)} %bitcast.28, bf16[2,16,2,128,256]{4,3,2,1,0:T(8,128)(2,1)} %bitcast.30, bf16[16,2,128,128]{3,2,1,0:T(8,128)(2,1)} %bitcast.15.refs_0_, ...), custom_call_target="tpu_custom_call" | custom-call | flops 2147483648 | bytes 18874368 | tf_op jit(solution)/shard_map/pallas_call | solution.py:270
  227.3 6.1 %shard_map.131.refs_0_ = bf16[2,16,2,128,256]{4,3,2,1,0:T(8,128)(2,1)} custom-call(s32[8]{0:T(128)} %slab.3, s32[2]{0:T(128)} %pair.3, s32[2]{0:T(128)} %copy-done.5, f32[400]{0:T(512)} %occ_ref.3, f32[2,16,128,256]{3,2,1,0:T(8,128)} %shard_map.129.base_ref, bf16[16,2,128,256]{3,2,1,0:T(8,128)(2,1)} %all-to-all-done.4.cycle_ref, f32[1,4096]{1,0:T(1,128)} %bitcast.34, ...), custom_call_target="tpu_custom_call" | custom-call | flops 8388608 | bytes 8388608 | tf_op jit(solution)/shard_map/pallas_call | solution.py:305
  234.8 6.1 %shard_map.132 = bf16[2,16,2,128,256]{4,3,2,1,0:T(8,128)(2,1)} custom-call(s32[8]{0:T(128)} %slab.3, s32[2]{0:T(128)} %pair.3, s32[2]{0:T(128)} %copy-done.5, f32[400]{0:T(512)} %occ_ref.3, f32[2,16,128,256]{3,2,1,0:T(8,128)} %shard_map.127.base_ref, bf16[16,2,128,256]{3,2,1,0:T(8,128)(2,1)} %copy-done.7, ...), custom_call_target="tpu_custom_call", output_to_operand_aliasing={{}: (8, {})} | custom-call | flops 8388608 | bytes 8388608 | tf_op jit(solution)/shard_map/pallas_call | solution.py:305
  (80 shorter events, 53.7 us)
Async XLA Ops:
  2.3 27.7 %all-to-all-start = ((bf16[16,2,128,128]{3,2,1,0:T(8,128)(2,1)}), bf16[16,2,128,128]{3,2,1,0:T(8,128)(2,1)S(1)}, u32[]{:S(2)}, u32[]{:S(2)}) async-start(bf16[16,2,128,128]{3,2,1,0:T(8,128)(2,1)} %broadcast_in_dim.2), calls=%async_computation | async-start | bytes 2097152 | tf_op jit(solution)/shard_map/all_to_all | solution.py:218
  19.9 9.8 %collective-permute-start.1 = (bf16[2,128,128]{2,1,0:T(8,128)(2,1)S(1)}, bf16[2,128,128]{2,1,0:T(8,128)(2,1)S(1)}, u32[]{:S(2)}, u32[]{:S(2)}) collective-permute-start(bf16[2,128,128]{2,1,0:T(8,128)(2,1)S(1)} %constant_dynamic-slice_fusion.1), channel_id=1, source_target_pairs={{0,2},{1,3},{2,0},{3,1},{4,6},{5,7},{6,4},{7,5},{8,10},{9,11},{10,... | collective-permute-start | bytes 196616 | tf_op jit(solution)/shard_map/ppermute | solution.py:198
  20.5 9.5 %collective-permute-start = (bf16[2,128,128]{2,1,0:T(8,128)(2,1)S(1)}, bf16[2,128,128]{2,1,0:T(8,128)(2,1)S(1)}, u32[]{:S(2)}, u32[]{:S(2)}) collective-permute-start(bf16[2,128,128]{2,1,0:T(8,128)(2,1)S(1)} %constant_dynamic-slice_fusion.1), channel_id=1, source_target_pairs={{0,1},{1,2},{2,3},{3,0},{4,5},{5,6},{6,7},{7,4},{8,9},{9,10},{10,1... | collective-permute-start | bytes 196616 | tf_op jit(solution)/shard_map/ppermute | solution.py:198
  30.0 33.6 %all-to-all-start.1 = ((bf16[16,2,128,256]{3,2,1,0:T(8,128)(2,1)}), bf16[16,2,128,256]{3,2,1,0:T(8,128)(2,1)S(1)}, u32[]{:S(2)}, u32[]{:S(2)}) async-start(bf16[16,2,128,256]{3,2,1,0:T(8,128)(2,1)} %bitcast.32), calls=%async_computation.1 | async-start | bytes 4194304 | tf_op jit(solution)/shard_map/all_to_all | solution.py:230
  34.5 37.0 %collective-permute-start.7 = (bf16[16,2,128,128]{3,2,1,0:T(8,128)(2,1)S(1)}, bf16[16,2,128,128]{3,2,1,0:T(8,128)(2,1)}, u32[]{:S(2)}, u32[]{:S(2)}) collective-permute-start(bf16[16,2,128,128]{3,2,1,0:T(8,128)(2,1)S(1)} %all-to-all-done.refs_0_), channel_id=1, source_target_pairs={{0,96},{16,112},{32,0},{48,16},{64,32},{80,48},{96,64},{112,80},{1... | collective-permute-start | bytes 3145736 | tf_op jit(solution)/shard_map/ppermute | solution.py:191
  37.0 38.4 %collective-permute-start.6 = (bf16[16,2,128,128]{3,2,1,0:T(8,128)(2,1)S(1)}, bf16[16,2,128,128]{3,2,1,0:T(8,128)(2,1)}, u32[]{:S(2)}, u32[]{:S(2)}) collective-permute-start(bf16[16,2,128,128]{3,2,1,0:T(8,128)(2,1)S(1)} %all-to-all-done.refs_0_), channel_id=1, source_target_pairs={{0,32},{16,48},{32,64},{48,80},{64,96},{80,112},{96,0},{112,16},{1... | collective-permute-start | bytes 3145736 | tf_op jit(solution)/shard_map/ppermute | solution.py:191
  65.0 39.4 %all-to-all-start.2 = ((bf16[16,2,128,256]{3,2,1,0:T(8,128)(2,1)}), bf16[16,2,128,256]{3,2,1,0:T(8,128)(2,1)S(1)}, u32[]{:S(2)}, u32[]{:S(2)}) async-start(bf16[16,2,128,256]{3,2,1,0:T(8,128)(2,1)} %bitcast.31), calls=%async_computation.2 | async-start | bytes 4194304 | tf_op jit(solution)/shard_map/all_to_all | solution.py:230
  69.0 23.3 %collective-permute-start.10 = (bf16[16,2,128,128]{3,2,1,0:T(8,128)(2,1)S(1)}, bf16[16,2,128,128]{3,2,1,0:T(8,128)(2,1)}, u32[]{:S(2)}, u32[]{:S(2)}) collective-permute-start(bf16[16,2,128,128]{3,2,1,0:T(8,128)(2,1)S(1)} %all-to-all-done.refs_0_), channel_id=1, source_target_pairs={{0,16},{16,0},{32,48},{48,32},{64,80},{80,64},{96,112},{112,96},{1... | collective-permute-start | bytes 3145736 | tf_op jit(solution)/shard_map/ppermute | solution.py:194
  72.5 13.8 %collective-permute-start.9 = (bf16[8,2,128,128]{3,2,1,0:T(8,128)(2,1)S(1)}, bf16[8,2,128,128]{3,2,1,0:T(8,128)(2,1)}, u32[]{:S(2)}, u32[]{:S(2)}) collective-permute-start(bf16[8,2,128,128]{3,2,1,0:T(8,128)(2,1)S(1)} %slice.26), channel_id=1, source_target_pairs={{0,96},{16,112},{32,0},{48,16},{64,32},{80,48},{96,64},{112,80},{1... | collective-permute-start | bytes 1572872 | tf_op jit(solution)/shard_map/ppermute | solution.py:191
  75.0 17.3 %collective-permute-start.12 = (bf16[16,2,128,128]{3,2,1,0:T(8,128)(2,1)}, bf16[16,2,128,128]{3,2,1,0:T(8,128)(2,1)}, u32[]{:S(2)}, u32[]{:S(2)}) collective-permute-start(bf16[16,2,128,128]{3,2,1,0:T(8,128)(2,1)} %collective-permute-done.7.refs_2_), channel_id=1, source_target_pairs={{0,16},{16,0},{32,48},{48,32},{64,80},{80,64},{96,112},{112,96},{1... | collective-permute-start | bytes 3145736 | tf_op jit(solution)/shard_map/ppermute | solution.py:194
  76.4 14.7 %collective-permute-start.8 = (bf16[8,2,128,128]{3,2,1,0:T(8,128)(2,1)S(1)}, bf16[8,2,128,128]{3,2,1,0:T(8,128)(2,1)}, u32[]{:S(2)}, u32[]{:S(2)}) collective-permute-start(bf16[8,2,128,128]{3,2,1,0:T(8,128)(2,1)S(1)} %slice.25), channel_id=1, source_target_pairs={{0,32},{16,48},{32,64},{48,80},{64,96},{80,112},{96,0},{112,16},{1... | collective-permute-start | bytes 1572872 | tf_op jit(solution)/shard_map/ppermute | solution.py:191
  76.5 17.5 %collective-permute-start.11 = (bf16[16,2,128,128]{3,2,1,0:T(8,128)(2,1)}, bf16[16,2,128,128]{3,2,1,0:T(8,128)(2,1)}, u32[]{:S(2)}, u32[]{:S(2)}) collective-permute-start(bf16[16,2,128,128]{3,2,1,0:T(8,128)(2,1)} %collective-permute-done.6.refs_1_), channel_id=1, source_target_pairs={{0,16},{16,0},{32,48},{48,32},{64,80},{80,64},{96,112},{112,96},{1... | collective-permute-start | bytes 3145736 | tf_op jit(solution)/shard_map/ppermute | solution.py:194
  104.4 63.0 %all-to-all-start.4 = ((bf16[16,2,128,256]{3,2,1,0:T(8,128)(2,1)}), bf16[16,2,128,256]{3,2,1,0:T(8,128)(2,1)}, u32[]{:S(2)}, u32[]{:S(2)}) async-start(bf16[16,2,128,256]{3,2,1,0:T(8,128)(2,1)} %shard_map.130), calls=%async_computation.4 | async-start | bytes 4194304 | tf_op jit(solution)/shard_map/all_to_all | solution.py:333
  114.0 30.2 %collective-permute-start.5 = (bf16[4,2,128,128]{3,2,1,0:T(8,128)(2,1)S(1)}, bf16[4,2,128,128]{3,2,1,0:T(8,128)(2,1)}, u32[]{:S(2)}, u32[]{:S(2)}) collective-permute-start(bf16[4,2,128,128]{3,2,1,0:T(8,128)(2,1)S(1)} %pad_maximum_fusion.1), channel_id=1, source_target_pairs={{0,12},{1,13},{2,14},{3,15},{4,0},{5,1},{6,2},{7,3},{8,4},{9,5},{1... | collective-permute-start | bytes 786440 | tf_op jit(solution)/shard_map/ppermute | solution.py:198
  116.5 29.9 %collective-permute-start.4 = (bf16[4,2,128,128]{3,2,1,0:T(8,128)(2,1)S(1)}, bf16[4,2,128,128]{3,2,1,0:T(8,128)(2,1)}, u32[]{:S(2)}, u32[]{:S(2)}) collective-permute-start(bf16[4,2,128,128]{3,2,1,0:T(8,128)(2,1)S(1)} %pad_maximum_fusion.1), channel_id=1, source_target_pairs={{0,8},{1,9},{2,10},{3,11},{4,12},{5,13},{6,14},{7,15},{8,0},{9,1},... | collective-permute-start | bytes 786440 | tf_op jit(solution)/shard_map/ppermute | solution.py:198
  117.1 34.2 %collective-permute-start.3 = (bf16[4,2,128,128]{3,2,1,0:T(8,128)(2,1)S(1)}, bf16[4,2,128,128]{3,2,1,0:T(8,128)(2,1)}, u32[]{:S(2)}, u32[]{:S(2)}) collective-permute-start(bf16[4,2,128,128]{3,2,1,0:T(8,128)(2,1)S(1)} %pad_maximum_fusion.1), channel_id=1, source_target_pairs={{0,4},{1,5},{2,6},{3,7},{4,8},{5,9},{6,10},{7,11},{8,12},{9,13},{1... | collective-permute-start | bytes 786440 | tf_op jit(solution)/shard_map/ppermute | solution.py:198
  158.9 23.5 %collective-permute-start.16 = (bf16[16,2,128,128]{3,2,1,0:T(8,128)(2,1)}, bf16[16,2,128,128]{3,2,1,0:T(8,128)(2,1)}, u32[]{:S(2)}, u32[]{:S(2)}) collective-permute-start(bf16[16,2,128,128]{3,2,1,0:T(8,128)(2,1)} %bitcast.15.refs_0_), channel_id=1, source_target_pairs={{0,96},{16,112},{32,0},{48,16},{64,32},{80,48},{96,64},{112,80},{1... | collective-permute-start | bytes 3145736 | tf_op jit(solution)/shard_map/ppermute | solution.py:191
  158.9 26.2 %collective-permute-start.15 = (bf16[16,2,128,128]{3,2,1,0:T(8,128)(2,1)}, bf16[16,2,128,128]{3,2,1,0:T(8,128)(2,1)}, u32[]{:S(2)}, u32[]{:S(2)}) collective-permute-start(bf16[16,2,128,128]{3,2,1,0:T(8,128)(2,1)} %bitcast.15.refs_0_), channel_id=1, source_target_pairs={{0,32},{16,48},{32,64},{48,80},{64,96},{80,112},{96,0},{112,16},{1... | collective-permute-start | bytes 3145736 | tf_op jit(solution)/shard_map/ppermute | solution.py:191
  167.4 65.9 %all-to-all-start.3 = ((bf16[16,2,128,256]{3,2,1,0:T(8,128)(2,1)}), bf16[16,2,128,256]{3,2,1,0:T(8,128)(2,1)S(1)}, u32[]{:S(2)}, u32[]{:S(2)}) async-start(bf16[16,2,128,256]{3,2,1,0:T(8,128)(2,1)} %shard_map.128), calls=%async_computation.3 | async-start | bytes 4194304 | tf_op jit(solution)/shard_map/all_to_all | solution.py:333
  176.0 26.6 %collective-permute-start.19 = (bf16[16,2,128,128]{3,2,1,0:T(8,128)(2,1)}, bf16[16,2,128,128]{3,2,1,0:T(8,128)(2,1)}, u32[]{:S(2)}, u32[]{:S(2)}) collective-permute-start(bf16[16,2,128,128]{3,2,1,0:T(8,128)(2,1)} %bitcast.15.refs_0_), channel_id=1, source_target_pairs={{0,16},{16,0},{32,48},{48,32},{64,80},{80,64},{96,112},{112,96},{1... | collective-permute-start | bytes 3145736 | tf_op jit(solution)/shard_map/ppermute | solution.py:194
  183.5 11.3 %collective-permute-start.18 = (bf16[8,2,128,128]{3,2,1,0:T(8,128)(2,1)S(1)}, bf16[8,2,128,128]{3,2,1,0:T(8,128)(2,1)S(1)}, u32[]{:S(2)}, u32[]{:S(2)}) collective-permute-start(bf16[8,2,128,128]{3,2,1,0:T(8,128)(2,1)S(1)} %slice.28), channel_id=1, source_target_pairs={{0,96},{16,112},{32,0},{48,16},{64,32},{80,48},{96,64},{112,80},{1... | collective-permute-start | bytes 1572872 | tf_op jit(solution)/shard_map/ppermute | solution.py:191
  186.2 12.5 %collective-permute-start.17 = (bf16[8,2,128,128]{3,2,1,0:T(8,128)(2,1)S(1)}, bf16[8,2,128,128]{3,2,1,0:T(8,128)(2,1)}, u32[]{:S(2)}, u32[]{:S(2)}) collective-permute-start(bf16[8,2,128,128]{3,2,1,0:T(8,128)(2,1)S(1)} %slice.27), channel_id=1, source_target_pairs={{0,32},{16,48},{32,64},{48,80},{64,96},{80,112},{96,0},{112,16},{1... | collective-permute-start | bytes 1572872 | tf_op jit(solution)/shard_map/ppermute | solution.py:191
  186.3 17.5 %collective-permute-start.21 = (bf16[16,2,128,128]{3,2,1,0:T(8,128)(2,1)}, bf16[16,2,128,128]{3,2,1,0:T(8,128)(2,1)}, u32[]{:S(2)}, u32[]{:S(2)}) collective-permute-start(bf16[16,2,128,128]{3,2,1,0:T(8,128)(2,1)} %collective-permute-done.16.refs_2_), channel_id=1, source_target_pairs={{0,16},{16,0},{32,48},{48,32},{64,80},{80,64},{96,112},{112,96},{1... | collective-permute-start | bytes 3145736 | tf_op jit(solution)/shard_map/ppermute | solution.py:194
  189.1 14.6 %collective-permute-start.20 = (bf16[16,2,128,128]{3,2,1,0:T(8,128)(2,1)}, bf16[16,2,128,128]{3,2,1,0:T(8,128)(2,1)}, u32[]{:S(2)}, u32[]{:S(2)}) collective-permute-start(bf16[16,2,128,128]{3,2,1,0:T(8,128)(2,1)} %collective-permute-done.15.refs_1_), channel_id=1, source_target_pairs={{0,16},{16,0},{32,48},{48,32},{64,80},{80,64},{96,112},{112,96},{1... | collective-permute-start | bytes 3145736 | tf_op jit(solution)/shard_map/ppermute | solution.py:194
  (16 other events, 219.0 us)

commit v5 on v3

v5 whole, which is shorter than its diff:
```python
import jax
import jax.numpy as jnp
from jax import lax
from jax.experimental import pallas as pl
from jax.experimental.pallas import tpu as pltpu
from jax.sharding import PartitionSpec as P


F32 = jnp.float32
BF16 = jnp.bfloat16
ANY = pl.BlockSpec(memory_space=pl.ANY)
SCALARS = pl.BlockSpec(memory_space=pltpu.SMEM)


def room(mib):
    return pltpu.CompilerParams(vmem_limit_bytes=mib << 20)


def cost(flops, bytes_accessed):
    return pl.CostEstimate(flops=flops, bytes_accessed=bytes_accessed, transcendentals=0)


def tile_copies(place, pieces, buf, sem):
    xs = buf.shape[1]
    core, x = place[0] & 1, place[0] // 2
    groups = [[], [], [], []]
    half = buf.shape[0] // 2
    for side, at in ((pieces[:8], core), (pieces[8:], 1 - core)):
        for number, src in enumerate(side):
            group = number // 2
            dst = buf.at[pl.ds(number % 2 * half, half), (x + (0, xs - 1, 1, 2)[group]) & (xs - 1), at]
            count = sum(map(len, groups))
            groups[group].append(pltpu.make_async_copy(src, dst, sem.at[count]))
    return groups


def cycle_kernel(screen, rows, count, place, t_hbm, *refs):
    pieces, (out_hbm, mask, t_ref, z_ref, o_ref, t_sem, z_sem, o_sem) = refs[:16], refs[16:]
    keep, tile = screen.shape[1], z_ref.shape[-1]
    _, window, height, width = t_ref.shape
    tiles_here, tiles_wide = height // tile, width // tile
    tile_count = screen.shape[0] // window
    vir, xs = z_ref.shape[:2]
    first = place[1] * tiles_here
    moves = [pltpu.make_async_copy(t_hbm, t_ref, t_sem)]
    groups = tile_copies(place, pieces, z_ref, z_sem)
    for copy in moves + sum(groups, []):
        copy.start()
    for a in range(tiles_here):

        @pl.loop(0, mask.shape[1])
        def _(q):
            mask[a, q] = 0

        @pl.loop(0, count[first + a])
        def _(e):
            mask[a, rows[first + a, e]] = 1

    for copy in moves:
        copy.wait()

    pairs = o_ref.shape[1]

    def one(v, x):
        q = v * xs + x
        left = []
        for m in range(keep):
            u = screen[q, m]
            c = u % tile_count
            lane = pl.multiple_of((c % tiles_wide) * tile, tile)
            left.append(t_ref[c // tiles_wide, u // tile_count, :, pl.ds(lane, tile)])
        right = z_ref[v, x].reshape(keep * tile, tile)
        part = jnp.dot(jnp.concatenate(left, axis=1), right, preferred_element_type=F32)
        for a in range(tiles_here):
            here = slice(a * tile, (a + 1) * tile)
            used = jnp.full((tile, tile), mask[a, q], jnp.int32) > 0
            o_ref[x, v % pairs, v // pairs, here] = jnp.where(used, part[here], 0.0).astype(BF16)

    unroll = 16
    leaves = []
    for group, shift in zip(groups, (0, xs - 1, 1, 2), strict=True):
        for copy in group:
            copy.wait()
        x = (place[0] // 2 + shift) & (xs - 1)

        @pl.loop(0, vir // unroll)
        def _(outer):
            for inner in range(unroll):
                one(outer * unroll + inner, x)

        lanes = pl.ds(pl.multiple_of((x % tiles_wide) * tile, tile), tile)
        there = out_hbm.at[:, x // tiles_wide, :, :, lanes]
        leaves.append(pltpu.make_async_copy(o_ref.at[x], there, o_sem.at[len(leaves)]))
        leaves[-1].start()
    for copy in leaves:
        copy.wait()


def ladder_kernel(screen, slots, place, t_hbm, near_hbm, *refs):
    pieces, (out_hbm, t_ref, near_ref, w_ref, out_ref, t_sem, near_sem, w_sem, o_sem) = (
        refs[:16],
        refs[16:],
    )
    keep = screen.shape[1]
    window, blocks, _, _ = t_ref.shape
    vir, xs, cores, share = w_ref.shape[:4]
    zs = vir // xs
    per_dev = xs * cores * share
    chunks = o_sem.shape[0]
    size = blocks // chunks
    copies = sum(tile_copies(place, pieces, w_ref, w_sem), [])
    copies.append(pltpu.make_async_copy(t_hbm, t_ref, t_sem))

    def arrive(chunk):
        where = pl.ds(chunk * size, size)
        return pltpu.make_async_copy(
            near_hbm.at[:, where], near_ref.at[:, where], near_sem.at[chunk]
        )

    for copy in copies + [arrive(chunk) for chunk in range(chunks)]:
        copy.start()
    y, z = place[1] // zs, place[1] % zs
    for copy in copies:
        copy.wait()

    def one(block):
        tiles = []
        for k in range(keep):
            slot = slots[block * keep + k]
            v, within = slot // per_dev, slot % per_dev
            behind = ((y - v // zs) & (zs - 1)) * zs + ((z - v % zs) & (zs - 1))
            tiles.append(
                w_ref[behind, within // (cores * share), (within // share) % cores, within % share]
            )
        left = jnp.concatenate(tiles, axis=1)
        for j in range(window):
            right = jnp.concatenate([t_ref[j, screen[block, k]] for k in range(keep)], axis=0)
            out_ref[j, block] = near_ref[j, block].astype(F32) + jnp.dot(
                left, right, preferred_element_type=F32
            )

    unroll = 4

    def leave(chunk):
        where = pl.ds(chunk * size, size)
        return pltpu.make_async_copy(out_ref.at[:, where], out_hbm.at[:, where], o_sem.at[chunk])

    for chunk in range(chunks):
        arrive(chunk).wait()

        @pl.loop(0, size // unroll)
        def _(outer):
            for inner in range(unroll):
                one(chunk * size + outer * unroll + inner)

        leave(chunk).start()
    for chunk in range(chunks):
        leave(chunk).wait()


def final_kernel(slab, pair, place, occ_ref, base_ref, cycle_ref, va_ref, vb_ref, out_ref):
    group, window, rows, cols = cycle_ref.shape
    for g in range(group):
        here = slice(g * rows, (g + 1) * rows)
        energy_a = jnp.broadcast_to(va_ref[:, here], (128, rows)).T
        pairs = jnp.concatenate([energy_a] * (cols // 128), axis=1) + vb_ref[...]
        for j in range(window):
            below = (pairs - occ_ref[slab[place[0]]]) - occ_ref[pair[j]]
            value = base_ref[j, here] + cycle_ref[g, j].astype(F32)
            out_ref[j, here] = (value / below).astype(BF16)


def body(
    amplitudes,
    coulomb,
    ladder_tiles,
    cycle_tiles,
    ladder_screen,
    tile_slot,
    cycle_screen,
    cycle_rows,
    cycle_count,
    slab_occ,
    window_occ,
    occ_energy,
    vir_energy,
):
    occ_count, vir_count = lax.axis_size("occ"), lax.axis_size("vir")
    _, window, width_all, block_cols = amplitudes.shape
    stored, tile, _ = ladder_tiles.shape
    tile_count = width_all // tile
    rows_here = width_all // vir_count
    share = stored // occ_count
    xs, zs = occ_count // 2, 4
    occ_at, vir_at = lax.axis_index("occ"), lax.axis_index("vir")
    place = jnp.stack([occ_at, vir_at]).astype(jnp.int32)
    t = amplitudes[0]
    near = coulomb[0]

    def occ_shift(value, by):
        return lax.ppermute(value, "occ", [(i, (i + 2 * by) % occ_count) for i in range(occ_count)])

    def core_swap(value):
        return lax.ppermute(value, "occ", [(i, i ^ 1) for i in range(occ_count)])

    def vir_shift(value, dy, dz):
        ys = vir_count // zs
        return lax.ppermute(
            value,
            "vir",
            [(y * zs + z, (y + dy) % ys * zs + (z + dz) % zs) for y in range(ys) for z in range(zs)],
        )

    def ring(value, shift, size):
        return jnp.stack([value] + [shift(value, d) for d in range(1, size)])

    def spread(piece):
        half = vir_count // 2
        low, high = piece[:half], piece[half:]
        behind_low, ahead_high = occ_shift(low, 1), occ_shift(high, -1)
        behind_high, ahead_low = occ_shift(high, 1), occ_shift(low, -1)
        far_low, far_high = occ_shift(behind_low, 1), occ_shift(ahead_high, -1)
        mine = (low, high, behind_low, behind_high, ahead_low, ahead_high, far_low, far_high)
        return mine + tuple(core_swap(p) for p in mine)

    def my_share(tiles):
        return lax.dynamic_slice_in_dim(tiles, occ_at * share, share, 0)

    sent = jnp.broadcast_to(my_share(cycle_tiles)[None], (vir_count, share, tile, tile))
    cycle_piece = lax.all_to_all(sent, "vir", 0, 0, tiled=True)
    flat = t.reshape(window, vir_count, rows_here, block_cols).transpose(1, 0, 2, 3)
    line = ring(my_share(ladder_tiles), lambda value, by: vir_shift(value, 0, by), zs)
    flat, cycle_piece, line = lax.optimization_barrier((flat, cycle_piece, line))
    plane = ring(line, lambda value, by: vir_shift(value, by, 0), vir_count // zs)
    moved = lax.all_to_all(flat, "vir", 0, 0, tiled=True)
    cycle_parts = spread(cycle_piece)

    tile_buf = pltpu.VMEM((vir_count, xs, 2, share, tile, tile), BF16)
    dma = pltpu.SemaphoreType.DMA
    size = window * width_all * block_cols
    tile_bytes = 2 * stored * vir_count * tile * tile
    whole = (vir_count, window, rows_here, block_cols)
    paired = (vir_count // 2, 2, window, rows_here, block_cols)
    part = pl.pallas_call(
        cycle_kernel,
        out_shape=pltpu.HBM(paired, BF16),
        grid_spec=pltpu.PrefetchScalarGridSpec(
            num_scalar_prefetch=4,
            grid=(1,),
            in_specs=[ANY] * 17,
            out_specs=ANY,
            scratch_shapes=[
                pltpu.SMEM((rows_here // tile, window * tile_count), jnp.int32),
                pltpu.VMEM(whole, BF16),
                tile_buf,
                pltpu.VMEM((xs, vir_count // 2, window, rows_here, tile), BF16),
                dma(()),
                dma((16,)),
                dma((4,)),
            ],
        ),
        compiler_params=room(60),
        cost_estimate=cost(8 * size * tile, 4 * size + tile_bytes),
    )(cycle_screen, cycle_rows, cycle_count, place, moved, *cycle_parts)
    cycle = lax.all_to_all(part.reshape(whole), "vir", 0, 0, tiled=True)

    ladder_parts = spread(plane.reshape(vir_count, share, tile, tile))
    blocked = (window, tile_count, tile, block_cols)
    base = pl.pallas_call(
        ladder_kernel,
        out_shape=pltpu.HBM(blocked, F32),
        grid_spec=pltpu.PrefetchScalarGridSpec(
            num_scalar_prefetch=3,
            grid=(1,),
            in_specs=[ANY] * 18,
            out_specs=ANY,
            scratch_shapes=[
                pltpu.VMEM(blocked, BF16),
                pltpu.VMEM(blocked, BF16),
                tile_buf,
                pltpu.VMEM(blocked, F32),
                dma(()),
                dma((4,)),
                dma((16,)),
                dma((4,)),
            ],
        ),
        compiler_params=room(60),
        cost_estimate=cost(16 * size * tile, 8 * size + tile_bytes),
    )(ladder_screen, tile_slot, place, t.reshape(blocked), near.reshape(blocked), *ladder_parts)

    energies = vir_energy.reshape(1, width_all)
    group = 4
    out = pl.pallas_call(
        final_kernel,
        out_shape=jax.ShapeDtypeStruct(t.shape, BF16),
        grid_spec=pltpu.PrefetchScalarGridSpec(
            num_scalar_prefetch=3,
            grid=(vir_count // group,),
            in_specs=[
                SCALARS,
                pl.BlockSpec((window, group * rows_here, block_cols), lambda g, *_: (0, g, 0)),
                pl.BlockSpec((group, window, rows_here, block_cols), lambda g, *_: (g, 0, 0, 0)),
                pl.BlockSpec((1, group * rows_here), lambda g, *_: (0, g)),
                pl.BlockSpec((1, block_cols), lambda g, slab, pair, place: (0, place[1])),
            ],
            out_specs=pl.BlockSpec(
                (window, group * rows_here, block_cols), lambda g, *_: (0, g, 0)
            ),
        ),
        compiler_params=room(60),
        cost_estimate=cost(8 * size, 8 * size),
    )(
        slab_occ,
        window_occ,
        place,
        occ_energy,
        base.reshape(t.shape),
        cycle,
        energies,
        energies,
    )
    return out[None]


def solution(mesh):
    wide = P("occ", None, None, "vir")
    tiles = P("vir", None, None)
    return jax.shard_map(
        body,
        mesh=mesh,
        in_specs=(wide, wide, tiles, tiles) + (P(),) * 9,
        out_specs=wide,
        check_vma=False,
    )
```

time: 191 us -> 253 us (1.32)
  the two profiles are of different devices: /device:TPU:1 before, /device:TPU:9 now
where the time goes in v5:
time: 253 us; the launch traced here: 252 us
  waiting for transfers between devices  122 us (48%)
  starting transfers between devices  82.6 us (33%)
  Pallas kernels  36.3 us (14%)
  local copies, waits for them, and re-layouts  9.91 us (4%)
    ppermute x6, waiting for transfers between devices, vir_shift(): lax.ppermute(value, 'vir', [(y * zs + z, (y + dy) % ys * zs + (z + dz) %...  69.1 us
    ppermute x12, waiting for transfers between devices, occ_shift(): lax.ppermute(value, 'occ', [(i, (i + 2 * by) % occ_count) for i in range(...  40.9 us
    ppermute x16, starting transfers between devices, core_swap(): return lax.ppermute(value, 'occ', [(i, i ^ 1) for i in range(occ_count)])  25.2 us
    all_to_all x1, starting transfers between devices, body(): cycle = lax.all_to_all(part.reshape(whole), 'vir', 0, 0, tiled=True)  19.1 us
    pallas_call x1, Pallas kernels, body(): pl.pallas_call(ladder_kernel, out_shape=pltpu.HBM(blocked, F32), grid_spe...  17.3 us
    ppermute x12, starting transfers between devices, occ_shift(): lax.ppermute(value, 'occ', [(i, (i + 2 * by) % occ_count) for i in range(...  15.8 us
    pallas_call x1, Pallas kernels, body(): pl.pallas_call(cycle_kernel, out_shape=pltpu.HBM(paired, BF16), grid_spec...  10.7 us
    all_to_all x1, waiting for transfers between devices, body(): moved = lax.all_to_all(flat, 'vir', 0, 0, tiled=True)  10.4 us
  transfers between devices with their start and end apart: 37, of which 14 were waited for; matrix products, arithmetic and copies ran while one was open for 3% of the time, Pallas kernels for 7%

profile of v5, /device:TPU:9, one launch (start us, length us, event | category | flops | bytes accessed | tf_op | source)
XLA Modules:
  0.0 252.3 jit_solution(3124900496487194493)
XLA Ops:
  2.2 7.8 %all-to-all-start = ((bf16[16,2,128,128]{3,2,1,0:T(8,128)(2,1)}), bf16[16,2,128,128]{3,2,1,0:T(8,128)(2,1)S(1)}, u32[]{:S(2)}, u32[]{:S(2)}) async-start(bf16[16,2,128,128]{3,2,1,0:T(8,128)(2,1)} %broadcast_in_dim.4), calls=%async_computation | async-start | bytes 2097152 | tf_op jit(solution)/shard_map/all_to_all | solution.py:230
  14.9 4.6 %copy.20 = bf16[2,16,256,256]{3,2,0,1:T(8,128)(2,1)} copy(bf16[2,16,256,256]{3,2,1,0:T(8,128)(2,1)} %bitcast.24) | data formatting | bytes 8388608 | tf_op jit(solution)/shard_map/reshape;squeeze | solution.py:231
  19.5 6.9 %collective-permute-done = bf16[2,128,128]{2,1,0:T(8,128)(2,1)S(1)} collective-permute-done((bf16[2,128,128]{2,1,0:T(8,128)(2,1)S(1)}, bf16[2,128,128]{2,1,0:T(8,128)(2,1)S(1)}, u32[]{:S(2)}, u32[]{:S(2)}) %collective-permute-start) | collective-permute-done | bytes 65568 | tf_op jit(solution)/shard_map/ppermute | solution.py:208
  27.0 6.6 %all-to-all-start.1 = ((bf16[16,2,256,256]{3,2,1,0:T(8,128)(2,1)}), bf16[16,2,256,256]{3,2,1,0:T(8,128)(2,1)}, u32[]{:S(2)}, u32[]{:S(2)}) async-start(bf16[16,2,256,256]{3,2,1,0:T(8,128)(2,1)} %bitcast.27), calls=%async_computation.1 | async-start | bytes 8388608 | tf_op jit(solution)/shard_map/all_to_all | solution.py:235
  36.4 2.7 %collective-permute-start.22 = (bf16[8,2,128,128]{3,2,1,0:T(8,128)(2,1)S(1)}, bf16[8,2,128,128]{3,2,1,0:T(8,128)(2,1)}, u32[]{:S(2)}, u32[]{:S(2)}) collective-permute-start(bf16[8,2,128,128]{3,2,1,0:T(8,128)(2,1)S(1)} %get-tuple-element.12.refs_0_), channel_id=1, source_target_pairs={{0,96},{16,112},{32,0},{48,16},{64,32},{80,48},{96,64},{112,80},{1... | collective-permute-start | bytes 1572872 | tf_op jit(solution)/shard_map/ppermute | solution.py:201
  41.2 6.4 %collective-permute-done.20.refs_2_ = bf16[8,2,128,128]{3,2,1,0:T(8,128)(2,1)S(1)} collective-permute-done((bf16[8,2,128,128]{3,2,1,0:T(8,128)(2,1)S(1)}, bf16[8,2,128,128]{3,2,1,0:T(8,128)(2,1)S(1)}, u32[]{:S(2)}, u32[]{:S(2)}) %collective-permute-start.20) | collective-permute-done | bytes 524320 | tf_op jit(solution)/shard_map/ppermute | solution.py:201
  47.6 3.2 %collective-permute-start.27 = (bf16[8,2,128,128]{3,2,1,0:T(8,128)(2,1)S(1)}, bf16[8,2,128,128]{3,2,1,0:T(8,128)(2,1)S(1)}, u32[]{:S(2)}, u32[]{:S(2)}) collective-permute-start(bf16[8,2,128,128]{3,2,1,0:T(8,128)(2,1)S(1)} %get-tuple-element.11.refs_1_), channel_id=1, source_target_pairs={{0,16},{16,0},{32,48},{48,32},{64,80},{80,64},{96,112},{112,96},{1... | collective-permute-start | bytes 1572872 | tf_op jit(solution)/shard_map/ppermute | solution.py:204
  50.7 8.1 %collective-permute-done.21.refs_3_ = bf16[8,2,128,128]{3,2,1,0:T(8,128)(2,1)S(1)} collective-permute-done((bf16[8,2,128,128]{3,2,1,0:T(8,128)(2,1)S(1)}, bf16[8,2,128,128]{3,2,1,0:T(8,128)(2,1)S(1)}, u32[]{:S(2)}, u32[]{:S(2)}) %collective-permute-start.21) | collective-permute-done | bytes 524320 | tf_op jit(solution)/shard_map/ppermute | solution.py:201
  60.1 3.4 %collective-permute-start.28 = (bf16[8,2,128,128]{3,2,1,0:T(8,128)(2,1)S(1)}, bf16[8,2,128,128]{3,2,1,0:T(8,128)(2,1)S(1)}, u32[]{:S(2)}, u32[]{:S(2)}) collective-permute-start(bf16[8,2,128,128]{3,2,1,0:T(8,128)(2,1)S(1)} %collective-permute-done.20.refs_2_), channel_id=1, source_target_pairs={{0,16},{16,0},{32,48},{48,32},{64,80},{80,64},{96,112},{112,96},{1... | collective-permute-start | bytes 1572872 | tf_op jit(solution)/shard_map/ppermute | solution.py:204
  64.0 6.0 %collective-permute-done.24.refs_6_ = bf16[8,2,128,128]{3,2,1,0:T(8,128)(2,1)} collective-permute-done((bf16[8,2,128,128]{3,2,1,0:T(8,128)(2,1)S(1)}, bf16[8,2,128,128]{3,2,1,0:T(8,128)(2,1)}, u32[]{:S(2)}, u32[]{:S(2)}) %collective-permute-start.24) | collective-permute-done | bytes 524320 | tf_op jit(solution)/shard_map/ppermute | solution.py:201
  76.4 10.4 %all-to-all-done.1.t_hbm = bf16[16,2,256,256]{3,2,1,0:T(8,128)(2,1)} async-done(((bf16[16,2,256,256]{3,2,1,0:T(8,128)(2,1)}), bf16[16,2,256,256]{3,2,1,0:T(8,128)(2,1)}, u32[]{:S(2)}, u32[]{:S(2)}) %all-to-all-start.1) | async-done | bytes 4194336 | tf_op jit(solution)/shard_map/all_to_all | solution.py:235
  86.7 10.7 %shard_map.128 = bf16[8,2,2,256,256]{4,3,2,1,0:T(8,128)(2,1)} custom-call(s32[64,4]{1,0:T(8,128)} %copy.18.screen, s32[32,48]{1,0:T(8,128)} %rows.1, s32[32]{0:T(128)} %count.1, s32[2]{0:T(128)} %pad_add_fusion.place, bf16[16,2,256,256]{3,2,1,0:T(8,128)(2,1)} %all-to-all-done.1.t_hbm, bf16[8,2,128,128]{3,2,1,0:T(8,128)(2,1)} %copy-done.4, ...), custom_call_target="tpu_custom_call" | custom-call | flops 2147483648 | bytes 16777216 | tf_op jit(solution)/shard_map/pallas_call | solution.py:244
  97.5 19.1 %all-to-all-start.2 = ((bf16[16,2,256,256]{3,2,1,0:T(8,128)(2,1)}), bf16[16,2,256,256]{3,2,1,0:T(8,128)(2,1)}, u32[]{:S(2)}, u32[]{:S(2)}) async-start(bf16[16,2,256,256]{3,2,1,0:T(8,128)(2,1)} %bitcast.26), calls=%async_computation.2 | async-start | bytes 8388608 | tf_op jit(solution)/shard_map/all_to_all | solution.py:265
  119.8 55.7 %collective-permute-done.4 = bf16[4,2,128,128]{3,2,1,0:T(8,128)(2,1)S(1)} collective-permute-done((bf16[4,2,128,128]{3,2,1,0:T(8,128)(2,1)S(1)}, bf16[4,2,128,128]{3,2,1,0:T(8,128)(2,1)S(1)}, u32[]{:S(2)}, u32[]{:S(2)}) %collective-permute-start.4) | collective-permute-done | bytes 262176 | tf_op jit(solution)/shard_map/ppermute | solution.py:208
  175.5 6.1 %collective-permute-done.5 = bf16[4,2,128,128]{3,2,1,0:T(8,128)(2,1)S(1)} collective-permute-done((bf16[4,2,128,128]{3,2,1,0:T(8,128)(2,1)S(1)}, bf16[4,2,128,128]{3,2,1,0:T(8,128)(2,1)S(1)}, u32[]{:S(2)}, u32[]{:S(2)}) %collective-permute-start.5) | collective-permute-done | bytes 262176 | tf_op jit(solution)/shard_map/ppermute | solution.py:208
  186.2 2.6 %collective-permute-start.8 = (bf16[8,2,128,128]{3,2,1,0:T(8,128)(2,1)S(1)}, bf16[8,2,128,128]{3,2,1,0:T(8,128)(2,1)}, u32[]{:S(2)}, u32[]{:S(2)}) collective-permute-start(bf16[8,2,128,128]{3,2,1,0:T(8,128)(2,1)S(1)} %bitcast.34), channel_id=1, source_target_pairs={{0,96},{16,112},{32,0},{48,16},{64,32},{80,48},{96,64},{112,80},{1... | collective-permute-start | bytes 1572872 | tf_op jit(solution)/shard_map/ppermute | solution.py:201
  188.8 5.6 %collective-permute-done.9.refs_5_ = bf16[8,2,128,128]{3,2,1,0:T(8,128)(2,1)S(1)} collective-permute-done((bf16[8,2,128,128]{3,2,1,0:T(8,128)(2,1)S(1)}, bf16[8,2,128,128]{3,2,1,0:T(8,128)(2,1)S(1)}, u32[]{:S(2)}, u32[]{:S(2)}) %collective-permute-start.9) | collective-permute-done | bytes 524320 | tf_op jit(solution)/shard_map/ppermute | solution.py:201
  194.4 3.5 %collective-permute-start.12 = (bf16[8,2,128,128]{3,2,1,0:T(8,128)(2,1)S(1)}, bf16[8,2,128,128]{3,2,1,0:T(8,128)(2,1)S(1)}, u32[]{:S(2)}, u32[]{:S(2)}) collective-permute-start(bf16[8,2,128,128]{3,2,1,0:T(8,128)(2,1)S(1)} %bitcast.35), channel_id=1, source_target_pairs={{0,16},{16,0},{32,48},{48,32},{64,80},{80,64},{96,112},{112,96},{1... | collective-permute-start | bytes 1572872 | tf_op jit(solution)/shard_map/ppermute | solution.py:204
  197.9 3.4 %collective-permute-start.11 = (bf16[8,2,128,128]{3,2,1,0:T(8,128)(2,1)S(1)}, bf16[8,2,128,128]{3,2,1,0:T(8,128)(2,1)}, u32[]{:S(2)}, u32[]{:S(2)}) collective-permute-start(bf16[8,2,128,128]{3,2,1,0:T(8,128)(2,1)S(1)} %collective-permute-done.9.refs_5_), channel_id=1, source_target_pairs={{0,96},{16,112},{32,0},{48,16},{64,32},{80,48},{96,64},{112,80},{1... | collective-permute-start | bytes 1572872 | tf_op jit(solution)/shard_map/ppermute | solution.py:201
  201.7 7.2 %collective-permute-done.6.refs_2_ = bf16[8,2,128,128]{3,2,1,0:T(8,128)(2,1)} collective-permute-done((bf16[8,2,128,128]{3,2,1,0:T(8,128)(2,1)S(1)}, bf16[8,2,128,128]{3,2,1,0:T(8,128)(2,1)}, u32[]{:S(2)}, u32[]{:S(2)}) %collective-permute-start.6) | collective-permute-done | bytes 524320 | tf_op jit(solution)/shard_map/ppermute | solution.py:201
  211.2 5.6 %collective-permute-done.11.refs_7_ = bf16[8,2,128,128]{3,2,1,0:T(8,128)(2,1)} collective-permute-done((bf16[8,2,128,128]{3,2,1,0:T(8,128)(2,1)S(1)}, bf16[8,2,128,128]{3,2,1,0:T(8,128)(2,1)}, u32[]{:S(2)}, u32[]{:S(2)}) %collective-permute-start.11) | collective-permute-done | bytes 524320 | tf_op jit(solution)/shard_map/ppermute | solution.py:201
  221.6 3.1 %collective-permute-start.18 = (bf16[8,2,128,128]{3,2,1,0:T(8,128)(2,1)}, bf16[8,2,128,128]{3,2,1,0:T(8,128)(2,1)}, u32[]{:S(2)}, u32[]{:S(2)}) collective-permute-start(bf16[8,2,128,128]{3,2,1,0:T(8,128)(2,1)} %collective-permute-done.10.refs_6_), channel_id=1, source_target_pairs={{0,16},{16,0},{32,48},{48,32},{64,80},{80,64},{96,112},{112,96},{1... | collective-permute-start | bytes 1572872 | tf_op jit(solution)/shard_map/ppermute | solution.py:204
  226.6 17.3 %shard_map.127 = f32[2,32,128,256]{3,2,1,0:T(8,128)} custom-call(s32[32,8]{1,0:T(8,128)} %copy.17.screen, s32[256]{0:T(256)} %slots.1, s32[2]{0:T(128)} %pad_add_fusion.place, bf16[2,32,128,256]{3,2,1,0:T(8,128)(2,1)} %bitcast.25, bf16[2,32,128,256]{3,2,1,0:T(8,128)(2,1)} %bitcast.28, bf16[8,2,128,128]{3,2,1,0:T(8,128)(2,1)} %bitcast.36, ...), custom_call_target="tpu_custom_call" | custom-call | flops 4294967296 | bytes 25165824 | tf_op jit(solution)/shard_map/pallas_call | solution.py:269
  244.0 8.3 %shard_map.129 = bf16[2,4096,256]{2,1,0:T(8,128)(2,1)} custom-call(s32[8]{0:T(128)} %slab.1, s32[2]{0:T(128)} %pair.1, s32[2]{0:T(128)} %pad_add_fusion.place, f32[400]{0:T(512)} %occ_ref.1, f32[2,4096,256]{2,1,0:T(8,128)} %bitcast.23, bf16[16,2,256,256]{3,2,1,0:T(8,128)(2,1)} %all-to-all-done.2.cycle_ref, f32[1,4096]{1,0:T(1,128)} %bitcast.44, ...), custom_call_target="tpu_custom_call" | custom-call | flops 16777216 | bytes 16777216 | tf_op jit(solution)/shard_map/pallas_call | solution.py:294
  (101 shorter events, 37.8 us)
Async XLA Ops:
  2.2 24.8 %all-to-all-start = ((bf16[16,2,128,128]{3,2,1,0:T(8,128)(2,1)}), bf16[16,2,128,128]{3,2,1,0:T(8,128)(2,1)S(1)}, u32[]{:S(2)}, u32[]{:S(2)}) async-start(bf16[16,2,128,128]{3,2,1,0:T(8,128)(2,1)} %broadcast_in_dim.4), calls=%async_computation | async-start | bytes 2097152 | tf_op jit(solution)/shard_map/all_to_all | solution.py:230
  10.0 16.3 %collective-permute-start = (bf16[2,128,128]{2,1,0:T(8,128)(2,1)S(1)}, bf16[2,128,128]{2,1,0:T(8,128)(2,1)S(1)}, u32[]{:S(2)}, u32[]{:S(2)}) collective-permute-start(bf16[2,128,128]{2,1,0:T(8,128)(2,1)S(1)} %constant_dynamic-slice_fusion), channel_id=1, source_target_pairs={{0,1},{1,2},{2,3},{3,0},{4,5},{5,6},{6,7},{7,4},{8,9},{9,10},{10,1... | collective-permute-start | bytes 196616 | tf_op jit(solution)/shard_map/ppermute | solution.py:208
  11.3 15.6 %collective-permute-start.1 = (bf16[2,128,128]{2,1,0:T(8,128)(2,1)S(1)}, bf16[2,128,128]{2,1,0:T(8,128)(2,1)S(1)}, u32[]{:S(2)}, u32[]{:S(2)}) collective-permute-start(bf16[2,128,128]{2,1,0:T(8,128)(2,1)S(1)} %constant_dynamic-slice_fusion), channel_id=1, source_target_pairs={{0,2},{1,3},{2,0},{3,1},{4,6},{5,7},{6,4},{7,5},{8,10},{9,11},{10,... | collective-permute-start | bytes 196616 | tf_op jit(solution)/shard_map/ppermute | solution.py:208
  27.0 59.7 %all-to-all-start.1 = ((bf16[16,2,256,256]{3,2,1,0:T(8,128)(2,1)}), bf16[16,2,256,256]{3,2,1,0:T(8,128)(2,1)}, u32[]{:S(2)}, u32[]{:S(2)}) async-start(bf16[16,2,256,256]{3,2,1,0:T(8,128)(2,1)} %bitcast.27), calls=%async_computation.1 | async-start | bytes 8388608 | tf_op jit(solution)/shard_map/all_to_all | solution.py:235
  33.7 13.9 %collective-permute-start.20 = (bf16[8,2,128,128]{3,2,1,0:T(8,128)(2,1)S(1)}, bf16[8,2,128,128]{3,2,1,0:T(8,128)(2,1)S(1)}, u32[]{:S(2)}, u32[]{:S(2)}) collective-permute-start(bf16[8,2,128,128]{3,2,1,0:T(8,128)(2,1)S(1)} %get-tuple-element.12.refs_0_), channel_id=1, source_target_pairs={{0,32},{16,48},{32,64},{48,80},{64,96},{80,112},{96,0},{112,16},{1... | collective-permute-start | bytes 1572872 | tf_op jit(solution)/shard_map/ppermute | solution.py:201
  35.0 15.8 %collective-permute-start.23 = (bf16[8,2,128,128]{3,2,1,0:T(8,128)(2,1)S(1)}, bf16[8,2,128,128]{3,2,1,0:T(8,128)(2,1)S(1)}, u32[]{:S(2)}, u32[]{:S(2)}) collective-permute-start(bf16[8,2,128,128]{3,2,1,0:T(8,128)(2,1)S(1)} %get-tuple-element.11.refs_1_), channel_id=1, source_target_pairs={{0,96},{16,112},{32,0},{48,16},{64,32},{80,48},{96,64},{112,80},{1... | collective-permute-start | bytes 1572872 | tf_op jit(solution)/shard_map/ppermute | solution.py:201
  36.4 22.4 %collective-permute-start.21 = (bf16[8,2,128,128]{3,2,1,0:T(8,128)(2,1)S(1)}, bf16[8,2,128,128]{3,2,1,0:T(8,128)(2,1)S(1)}, u32[]{:S(2)}, u32[]{:S(2)}) collective-permute-start(bf16[8,2,128,128]{3,2,1,0:T(8,128)(2,1)S(1)} %get-tuple-element.11.refs_1_), channel_id=1, source_target_pairs={{0,32},{16,48},{32,64},{48,80},{64,96},{80,112},{96,0},{112,16},{1... | collective-permute-start | bytes 1572872 | tf_op jit(solution)/shard_map/ppermute | solution.py:201
  36.4 23.7 %collective-permute-start.22 = (bf16[8,2,128,128]{3,2,1,0:T(8,128)(2,1)S(1)}, bf16[8,2,128,128]{3,2,1,0:T(8,128)(2,1)}, u32[]{:S(2)}, u32[]{:S(2)}) collective-permute-start(bf16[8,2,128,128]{3,2,1,0:T(8,128)(2,1)S(1)} %get-tuple-element.12.refs_0_), channel_id=1, source_target_pairs={{0,96},{16,112},{32,0},{48,16},{64,32},{80,48},{96,64},{112,80},{1... | collective-permute-start | bytes 1572872 | tf_op jit(solution)/shard_map/ppermute | solution.py:201
  39.1 24.4 %collective-permute-start.26 = (bf16[8,2,128,128]{3,2,1,0:T(8,128)(2,1)S(1)}, bf16[8,2,128,128]{3,2,1,0:T(8,128)(2,1)S(1)}, u32[]{:S(2)}, u32[]{:S(2)}) collective-permute-start(bf16[8,2,128,128]{3,2,1,0:T(8,128)(2,1)S(1)} %get-tuple-element.12.refs_0_), channel_id=1, source_target_pairs={{0,16},{16,0},{32,48},{48,32},{64,80},{80,64},{96,112},{112,96},{1... | collective-permute-start | bytes 1572872 | tf_op jit(solution)/shard_map/ppermute | solution.py:204
  47.6 16.0 %collective-permute-start.27 = (bf16[8,2,128,128]{3,2,1,0:T(8,128)(2,1)S(1)}, bf16[8,2,128,128]{3,2,1,0:T(8,128)(2,1)S(1)}, u32[]{:S(2)}, u32[]{:S(2)}) collective-permute-start(bf16[8,2,128,128]{3,2,1,0:T(8,128)(2,1)S(1)} %get-tuple-element.11.refs_1_), channel_id=1, source_target_pairs={{0,16},{16,0},{32,48},{48,32},{64,80},{80,64},{96,112},{112,96},{1... | collective-permute-start | bytes 1572872 | tf_op jit(solution)/shard_map/ppermute | solution.py:204
  50.7 19.3 %collective-permute-start.24 = (bf16[8,2,128,128]{3,2,1,0:T(8,128)(2,1)S(1)}, bf16[8,2,128,128]{3,2,1,0:T(8,128)(2,1)}, u32[]{:S(2)}, u32[]{:S(2)}) collective-permute-start(bf16[8,2,128,128]{3,2,1,0:T(8,128)(2,1)S(1)} %collective-permute-done.20.refs_2_), channel_id=1, source_target_pairs={{0,32},{16,48},{32,64},{48,80},{64,96},{80,112},{96,0},{112,16},{1... | collective-permute-start | bytes 1572872 | tf_op jit(solution)/shard_map/ppermute | solution.py:201
  97.5 146.5 %all-to-all-start.2 = ((bf16[16,2,256,256]{3,2,1,0:T(8,128)(2,1)}), bf16[16,2,256,256]{3,2,1,0:T(8,128)(2,1)}, u32[]{:S(2)}, u32[]{:S(2)}) async-start(bf16[16,2,256,256]{3,2,1,0:T(8,128)(2,1)} %bitcast.26), calls=%async_computation.2 | async-start | bytes 8388608 | tf_op jit(solution)/shard_map/all_to_all | solution.py:265
  116.6 58.9 %collective-permute-start.4 = (bf16[4,2,128,128]{3,2,1,0:T(8,128)(2,1)S(1)}, bf16[4,2,128,128]{3,2,1,0:T(8,128)(2,1)S(1)}, u32[]{:S(2)}, u32[]{:S(2)}) collective-permute-start(bf16[4,2,128,128]{3,2,1,0:T(8,128)(2,1)S(1)} %pad_maximum_fusion.2), channel_id=1, source_target_pairs={{0,8},{1,9},{2,10},{3,11},{4,12},{5,13},{6,14},{7,15},{8,0},{9,1},... | collective-permute-start | bytes 786440 | tf_op jit(solution)/shard_map/ppermute | solution.py:208
  118.4 63.2 %collective-permute-start.5 = (bf16[4,2,128,128]{3,2,1,0:T(8,128)(2,1)S(1)}, bf16[4,2,128,128]{3,2,1,0:T(8,128)(2,1)S(1)}, u32[]{:S(2)}, u32[]{:S(2)}) collective-permute-start(bf16[4,2,128,128]{3,2,1,0:T(8,128)(2,1)S(1)} %pad_maximum_fusion.2), channel_id=1, source_target_pairs={{0,12},{1,13},{2,14},{3,15},{4,0},{5,1},{6,2},{7,3},{8,4},{9,5},{1... | collective-permute-start | bytes 786440 | tf_op jit(solution)/shard_map/ppermute | solution.py:208
  119.6 66.1 %collective-permute-start.3 = (bf16[4,2,128,128]{3,2,1,0:T(8,128)(2,1)S(1)}, bf16[4,2,128,128]{3,2,1,0:T(8,128)(2,1)S(1)}, u32[]{:S(2)}, u32[]{:S(2)}) collective-permute-start(bf16[4,2,128,128]{3,2,1,0:T(8,128)(2,1)S(1)} %pad_maximum_fusion.2), channel_id=1, source_target_pairs={{0,4},{1,5},{2,6},{3,7},{4,8},{5,9},{6,10},{7,11},{8,12},{9,13},{1... | collective-permute-start | bytes 786440 | tf_op jit(solution)/shard_map/ppermute | solution.py:208
  184.2 13.7 %collective-permute-start.7 = (bf16[8,2,128,128]{3,2,1,0:T(8,128)(2,1)S(1)}, bf16[8,2,128,128]{3,2,1,0:T(8,128)(2,1)S(1)}, u32[]{:S(2)}, u32[]{:S(2)}) collective-permute-start(bf16[8,2,128,128]{3,2,1,0:T(8,128)(2,1)S(1)} %bitcast.30), channel_id=1, source_target_pairs={{0,32},{16,48},{32,64},{48,80},{64,96},{80,112},{96,0},{112,16},{1... | collective-permute-start | bytes 1572872 | tf_op jit(solution)/shard_map/ppermute | solution.py:201
  184.2 17.1 %collective-permute-start.13 = (bf16[8,2,128,128]{3,2,1,0:T(8,128)(2,1)S(1)}, bf16[8,2,128,128]{3,2,1,0:T(8,128)(2,1)S(1)}, u32[]{:S(2)}, u32[]{:S(2)}) collective-permute-start(bf16[8,2,128,128]{3,2,1,0:T(8,128)(2,1)S(1)} %bitcast.31), channel_id=1, source_target_pairs={{0,16},{16,0},{32,48},{48,32},{64,80},{80,64},{96,112},{112,96},{1... | collective-permute-start | bytes 1572872 | tf_op jit(solution)/shard_map/ppermute | solution.py:204
  185.7 23.2 %collective-permute-start.6 = (bf16[8,2,128,128]{3,2,1,0:T(8,128)(2,1)S(1)}, bf16[8,2,128,128]{3,2,1,0:T(8,128)(2,1)}, u32[]{:S(2)}, u32[]{:S(2)}) collective-permute-start(bf16[8,2,128,128]{3,2,1,0:T(8,128)(2,1)S(1)} %bitcast.33), channel_id=1, source_target_pairs={{0,32},{16,48},{32,64},{48,80},{64,96},{80,112},{96,0},{112,16},{1... | collective-permute-start | bytes 1572872 | tf_op jit(solution)/shard_map/ppermute | solution.py:201
  186.2 22.7 %collective-permute-start.8 = (bf16[8,2,128,128]{3,2,1,0:T(8,128)(2,1)S(1)}, bf16[8,2,128,128]{3,2,1,0:T(8,128)(2,1)}, u32[]{:S(2)}, u32[]{:S(2)}) collective-permute-start(bf16[8,2,128,128]{3,2,1,0:T(8,128)(2,1)S(1)} %bitcast.34), channel_id=1, source_target_pairs={{0,96},{16,112},{32,0},{48,16},{64,32},{80,48},{96,64},{112,80},{1... | collective-permute-start | bytes 1572872 | tf_op jit(solution)/shard_map/ppermute | solution.py:201
  194.4 16.7 %collective-permute-start.12 = (bf16[8,2,128,128]{3,2,1,0:T(8,128)(2,1)S(1)}, bf16[8,2,128,128]{3,2,1,0:T(8,128)(2,1)S(1)}, u32[]{:S(2)}, u32[]{:S(2)}) collective-permute-start(bf16[8,2,128,128]{3,2,1,0:T(8,128)(2,1)S(1)} %bitcast.35), channel_id=1, source_target_pairs={{0,16},{16,0},{32,48},{48,32},{64,80},{80,64},{96,112},{112,96},{1... | collective-permute-start | bytes 1572872 | tf_op jit(solution)/shard_map/ppermute | solution.py:204
  197.9 18.9 %collective-permute-start.11 = (bf16[8,2,128,128]{3,2,1,0:T(8,128)(2,1)S(1)}, bf16[8,2,128,128]{3,2,1,0:T(8,128)(2,1)}, u32[]{:S(2)}, u32[]{:S(2)}) collective-permute-start(bf16[8,2,128,128]{3,2,1,0:T(8,128)(2,1)S(1)} %collective-permute-done.9.refs_5_), channel_id=1, source_target_pairs={{0,96},{16,112},{32,0},{48,16},{64,32},{80,48},{96,64},{112,80},{1... | collective-permute-start | bytes 1572872 | tf_op jit(solution)/shard_map/ppermute | solution.py:201
  201.3 17.5 %collective-permute-start.15 = (bf16[8,2,128,128]{3,2,1,0:T(8,128)(2,1)S(1)}, bf16[8,2,128,128]{3,2,1,0:T(8,128)(2,1)S(1)}, u32[]{:S(2)}, u32[]{:S(2)}) collective-permute-start(bf16[8,2,128,128]{3,2,1,0:T(8,128)(2,1)S(1)} %collective-permute-done.7.refs_3_), channel_id=1, source_target_pairs={{0,16},{16,0},{32,48},{48,32},{64,80},{80,64},{96,112},{112,96},{1... | collective-permute-start | bytes 1572872 | tf_op jit(solution)/shard_map/ppermute | solution.py:204
  208.9 16.5 %collective-permute-start.17 = (bf16[8,2,128,128]{3,2,1,0:T(8,128)(2,1)S(1)}, bf16[8,2,128,128]{3,2,1,0:T(8,128)(2,1)}, u32[]{:S(2)}, u32[]{:S(2)}) collective-permute-start(bf16[8,2,128,128]{3,2,1,0:T(8,128)(2,1)S(1)} %collective-permute-done.9.refs_5_), channel_id=1, source_target_pairs={{0,16},{16,0},{32,48},{48,32},{64,80},{80,64},{96,112},{112,96},{1... | collective-permute-start | bytes 1572872 | tf_op jit(solution)/shard_map/ppermute | solution.py:204
  211.1 14.3 %collective-permute-start.14 = (bf16[8,2,128,128]{3,2,1,0:T(8,128)(2,1)}, bf16[8,2,128,128]{3,2,1,0:T(8,128)(2,1)}, u32[]{:S(2)}, u32[]{:S(2)}) collective-permute-start(bf16[8,2,128,128]{3,2,1,0:T(8,128)(2,1)} %collective-permute-done.6.refs_2_), channel_id=1, source_target_pairs={{0,16},{16,0},{32,48},{48,32},{64,80},{80,64},{96,112},{112,96},{1... | collective-permute-start | bytes 1572872 | tf_op jit(solution)/shard_map/ppermute | solution.py:204
  (31 other events, 714.7 us)

commit v6 on v5

--- a/solution.py
+++ b/solution.py
@@ -229,8 +229,9 @@
     sent = jnp.broadcast_to(my_share(cycle_tiles)[None], (vir_count, share, tile, tile))
     cycle_piece = lax.all_to_all(sent, "vir", 0, 0, tiled=True)
     flat = t.reshape(window, vir_count, rows_here, block_cols).transpose(1, 0, 2, 3)
-    line = ring(my_share(ladder_tiles), lambda value, by: vir_shift(value, 0, by), zs)
-    flat, cycle_piece, line = lax.optimization_barrier((flat, cycle_piece, line))
+    ladder_share = my_share(ladder_tiles)
+    line = ring(ladder_share, lambda value, by: vir_shift(value, 0, by), zs)
+    flat, cycle_piece = lax.optimization_barrier((flat, cycle_piece))
     plane = ring(line, lambda value, by: vir_shift(value, by, 0), vir_count // zs)
     moved = lax.all_to_all(flat, "vir", 0, 0, tiled=True)
     cycle_parts = spread(cycle_piece)
@@ -290,7 +291,7 @@
     )(ladder_screen, tile_slot, place, t.reshape(blocked), near.reshape(blocked), *ladder_parts)
 
     energies = vir_energy.reshape(1, width_all)
-    group = 4
+    group = 8
     out = pl.pallas_call(
         final_kernel,
         out_shape=jax.ShapeDtypeStruct(t.shape, BF16),

time: 253 us -> 238 us (0.941)
  the two profiles are of different devices: /device:TPU:9 before, /device:TPU:1 now
where the time goes in v6:
time: 238 us; the launch traced here: 237 us
  starting transfers between devices  95.7 us (40%)
  waiting for transfers between devices  95 us (40%)
  Pallas kernels  36.4 us (15%)
  local copies, waits for them, and re-layouts  9.18 us (4%)
    ppermute x6, waiting for transfers between devices, vir_shift(): lax.ppermute(value, 'vir', [(y * zs + z, (y + dy) % ys * zs + (z + dz) %...  46.7 us
    ppermute x16, starting transfers between devices, core_swap(): return lax.ppermute(value, 'occ', [(i, i ^ 1) for i in range(occ_count)])  40.5 us
    ppermute x12, waiting for transfers between devices, occ_shift(): lax.ppermute(value, 'occ', [(i, (i + 2 * by) % occ_count) for i in range(...  28.8 us
    ppermute x6, starting transfers between devices, vir_shift(): lax.ppermute(value, 'vir', [(y * zs + z, (y + dy) % ys * zs + (z + dz) %...  19.8 us
    pallas_call x1, Pallas kernels, body(): pl.pallas_call(ladder_kernel, out_shape=pltpu.HBM(blocked, F32), grid_spe...  17.4 us
    ppermute x12, starting transfers between devices, occ_shift(): lax.ppermute(value, 'occ', [(i, (i + 2 * by) % occ_count) for i in range(...  15.2 us
    all_to_all x1, waiting for transfers between devices, body(): cycle_piece = lax.all_to_all(sent, 'vir', 0, 0, tiled=True)  11 us
    pallas_call x1, Pallas kernels, body(): pl.pallas_call(cycle_kernel, out_shape=pltpu.HBM(paired, BF16), grid_spec...  10.7 us
  transfers between devices with their start and end apart: 37, of which 14 were waited for; matrix products, arithmetic and copies ran while one was open for 3% of the time, Pallas kernels for 7%

profile of v6, /device:TPU:1, one launch (start us, length us, event | category | flops | bytes accessed | tf_op | source)
XLA Modules:
  0.0 237.3 jit_solution(15744864746054442394)
XLA Ops:
  2.2 8.6 %all-to-all-start = ((bf16[16,2,128,128]{3,2,1,0:T(8,128)(2,1)}), bf16[16,2,128,128]{3,2,1,0:T(8,128)(2,1)S(1)}, u32[]{:S(2)}, u32[]{:S(2)}) async-start(bf16[16,2,128,128]{3,2,1,0:T(8,128)(2,1)} %broadcast_in_dim.4), calls=%async_computation | async-start | bytes 2097152 | tf_op jit(solution)/shard_map/all_to_all | solution.py:230
  10.7 4.6 %copy.20 = bf16[2,16,256,256]{3,2,0,1:T(8,128)(2,1)} copy(bf16[2,16,256,256]{3,2,1,0:T(8,128)(2,1)} %bitcast.25) | data formatting | bytes 8388608 | tf_op jit(solution)/shard_map/reshape;squeeze | solution.py:231
  15.4 11.0 %all-to-all-done = bf16[16,2,128,128]{3,2,1,0:T(8,128)(2,1)S(1)} async-done(((bf16[16,2,128,128]{3,2,1,0:T(8,128)(2,1)}), bf16[16,2,128,128]{3,2,1,0:T(8,128)(2,1)S(1)}, u32[]{:S(2)}, u32[]{:S(2)}) %all-to-all-start) | async-done | bytes 1048608 | tf_op jit(solution)/shard_map/all_to_all | solution.py:230
  26.4 4.7 %all-to-all-start.1 = ((bf16[16,2,256,256]{3,2,1,0:T(8,128)(2,1)}), bf16[16,2,256,256]{3,2,1,0:T(8,128)(2,1)}, u32[]{:S(2)}, u32[]{:S(2)}) async-start(bf16[16,2,256,256]{3,2,1,0:T(8,128)(2,1)} %bitcast.28), calls=%async_computation.1 | async-start | bytes 8388608 | tf_op jit(solution)/shard_map/all_to_all | solution.py:236
  36.7 4.2 %collective-permute-start.26 = (bf16[8,2,128,128]{3,2,1,0:T(8,128)(2,1)S(1)}, bf16[8,2,128,128]{3,2,1,0:T(8,128)(2,1)S(1)}, u32[]{:S(2)}, u32[]{:S(2)}) collective-permute-start(bf16[8,2,128,128]{3,2,1,0:T(8,128)(2,1)S(1)} %get-tuple-element.10.refs_0_), channel_id=1, source_target_pairs={{0,16},{16,0},{32,48},{48,32},{64,80},{80,64},{96,112},{112,96},{1... | collective-permute-start | bytes 1572872 | tf_op jit(solution)/shard_map/ppermute | solution.py:204
  43.1 7.3 %collective-permute-start.27 = (bf16[8,2,128,128]{3,2,1,0:T(8,128)(2,1)S(1)}, bf16[8,2,128,128]{3,2,1,0:T(8,128)(2,1)S(1)}, u32[]{:S(2)}, u32[]{:S(2)}) collective-permute-start(bf16[8,2,128,128]{3,2,1,0:T(8,128)(2,1)S(1)} %get-tuple-element.9.refs_1_), channel_id=1, source_target_pairs={{0,16},{16,0},{32,48},{48,32},{64,80},{80,64},{96,112},{112,96},{1... | collective-permute-start | bytes 1572872 | tf_op jit(solution)/shard_map/ppermute | solution.py:204
  50.4 3.9 %collective-permute-done.21.refs_3_ = bf16[8,2,128,128]{3,2,1,0:T(8,128)(2,1)S(1)} collective-permute-done((bf16[8,2,128,128]{3,2,1,0:T(8,128)(2,1)S(1)}, bf16[8,2,128,128]{3,2,1,0:T(8,128)(2,1)S(1)}, u32[]{:S(2)}, u32[]{:S(2)}) %collective-permute-start.21) | collective-permute-done | bytes 524320 | tf_op jit(solution)/shard_map/ppermute | solution.py:201
  55.6 7.6 %collective-permute-start.28 = (bf16[8,2,128,128]{3,2,1,0:T(8,128)(2,1)S(1)}, bf16[8,2,128,128]{3,2,1,0:T(8,128)(2,1)S(1)}, u32[]{:S(2)}, u32[]{:S(2)}) collective-permute-start(bf16[8,2,128,128]{3,2,1,0:T(8,128)(2,1)S(1)} %collective-permute-done.20.refs_2_), channel_id=1, source_target_pairs={{0,16},{16,0},{32,48},{48,32},{64,80},{80,64},{96,112},{112,96},{1... | collective-permute-start | bytes 1572872 | tf_op jit(solution)/shard_map/ppermute | solution.py:204
  65.6 3.8 %collective-permute-start.30 = (bf16[8,2,128,128]{3,2,1,0:T(8,128)(2,1)}, bf16[8,2,128,128]{3,2,1,0:T(8,128)(2,1)}, u32[]{:S(2)}, u32[]{:S(2)}) collective-permute-start(bf16[8,2,128,128]{3,2,1,0:T(8,128)(2,1)} %collective-permute-done.22.refs_4_), channel_id=1, source_target_pairs={{0,16},{16,0},{32,48},{48,32},{64,80},{80,64},{96,112},{112,96},{1... | collective-permute-start | bytes 1572872 | tf_op jit(solution)/shard_map/ppermute | solution.py:204
  73.9 6.4 %all-to-all-done.1.t_hbm = bf16[16,2,256,256]{3,2,1,0:T(8,128)(2,1)} async-done(((bf16[16,2,256,256]{3,2,1,0:T(8,128)(2,1)}), bf16[16,2,256,256]{3,2,1,0:T(8,128)(2,1)}, u32[]{:S(2)}, u32[]{:S(2)}) %all-to-all-start.1) | async-done | bytes 4194336 | tf_op jit(solution)/shard_map/all_to_all | solution.py:236
  80.3 10.7 %shard_map.128 = bf16[8,2,2,256,256]{4,3,2,1,0:T(8,128)(2,1)} custom-call(s32[64,4]{1,0:T(8,128)} %copy.18.screen, s32[32,48]{1,0:T(8,128)} %rows.1, s32[32]{0:T(128)} %count.1, s32[2]{0:T(128)} %pad_add_fusion.place, bf16[16,2,256,256]{3,2,1,0:T(8,128)(2,1)} %all-to-all-done.1.t_hbm, bf16[8,2,128,128]{3,2,1,0:T(8,128)(2,1)} %copy-done.4, ...), custom_call_target="tpu_custom_call" | custom-call | flops 2147483648 | bytes 16777216 | tf_op jit(solution)/shard_map/pallas_call | solution.py:245
  91.0 6.9 %all-to-all-start.2 = ((bf16[16,2,256,256]{3,2,1,0:T(8,128)(2,1)}), bf16[16,2,256,256]{3,2,1,0:T(8,128)(2,1)}, u32[]{:S(2)}, u32[]{:S(2)}) async-start(bf16[16,2,256,256]{3,2,1,0:T(8,128)(2,1)} %bitcast.27), calls=%async_computation.2 | async-start | bytes 8388608 | tf_op jit(solution)/shard_map/all_to_all | solution.py:266
  103.1 35.8 %collective-permute-done = bf16[2,128,128]{2,1,0:T(8,128)(2,1)S(1)} collective-permute-done((bf16[2,128,128]{2,1,0:T(8,128)(2,1)S(1)}, bf16[2,128,128]{2,1,0:T(8,128)(2,1)S(1)}, u32[]{:S(2)}, u32[]{:S(2)}) %collective-permute-start) | collective-permute-done | bytes 65568 | tf_op jit(solution)/shard_map/ppermute | solution.py:208
  138.9 12.1 %collective-permute-start.4 = (bf16[4,2,128,128]{3,2,1,0:T(8,128)(2,1)S(1)}, bf16[4,2,128,128]{3,2,1,0:T(8,128)(2,1)S(1)}, u32[]{:S(2)}, u32[]{:S(2)}) collective-permute-start(bf16[4,2,128,128]{3,2,1,0:T(8,128)(2,1)S(1)} %get-tuple-element.12), channel_id=1, source_target_pairs={{0,8},{1,9},{2,10},{3,11},{4,12},{5,13},{6,14},{7,15},{8,0},{9,1},... | collective-permute-start | bytes 786440 | tf_op jit(solution)/shard_map/ppermute | solution.py:208
  154.9 9.6 %collective-permute-done.5 = bf16[4,2,128,128]{3,2,1,0:T(8,128)(2,1)S(1)} collective-permute-done((bf16[4,2,128,128]{3,2,1,0:T(8,128)(2,1)S(1)}, bf16[4,2,128,128]{3,2,1,0:T(8,128)(2,1)S(1)}, u32[]{:S(2)}, u32[]{:S(2)}) %collective-permute-start.5) | collective-permute-done | bytes 262176 | tf_op jit(solution)/shard_map/ppermute | solution.py:208
  172.6 3.8 %collective-permute-done.9.refs_5_ = bf16[8,2,128,128]{3,2,1,0:T(8,128)(2,1)S(1)} collective-permute-done((bf16[8,2,128,128]{3,2,1,0:T(8,128)(2,1)S(1)}, bf16[8,2,128,128]{3,2,1,0:T(8,128)(2,1)S(1)}, u32[]{:S(2)}, u32[]{:S(2)}) %collective-permute-start.9) | collective-permute-done | bytes 524320 | tf_op jit(solution)/shard_map/ppermute | solution.py:201
  176.4 5.3 %collective-permute-start.12 = (bf16[8,2,128,128]{3,2,1,0:T(8,128)(2,1)S(1)}, bf16[8,2,128,128]{3,2,1,0:T(8,128)(2,1)S(1)}, u32[]{:S(2)}, u32[]{:S(2)}) collective-permute-start(bf16[8,2,128,128]{3,2,1,0:T(8,128)(2,1)S(1)} %bitcast.36), channel_id=1, source_target_pairs={{0,16},{16,0},{32,48},{48,32},{64,80},{80,64},{96,112},{112,96},{1... | collective-permute-start | bytes 1572872 | tf_op jit(solution)/shard_map/ppermute | solution.py:204
  181.7 3.4 %collective-permute-start.11 = (bf16[8,2,128,128]{3,2,1,0:T(8,128)(2,1)S(1)}, bf16[8,2,128,128]{3,2,1,0:T(8,128)(2,1)}, u32[]{:S(2)}, u32[]{:S(2)}) collective-permute-start(bf16[8,2,128,128]{3,2,1,0:T(8,128)(2,1)S(1)} %collective-permute-done.9.refs_5_), channel_id=1, source_target_pairs={{0,96},{16,112},{32,0},{48,16},{64,32},{80,48},{96,64},{112,80},{1... | collective-permute-start | bytes 1572872 | tf_op jit(solution)/shard_map/ppermute | solution.py:201
  185.1 5.7 %collective-permute-done.6.refs_2_ = bf16[8,2,128,128]{3,2,1,0:T(8,128)(2,1)S(1)} collective-permute-done((bf16[8,2,128,128]{3,2,1,0:T(8,128)(2,1)S(1)}, bf16[8,2,128,128]{3,2,1,0:T(8,128)(2,1)S(1)}, u32[]{:S(2)}, u32[]{:S(2)}) %collective-permute-start.6) | collective-permute-done | bytes 524320 | tf_op jit(solution)/shard_map/ppermute | solution.py:201
  190.8 3.1 %collective-permute-start.17 = (bf16[8,2,128,128]{3,2,1,0:T(8,128)(2,1)S(1)}, bf16[8,2,128,128]{3,2,1,0:T(8,128)(2,1)S(1)}, u32[]{:S(2)}, u32[]{:S(2)}) collective-permute-start(bf16[8,2,128,128]{3,2,1,0:T(8,128)(2,1)S(1)} %collective-permute-done.9.refs_5_), channel_id=1, source_target_pairs={{0,16},{16,0},{32,48},{48,32},{64,80},{80,64},{96,112},{112,96},{1... | collective-permute-start | bytes 1572872 | tf_op jit(solution)/shard_map/ppermute | solution.py:204
  194.6 4.4 %collective-permute-done.11.refs_7_ = bf16[8,2,128,128]{3,2,1,0:T(8,128)(2,1)} collective-permute-done((bf16[8,2,128,128]{3,2,1,0:T(8,128)(2,1)S(1)}, bf16[8,2,128,128]{3,2,1,0:T(8,128)(2,1)}, u32[]{:S(2)}, u32[]{:S(2)}) %collective-permute-start.11) | collective-permute-done | bytes 524320 | tf_op jit(solution)/shard_map/ppermute | solution.py:201
  201.8 6.8 %collective-permute-done.10.refs_6_ = bf16[8,2,128,128]{3,2,1,0:T(8,128)(2,1)} collective-permute-done((bf16[8,2,128,128]{3,2,1,0:T(8,128)(2,1)S(1)}, bf16[8,2,128,128]{3,2,1,0:T(8,128)(2,1)}, u32[]{:S(2)}, u32[]{:S(2)}) %collective-permute-start.10) | collective-permute-done | bytes 524320 | tf_op jit(solution)/shard_map/ppermute | solution.py:201
  211.6 17.4 %shard_map.127 = f32[2,32,128,256]{3,2,1,0:T(8,128)} custom-call(s32[32,8]{1,0:T(8,128)} %copy.16.screen, s32[256]{0:T(256)} %slots.1, s32[2]{0:T(128)} %pad_add_fusion.place, bf16[2,32,128,256]{3,2,1,0:T(8,128)(2,1)} %bitcast.26, bf16[2,32,128,256]{3,2,1,0:T(8,128)(2,1)} %bitcast.29, bf16[8,2,128,128]{3,2,1,0:T(8,128)(2,1)} %bitcast.37, ...), custom_call_target="tpu_custom_call" | custom-call | flops 4294967296 | bytes 25165824 | tf_op jit(solution)/shard_map/pallas_call | solution.py:270
  229.0 8.3 %shard_map.129 = bf16[2,4096,256]{2,1,0:T(8,128)(2,1)} custom-call(s32[8]{0:T(128)} %slab.1, s32[2]{0:T(128)} %pair.1, s32[2]{0:T(128)} %pad_add_fusion.place, f32[400]{0:T(512)} %occ_ref.1, f32[2,4096,256]{2,1,0:T(8,128)} %bitcast.24, bf16[16,2,256,256]{3,2,1,0:T(8,128)(2,1)} %all-to-all-done.2.cycle_ref, f32[1,4096]{1,0:T(1,128)} %bitcast.44, ...), custom_call_target="tpu_custom_call" | custom-call | flops 16777216 | bytes 16777216 | tf_op jit(solution)/shard_map/pallas_call | solution.py:295
  (103 shorter events, 41.7 us)
Async XLA Ops:
  2.2 24.3 %all-to-all-start = ((bf16[16,2,128,128]{3,2,1,0:T(8,128)(2,1)}), bf16[16,2,128,128]{3,2,1,0:T(8,128)(2,1)S(1)}, u32[]{:S(2)}, u32[]{:S(2)}) async-start(bf16[16,2,128,128]{3,2,1,0:T(8,128)(2,1)} %broadcast_in_dim.4), calls=%async_computation | async-start | bytes 2097152 | tf_op jit(solution)/shard_map/all_to_all | solution.py:230
  26.4 53.8 %all-to-all-start.1 = ((bf16[16,2,256,256]{3,2,1,0:T(8,128)(2,1)}), bf16[16,2,256,256]{3,2,1,0:T(8,128)(2,1)}, u32[]{:S(2)}, u32[]{:S(2)}) async-start(bf16[16,2,256,256]{3,2,1,0:T(8,128)(2,1)} %bitcast.28), calls=%async_computation.1 | async-start | bytes 8388608 | tf_op jit(solution)/shard_map/all_to_all | solution.py:236
  32.5 17.8 %collective-permute-start.23 = (bf16[8,2,128,128]{3,2,1,0:T(8,128)(2,1)S(1)}, bf16[8,2,128,128]{3,2,1,0:T(8,128)(2,1)S(1)}, u32[]{:S(2)}, u32[]{:S(2)}) collective-permute-start(bf16[8,2,128,128]{3,2,1,0:T(8,128)(2,1)S(1)} %get-tuple-element.9.refs_1_), channel_id=1, source_target_pairs={{0,96},{16,112},{32,0},{48,16},{64,32},{80,48},{96,64},{112,80},{1... | collective-permute-start | bytes 1572872 | tf_op jit(solution)/shard_map/ppermute | solution.py:201
  34.0 20.3 %collective-permute-start.21 = (bf16[8,2,128,128]{3,2,1,0:T(8,128)(2,1)S(1)}, bf16[8,2,128,128]{3,2,1,0:T(8,128)(2,1)S(1)}, u32[]{:S(2)}, u32[]{:S(2)}) collective-permute-start(bf16[8,2,128,128]{3,2,1,0:T(8,128)(2,1)S(1)} %get-tuple-element.9.refs_1_), channel_id=1, source_target_pairs={{0,32},{16,48},{32,64},{48,80},{64,96},{80,112},{96,0},{112,16},{1... | collective-permute-start | bytes 1572872 | tf_op jit(solution)/shard_map/ppermute | solution.py:201
  34.0 21.6 %collective-permute-start.22 = (bf16[8,2,128,128]{3,2,1,0:T(8,128)(2,1)S(1)}, bf16[8,2,128,128]{3,2,1,0:T(8,128)(2,1)}, u32[]{:S(2)}, u32[]{:S(2)}) collective-permute-start(bf16[8,2,128,128]{3,2,1,0:T(8,128)(2,1)S(1)} %get-tuple-element.10.refs_0_), channel_id=1, source_target_pairs={{0,96},{16,112},{32,0},{48,16},{64,32},{80,48},{96,64},{112,80},{1... | collective-permute-start | bytes 1572872 | tf_op jit(solution)/shard_map/ppermute | solution.py:201
  36.7 26.5 %collective-permute-start.26 = (bf16[8,2,128,128]{3,2,1,0:T(8,128)(2,1)S(1)}, bf16[8,2,128,128]{3,2,1,0:T(8,128)(2,1)S(1)}, u32[]{:S(2)}, u32[]{:S(2)}) collective-permute-start(bf16[8,2,128,128]{3,2,1,0:T(8,128)(2,1)S(1)} %get-tuple-element.10.refs_0_), channel_id=1, source_target_pairs={{0,16},{16,0},{32,48},{48,32},{64,80},{80,64},{96,112},{112,96},{1... | collective-permute-start | bytes 1572872 | tf_op jit(solution)/shard_map/ppermute | solution.py:204
  43.1 20.2 %collective-permute-start.27 = (bf16[8,2,128,128]{3,2,1,0:T(8,128)(2,1)S(1)}, bf16[8,2,128,128]{3,2,1,0:T(8,128)(2,1)S(1)}, u32[]{:S(2)}, u32[]{:S(2)}) collective-permute-start(bf16[8,2,128,128]{3,2,1,0:T(8,128)(2,1)S(1)} %get-tuple-element.9.refs_1_), channel_id=1, source_target_pairs={{0,16},{16,0},{32,48},{48,32},{64,80},{80,64},{96,112},{112,96},{1... | collective-permute-start | bytes 1572872 | tf_op jit(solution)/shard_map/ppermute | solution.py:204
  50.4 15.3 %collective-permute-start.24 = (bf16[8,2,128,128]{3,2,1,0:T(8,128)(2,1)S(1)}, bf16[8,2,128,128]{3,2,1,0:T(8,128)(2,1)}, u32[]{:S(2)}, u32[]{:S(2)}) collective-permute-start(bf16[8,2,128,128]{3,2,1,0:T(8,128)(2,1)S(1)} %collective-permute-done.20.refs_2_), channel_id=1, source_target_pairs={{0,32},{16,48},{32,64},{48,80},{64,96},{80,112},{96,0},{112,16},{1... | collective-permute-start | bytes 1572872 | tf_op jit(solution)/shard_map/ppermute | solution.py:201
  54.3 15.1 %collective-permute-start.25 = (bf16[8,2,128,128]{3,2,1,0:T(8,128)(2,1)S(1)}, bf16[8,2,128,128]{3,2,1,0:T(8,128)(2,1)}, u32[]{:S(2)}, u32[]{:S(2)}) collective-permute-start(bf16[8,2,128,128]{3,2,1,0:T(8,128)(2,1)S(1)} %collective-permute-done.23.refs_5_), channel_id=1, source_target_pairs={{0,96},{16,112},{32,0},{48,16},{64,32},{80,48},{96,64},{112,80},{1... | collective-permute-start | bytes 1572872 | tf_op jit(solution)/shard_map/ppermute | solution.py:201
  55.6 15.2 %collective-permute-start.28 = (bf16[8,2,128,128]{3,2,1,0:T(8,128)(2,1)S(1)}, bf16[8,2,128,128]{3,2,1,0:T(8,128)(2,1)S(1)}, u32[]{:S(2)}, u32[]{:S(2)}) collective-permute-start(bf16[8,2,128,128]{3,2,1,0:T(8,128)(2,1)S(1)} %collective-permute-done.20.refs_2_), channel_id=1, source_target_pairs={{0,16},{16,0},{32,48},{48,32},{64,80},{80,64},{96,112},{112,96},{1... | collective-permute-start | bytes 1572872 | tf_op jit(solution)/shard_map/ppermute | solution.py:204
  91.0 137.9 %all-to-all-start.2 = ((bf16[16,2,256,256]{3,2,1,0:T(8,128)(2,1)}), bf16[16,2,256,256]{3,2,1,0:T(8,128)(2,1)}, u32[]{:S(2)}, u32[]{:S(2)}) async-start(bf16[16,2,256,256]{3,2,1,0:T(8,128)(2,1)} %bitcast.27), calls=%async_computation.2 | async-start | bytes 8388608 | tf_op jit(solution)/shard_map/all_to_all | solution.py:266
  98.0 40.9 %collective-permute-start = (bf16[2,128,128]{2,1,0:T(8,128)(2,1)S(1)}, bf16[2,128,128]{2,1,0:T(8,128)(2,1)S(1)}, u32[]{:S(2)}, u32[]{:S(2)}) collective-permute-start(bf16[2,128,128]{2,1,0:T(8,128)(2,1)S(1)} %constant_dynamic-slice_fusion.1), channel_id=1, source_target_pairs={{0,1},{1,2},{2,3},{3,0},{4,5},{5,6},{6,7},{7,4},{8,9},{9,10},{10,1... | collective-permute-start | bytes 196616 | tf_op jit(solution)/shard_map/ppermute | solution.py:208
  99.5 39.3 %collective-permute-start.1 = (bf16[2,128,128]{2,1,0:T(8,128)(2,1)S(1)}, bf16[2,128,128]{2,1,0:T(8,128)(2,1)S(1)}, u32[]{:S(2)}, u32[]{:S(2)}) collective-permute-start(bf16[2,128,128]{2,1,0:T(8,128)(2,1)S(1)} %constant_dynamic-slice_fusion.1), channel_id=1, source_target_pairs={{0,2},{1,3},{2,0},{3,1},{4,6},{5,7},{6,4},{7,5},{8,10},{9,11},{10,... | collective-permute-start | bytes 196616 | tf_op jit(solution)/shard_map/ppermute | solution.py:208
  101.9 36.9 %collective-permute-start.2 = (bf16[2,128,128]{2,1,0:T(8,128)(2,1)S(1)}, bf16[2,128,128]{2,1,0:T(8,128)(2,1)S(1)}, u32[]{:S(2)}, u32[]{:S(2)}) collective-permute-start(bf16[2,128,128]{2,1,0:T(8,128)(2,1)S(1)} %constant_dynamic-slice_fusion.1), channel_id=1, source_target_pairs={{0,3},{1,0},{2,1},{3,2},{4,7},{5,4},{6,5},{7,6},{8,11},{9,8},{10,9... | collective-permute-start | bytes 196616 | tf_op jit(solution)/shard_map/ppermute | solution.py:208
  138.9 16.0 %collective-permute-start.4 = (bf16[4,2,128,128]{3,2,1,0:T(8,128)(2,1)S(1)}, bf16[4,2,128,128]{3,2,1,0:T(8,128)(2,1)S(1)}, u32[]{:S(2)}, u32[]{:S(2)}) collective-permute-start(bf16[4,2,128,128]{3,2,1,0:T(8,128)(2,1)S(1)} %get-tuple-element.12), channel_id=1, source_target_pairs={{0,8},{1,9},{2,10},{3,11},{4,12},{5,13},{6,14},{7,15},{8,0},{9,1},... | collective-permute-start | bytes 786440 | tf_op jit(solution)/shard_map/ppermute | solution.py:208
  167.1 14.6 %collective-permute-start.7 = (bf16[8,2,128,128]{3,2,1,0:T(8,128)(2,1)S(1)}, bf16[8,2,128,128]{3,2,1,0:T(8,128)(2,1)S(1)}, u32[]{:S(2)}, u32[]{:S(2)}) collective-permute-start(bf16[8,2,128,128]{3,2,1,0:T(8,128)(2,1)S(1)} %bitcast.31), channel_id=1, source_target_pairs={{0,32},{16,48},{32,64},{48,80},{64,96},{80,112},{96,0},{112,16},{1... | collective-permute-start | bytes 1572872 | tf_op jit(solution)/shard_map/ppermute | solution.py:201
  167.2 23.6 %collective-permute-start.6 = (bf16[8,2,128,128]{3,2,1,0:T(8,128)(2,1)S(1)}, bf16[8,2,128,128]{3,2,1,0:T(8,128)(2,1)S(1)}, u32[]{:S(2)}, u32[]{:S(2)}) collective-permute-start(bf16[8,2,128,128]{3,2,1,0:T(8,128)(2,1)S(1)} %bitcast.34), channel_id=1, source_target_pairs={{0,32},{16,48},{32,64},{48,80},{64,96},{80,112},{96,0},{112,16},{1... | collective-permute-start | bytes 1572872 | tf_op jit(solution)/shard_map/ppermute | solution.py:201
  167.5 26.5 %collective-permute-start.13 = (bf16[8,2,128,128]{3,2,1,0:T(8,128)(2,1)S(1)}, bf16[8,2,128,128]{3,2,1,0:T(8,128)(2,1)S(1)}, u32[]{:S(2)}, u32[]{:S(2)}) collective-permute-start(bf16[8,2,128,128]{3,2,1,0:T(8,128)(2,1)S(1)} %bitcast.32), channel_id=1, source_target_pairs={{0,16},{16,0},{32,48},{48,32},{64,80},{80,64},{96,112},{112,96},{1... | collective-permute-start | bytes 1572872 | tf_op jit(solution)/shard_map/ppermute | solution.py:204
  170.3 23.6 %collective-permute-start.8 = (bf16[8,2,128,128]{3,2,1,0:T(8,128)(2,1)S(1)}, bf16[8,2,128,128]{3,2,1,0:T(8,128)(2,1)}, u32[]{:S(2)}, u32[]{:S(2)}) collective-permute-start(bf16[8,2,128,128]{3,2,1,0:T(8,128)(2,1)S(1)} %bitcast.35), channel_id=1, source_target_pairs={{0,96},{16,112},{32,0},{48,16},{64,32},{80,48},{96,64},{112,80},{1... | collective-permute-start | bytes 1572872 | tf_op jit(solution)/shard_map/ppermute | solution.py:201
  176.4 17.7 %collective-permute-start.12 = (bf16[8,2,128,128]{3,2,1,0:T(8,128)(2,1)S(1)}, bf16[8,2,128,128]{3,2,1,0:T(8,128)(2,1)S(1)}, u32[]{:S(2)}, u32[]{:S(2)}) collective-permute-start(bf16[8,2,128,128]{3,2,1,0:T(8,128)(2,1)S(1)} %bitcast.36), channel_id=1, source_target_pairs={{0,16},{16,0},{32,48},{48,32},{64,80},{80,64},{96,112},{112,96},{1... | collective-permute-start | bytes 1572872 | tf_op jit(solution)/shard_map/ppermute | solution.py:204
  181.7 17.2 %collective-permute-start.11 = (bf16[8,2,128,128]{3,2,1,0:T(8,128)(2,1)S(1)}, bf16[8,2,128,128]{3,2,1,0:T(8,128)(2,1)}, u32[]{:S(2)}, u32[]{:S(2)}) collective-permute-start(bf16[8,2,128,128]{3,2,1,0:T(8,128)(2,1)S(1)} %collective-permute-done.9.refs_5_), channel_id=1, source_target_pairs={{0,96},{16,112},{32,0},{48,16},{64,32},{80,48},{96,64},{112,80},{1... | collective-permute-start | bytes 1572872 | tf_op jit(solution)/shard_map/ppermute | solution.py:201
  193.9 14.7 %collective-permute-start.10 = (bf16[8,2,128,128]{3,2,1,0:T(8,128)(2,1)S(1)}, bf16[8,2,128,128]{3,2,1,0:T(8,128)(2,1)}, u32[]{:S(2)}, u32[]{:S(2)}) collective-permute-start(bf16[8,2,128,128]{3,2,1,0:T(8,128)(2,1)S(1)} %collective-permute-done.6.refs_2_), channel_id=1, source_target_pairs={{0,32},{16,48},{32,64},{48,80},{64,96},{80,112},{96,0},{112,16},{1... | collective-permute-start | bytes 1572872 | tf_op jit(solution)/shard_map/ppermute | solution.py:201
  194.0 16.4 %collective-permute-start.14 = (bf16[8,2,128,128]{3,2,1,0:T(8,128)(2,1)S(1)}, bf16[8,2,128,128]{3,2,1,0:T(8,128)(2,1)}, u32[]{:S(2)}, u32[]{:S(2)}) collective-permute-start(bf16[8,2,128,128]{3,2,1,0:T(8,128)(2,1)S(1)} %collective-permute-done.6.refs_2_), channel_id=1, source_target_pairs={{0,16},{16,0},{32,48},{48,32},{64,80},{80,64},{96,112},{112,96},{1... | collective-permute-start | bytes 1572872 | tf_op jit(solution)/shard_map/ppermute | solution.py:204
  194.1 16.2 %collective-permute-start.15 = (bf16[8,2,128,128]{3,2,1,0:T(8,128)(2,1)S(1)}, bf16[8,2,128,128]{3,2,1,0:T(8,128)(2,1)}, u32[]{:S(2)}, u32[]{:S(2)}) collective-permute-start(bf16[8,2,128,128]{3,2,1,0:T(8,128)(2,1)S(1)} %collective-permute-done.7.refs_3_), channel_id=1, source_target_pairs={{0,16},{16,0},{32,48},{48,32},{64,80},{80,64},{96,112},{112,96},{1... | collective-permute-start | bytes 1572872 | tf_op jit(solution)/shard_map/ppermute | solution.py:204
  (32 other events, 800.0 us)
